TPU v7x, 512 devices: a whole 4x8x8 slice. The times are simulated.
512 devices in a mesh: sec: 32 (over y, z_hi, core), sub: 16 (over z_lo, x).
Axes of the slice: x: 4, y: 8, z: 8 (z_hi: 2, z_lo: 4; z = z_hi * 4 + z_lo), core: 2. Of those that a mesh axis runs over, the one named last changes fastest.
Arguments:
- forcing: float32 [32, 192, 64, 128], P('sec', 'sub'), may hold values from -60 to 60
- coupling: float32 [32, 192, 64, 128], P('sec', 'sub'), may hold values from -0.6 to 0.6
- diag_pair: float32 [32, 192, 64, 128], P('sec', 'sub'), may hold values from -1 to 9
- side: float32 [32, 192, 32], P('sec', 'sub'), may hold values from -1 to -0.3
- basis: float32 [32, 1024, 768], P('sec', 'sub'), may hold values from -0.21875 to 0.21875
- coarse_inverse: float32 [32, 1024, 1024], P('sec', 'sub'), may hold values from -0.05 to 0.3
Outputs:
- solution: float32 [32, 192, 64, 128], P('sec', 'sub')
All inputs are finite; a program needn't handle non-finite values.
Results may differ from a plain program's by a relative error of at most 0.0001.
Values sent between devices are 32-bit elements; how exact they have to be, the bound alone decides.
No kernel may reach another device: no remote copies, remote signals or barrier semaphores. Data moves between devices by JAX's collectives and lax.ppermute only.
A program may use at most 64 MiB of HBM per device.

v0:
```python
import jax
import jax.numpy as jnp
from jax import lax
from jax.sharding import PartitionSpec as P

SWEEPS = 4
ITERS = 2


PRECISE = lax.Precision.HIGHEST


def extended(block, sides, width):
    for axis, dim in sides:
        count = lax.axis_size(axis)
        forward = [(i, i + 1) for i in range(count - 1)]
        backward = [(target, source) for source, target in forward]
        low = lax.ppermute(
            lax.slice_in_dim(block, block.shape[dim] - width, None, axis=dim), axis, forward
        )
        high = lax.ppermute(lax.slice_in_dim(block, 0, width, axis=dim), axis, backward)
        block = jnp.concatenate([low, block, high], axis=dim)
    return block


def from_behind(value, axis, steps):
    count = lax.axis_size(axis)
    initial, last = (max(0, -steps), min(count, count - steps))
    return lax.ppermute(value, axis, [(source, source + steps) for source in range(initial, last)])


def tile_apply(tile_set, vector):
    return jnp.einsum("bij,bjc->bic", tile_set, vector, precision=PRECISE)


def couple(coupling, diagonal, centre, before, after):
    return tile_apply(diagonal, centre) + tile_apply(
        coupling, jnp.concatenate([before, after], axis=1)
    )


def chain_apply(coupling, diagonal, vector):
    zero_block = jnp.zeros_like(vector[:1])
    before = jnp.concatenate([zero_block, vector[:-1]], axis=0)
    after = jnp.concatenate([vector[1:], zero_block], axis=0)
    return couple(coupling, diagonal, vector, before, after)


def add_faces(linear, sides, below, above):
    face_rows = sides.shape[-1] // 2
    node_count = linear.shape[1]
    lower_term = sides[:, :face_rows, None] * below
    upper_term = sides[:, face_rows:, None] * above
    return jnp.concatenate(
        [
            linear[:, :face_rows] + lower_term,
            linear[:, face_rows : node_count - face_rows],
            linear[:, node_count - face_rows :] + upper_term,
        ],
        axis=1,
    )


def local_sweeps(residual_ext, coupling_ext, diagonal_ext, inverse_ext):
    update = tile_apply(inverse_ext, residual_ext)
    for sweep_index in range(SWEEPS - 1):
        update = update + tile_apply(
            inverse_ext, residual_ext - chain_apply(coupling_ext, diagonal_ext, update)
        )
    return update[1:-1]


def project(basis_rows, field):
    return jnp.dot(basis_rows, field.reshape(-1, field.shape[-1]), precision=PRECISE)


def expand(basis_rows, correction, target_shape):
    spread = lax.dot_general(basis_rows, correction, (((0,), (0,)), ((), ())), precision=PRECISE)
    return spread.reshape(target_shape)


def fold_rows(inverse_rows, segment):
    return jnp.dot(inverse_rows, segment, precision=PRECISE)


def coarse_direct(basis_rows, inverse_rows, residual):
    projected = project(basis_rows, residual)
    return fold_rows(inverse_rows, lax.all_gather(projected, "sub", axis=0, tiled=True))


def operate(update, coupling, diagonal, sides):
    update_ext = extended(update, (("sub", 0),), 1)
    linear = couple(coupling, diagonal, update, update_ext[:-2], update_ext[2:])
    face_rows = sides.shape[-1] // 2
    node_count = update.shape[1]
    north_face = update[:, node_count - face_rows :, :]
    south_face = update[:, :face_rows, :]
    below = from_behind(north_face, "sec", 1)
    above = from_behind(south_face, "sec", -1)
    return add_faces(linear, sides, below, above)


def step_length(image, residual):
    numerator, denominator = lax.psum(
        (jnp.sum(image * residual, axis=(0, 1)), jnp.sum(image * image, axis=(0, 1))),
        ("sec", "sub"),
    )
    return numerator / denominator


def shards(forcing, coupling, diag_pair, side, basis, coarse_inverse):
    residual = forcing[0]
    couplings = coupling[0]
    pairs = diag_pair[0]
    sides = side[0]
    basis_rows = basis[0]
    inverse_rows = coarse_inverse[0]
    node_count = residual.shape[1]
    stacked = jnp.concatenate([couplings, pairs], axis=2)
    stacked_ext = extended(stacked, (("sub", 0),), 1)
    coupling_ext = stacked_ext[:, :, : 2 * node_count]
    diagonal_ext = stacked_ext[:, :, 2 * node_count : 3 * node_count]
    inverse_ext = stacked_ext[:, :, 3 * node_count :]
    diagonal_own = pairs[:, :, :node_count]
    solution = jnp.zeros_like(residual)
    for iteration in range(ITERS):
        correction = coarse_direct(basis_rows, inverse_rows, residual)
        residual_ext = extended(residual, (("sub", 0),), 1)
        local_part = local_sweeps(residual_ext, coupling_ext, diagonal_ext, inverse_ext)
        update = local_part + expand(basis_rows, correction, residual.shape)
        image = operate(update, couplings, diagonal_own, sides)
        step_size = step_length(image, residual)
        solution = solution + step_size * update
        residual = residual - step_size * image
    return solution[None]


def solution(mesh):
    placed = (
        P("sec", "sub", None, None),
        P("sec", "sub", None, None),
        P("sec", "sub", None, None),
        P("sec", "sub", None),
        P("sec", "sub", None),
        P("sec", "sub", None),
    )
    return jax.shard_map(
        shards, mesh=mesh, in_specs=placed, out_specs=P("sec", "sub", None, None), check_vma=False
    )
```

profile of v0, /device:TPU:1, one launch (start us, length us, event | category | flops | bytes accessed | tf_op | source)
XLA Modules:
  0.0 371.0 jit_solution(13853140546099342183)
XLA Ops:
  0.0 1.4 slice_bitcast_fusion.1
  1.4 3.9 %collective-permute-start.2 = (f32[1,64,128]{2,1,0:T(8,128)}, f32[1,64,128]{2,1,0:T(8,128)S(1)}, u32[]{:S(2)}, u32[]{:S(2)}) collective-permute-start(f32[1,64,128]{2,1,0:T(8,128)} %get-tuple-element.43), channel_id=1, source_target_pairs={{0,1},{1,2},{2,3},{3,4},{4,5},{5,6},{6,7},{7,8},{8,9},{9,10},{10,1... | collective-permute-start | bytes 98312 | tf_op jit(solution)/shard_map/ppermute | solution.py:18
  5.4 1.3 collective-permute-start.3
  6.7 0.9 pad_maximum_fusion.12
  7.6 4.6 %collective-permute-start = (f32[1,64,256]{2,1,0:T(8,128)S(1)}, f32[1,64,256]{2,1,0:T(8,128)}, u32[]{:S(2)}, u32[]{:S(2)}) collective-permute-start(f32[1,64,256]{2,1,0:T(8,128)S(1)} %get-tuple-element.13), channel_id=1, source_target_pairs={{0,1},{1,2},{2,3},{3,4},{4,5},{5,6},{6,7},{7,8},{8,9},{9,10},{10,1... | collective-permute-start | bytes 196616 | tf_op jit(solution)/shard_map/ppermute | solution.py:18
  12.2 1.3 collective-permute-start.1
  13.5 0.4 fusion.90
  13.9 41.7 %all_gather.6 = f32[1024,128]{1,0:T(8,128)S(1)} all-gather(f32[64,128]{1,0:T(8,128)S(1)} %fusion.90), channel_id=1, replica_groups=mesh['sec'=32,'sub'=16] {'sub'}, dimensions={0}, use_global_device_ids=true | all-gather | bytes 557056 | tf_op jit(solution)/shard_map/all_gather | solution.py:88
  55.6 1.0 fusion.85
  56.6 0.5 convolution_bitcast_fusion.1
  57.2 0.2 copy.9
  57.4 0.8 copy-done.2
  58.3 0.9 pad_maximum_fusion
  59.3 0.6 fusion.81
  60.0 0.9 fusion.28
  60.9 0.6 fusion.5
  61.5 0.6 convolution_add_fusion.8
  62.2 0.9 fusion.24
  63.1 0.6 fusion.4
  63.7 0.6 convolution_add_fusion.6
  64.5 0.9 fusion.20
  65.4 0.6 fusion.3
  66.0 0.6 fusion.77
  66.7 0.5 fusion.57
  67.2 1.3 collective-permute-start.4
  68.5 1.3 collective-permute-start.5
  69.8 16.4 %collective-permute-start.6 = (f32[12,16,128]{2,1,0:T(8,128)S(1)}, f32[12,16,128]{2,1,0:T(8,128)S(1)}, u32[]{:S(2)}, u32[]{:S(2)}) collective-permute-start(f32[12,16,128]{2,1,0:T(8,128)S(1)} %get-tuple-element.39), channel_id=1, source_target_pairs={{0,16},{16,32},{32,48},{48,64},{64,80},{80,96},{96,112},{112,128},... | collective-permute-start | bytes 294920 | tf_op jit(solution)/shard_map/ppermute | solution.py:29
  86.3 1.9 collective-permute-start.7
  88.2 0.7 fusion.7
  89.0 0.7 fusion.125
  89.7 6.4 %collective-permute-done.7 = f32[12,16,128]{2,1,0:T(8,128)S(1)} collective-permute-done((f32[12,16,128]{2,1,0:T(8,128)S(1)}, f32[12,16,128]{2,1,0:T(8,128)S(1)}, u32[]{:S(2)}, u32[]{:S(2)}) %collective-permute-start.7) | collective-permute-done | bytes 98336 | tf_op jit(solution)/shard_map/ppermute | solution.py:29
  96.3 0.2 multiply_reduce_fusion.2
  96.4 0.5 copy-done.5
  96.9 97.6 %all-reduce.13 = (f32[128]{0:T(128)S(1)}, f32[128]{0:T(128)S(1)}) all-reduce(f32[128]{0:T(128)S(1)} %get-tuple-element.8, f32[128]{0:T(128)S(1)} %get-tuple-element.7), channel_id=1, replica_groups=mesh['sec'=32,'sub'=16] {'sec','sub'}, use_global_device_ids=true, to_apply=%region_1.0 | all-reduce | flops 256 | bytes 2048 | tf_op jit(solution)/shard_map/psum | solution.py:104
  194.6 1.0 multiply_subtract_fusion
  195.8 0.4 convolution_bitcast_fusion.2
  196.1 2.2 collective-permute-start.8
  198.4 1.3 collective-permute-start.9
  199.7 35.9 %all_gather.7 = f32[1024,128]{1,0:T(8,128)S(1)} all-gather(f32[64,128]{1,0:T(8,128)S(1)} %convolution_bitcast_fusion.2), channel_id=1, replica_groups=mesh['sec'=32,'sub'=16] {'sub'}, dimensions={0}, use_global_device_ids=true | all-gather | bytes 557056 | tf_op jit(solution)/shard_map/all_gather | solution.py:88
  235.5 1.0 fusion.83
  236.5 0.5 convolution_bitcast_fusion
  237.0 0.9 copy.10
  237.9 0.6 fusion.75
  238.7 0.9 fusion.16
  239.6 0.6 fusion.2
  240.2 0.6 convolution_add_fusion.3
  240.9 0.9 fusion.12
  241.8 0.6 fusion.1
  242.4 0.6 convolution_add_fusion.1
  243.2 0.9 fusion.8
  244.1 0.6 fusion
  244.7 0.6 fusion.71
  245.3 0.3 copy-done.9
  245.8 0.5 fusion.55
  246.2 1.3 collective-permute-start.10
  247.5 1.3 collective-permute-start.11
  248.9 13.5 %collective-permute-start.12 = (f32[12,16,128]{2,1,0:T(8,128)S(1)}, f32[12,16,128]{2,1,0:T(8,128)S(1)}, u32[]{:S(2)}, u32[]{:S(2)}) collective-permute-start(f32[12,16,128]{2,1,0:T(8,128)S(1)} %get-tuple-element.29), channel_id=1, source_target_pairs={{0,16},{16,32},{32,48},{48,64},{64,80},{80,96},{96,112},{112,128},... | collective-permute-start | bytes 294920 | tf_op jit(solution)/shard_map/ppermute | solution.py:29
  262.4 1.9 collective-permute-start.13
  264.3 0.7 fusion.6
  265.1 7.6 %collective-permute-done.13 = f32[12,16,128]{2,1,0:T(8,128)S(1)} collective-permute-done((f32[12,16,128]{2,1,0:T(8,128)S(1)}, f32[12,16,128]{2,1,0:T(8,128)S(1)}, u32[]{:S(2)}, u32[]{:S(2)}) %collective-permute-start.13) | collective-permute-done | bytes 98336 | tf_op jit(solution)/shard_map/ppermute | solution.py:29
  272.8 0.2 multiply_reduce_fusion
  273.0 96.6 %all-reduce.12 = (f32[128]{0:T(128)S(1)}, f32[128]{0:T(128)S(1)}) all-reduce(f32[128]{0:T(128)S(1)} %get-tuple-element.6, f32[128]{0:T(128)S(1)} %get-tuple-element.5), channel_id=1, replica_groups=mesh['sec'=32,'sub'=16] {'sec','sub'}, use_global_device_ids=true, to_apply=%region_5.0 | all-reduce | flops 256 | bytes 2048 | tf_op jit(solution)/shard_map/psum | solution.py:104
  369.6 0.6 copy-done.13
  370.2 0.8 add_bitcast_fusion
  (57 shorter events, 1.4 us)
Async XLA Ops:
  0.0 55.6 %copy-start = (f32[1,64,1024]{2,1,0:T(8,128)S(1)}, f32[1,64,1024]{2,1,0:T(8,128)}, u32[]{:S(2)}) copy-start(f32[1,64,1024]{2,1,0:T(8,128)} %param.11) | copy-start | bytes 786436
  1.4 57.8 %collective-permute-start.2 = (f32[1,64,128]{2,1,0:T(8,128)}, f32[1,64,128]{2,1,0:T(8,128)S(1)}, u32[]{:S(2)}, u32[]{:S(2)}) collective-permute-start(f32[1,64,128]{2,1,0:T(8,128)} %get-tuple-element.43), channel_id=1, source_target_pairs={{0,1},{1,2},{2,3},{3,4},{4,5},{5,6},{6,7},{7,8},{8,9},{9,10},{10,1... | collective-permute-start | bytes 98312 | tf_op jit(solution)/shard_map/ppermute | solution.py:18
  5.4 53.9 %collective-permute-start.3 = (f32[1,64,128]{2,1,0:T(8,128)S(1)}, f32[1,64,128]{2,1,0:T(8,128)S(1)}, u32[]{:S(2)}, u32[]{:S(2)}) collective-permute-start(f32[1,64,128]{2,1,0:T(8,128)S(1)} %get-tuple-element.44), channel_id=1, source_target_pairs={{1,0},{2,1},{3,2},{4,3},{5,4},{6,5},{7,6},{8,7},{9,8},{10,9},{11,1... | collective-permute-start | bytes 98312 | tf_op jit(solution)/shard_map/ppermute | solution.py:21
  6.7 6.8 %copy-start.11 = (f32[1,12,32]{2,0,1:T(1,128)S(1)}, f32[1,12,32]{2,0,1:T(1,128)}, u32[]{:S(2)}) copy-start(f32[1,12,32]{2,0,1:T(1,128)} %param.9) | copy-start | bytes 4612
  6.7 6.8 %copy-start.1 = (f32[1,12,64,128]{3,2,1,0:T(8,128)S(1)}, f32[1,12,64,128]{3,2,1,0:T(8,128)}, u32[]{:S(2)}) copy-start(f32[1,12,64,128]{3,2,1,0:T(8,128)} %param.6) | copy-start | bytes 1179652
  6.7 6.8 %copy-start.4 = (f32[1,64,768]{2,1,0:T(8,128)S(1)}, f32[1,64,768]{2,1,0:T(8,128)}, u32[]{:S(2)}) copy-start(f32[1,64,768]{2,1,0:T(8,128)} %param.10) | copy-start | bytes 589828
  7.6 49.8 %collective-permute-start = (f32[1,64,256]{2,1,0:T(8,128)S(1)}, f32[1,64,256]{2,1,0:T(8,128)}, u32[]{:S(2)}, u32[]{:S(2)}) collective-permute-start(f32[1,64,256]{2,1,0:T(8,128)S(1)} %get-tuple-element.13), channel_id=1, source_target_pairs={{0,1},{1,2},{2,3},{3,4},{4,5},{5,6},{6,7},{7,8},{8,9},{9,10},{10,1... | collective-permute-start | bytes 196616 | tf_op jit(solution)/shard_map/ppermute | solution.py:18
  12.2 45.2 %collective-permute-start.1 = (f32[1,64,256]{2,1,0:T(8,128)S(1)}, f32[1,64,256]{2,1,0:T(8,128)}, u32[]{:S(2)}, u32[]{:S(2)}) collective-permute-start(f32[1,64,256]{2,1,0:T(8,128)S(1)} %get-tuple-element.14), channel_id=1, source_target_pairs={{1,0},{2,1},{3,2},{4,3},{5,4},{6,5},{7,6},{8,7},{9,8},{10,9},{11,1... | collective-permute-start | bytes 196616 | tf_op jit(solution)/shard_map/ppermute | solution.py:21
  57.2 1.0 copy-start.2
  57.2 1.1 copy-start.3
  67.2 21.0 %collective-permute-start.4 = (f32[1,64,128]{2,1,0:T(8,128)S(1)}, f32[1,64,128]{2,1,0:T(8,128)S(1)}, u32[]{:S(2)}, u32[]{:S(2)}) collective-permute-start(f32[1,64,128]{2,1,0:T(8,128)S(1)} %get-tuple-element.41), channel_id=1, source_target_pairs={{0,1},{1,2},{2,3},{3,4},{4,5},{5,6},{6,7},{7,8},{8,9},{9,10},{10,1... | collective-permute-start | bytes 98312 | tf_op jit(solution)/shard_map/ppermute | solution.py:18
  68.5 19.7 %collective-permute-start.5 = (f32[1,64,128]{2,1,0:T(8,128)S(1)}, f32[1,64,128]{2,1,0:T(8,128)S(1)}, u32[]{:S(2)}, u32[]{:S(2)}) collective-permute-start(f32[1,64,128]{2,1,0:T(8,128)S(1)} %get-tuple-element.42), channel_id=1, source_target_pairs={{1,0},{2,1},{3,2},{4,3},{5,4},{6,5},{7,6},{8,7},{9,8},{10,9},{11,1... | collective-permute-start | bytes 98312 | tf_op jit(solution)/shard_map/ppermute | solution.py:21
  69.8 19.9 %collective-permute-start.6 = (f32[12,16,128]{2,1,0:T(8,128)S(1)}, f32[12,16,128]{2,1,0:T(8,128)S(1)}, u32[]{:S(2)}, u32[]{:S(2)}) collective-permute-start(f32[12,16,128]{2,1,0:T(8,128)S(1)} %get-tuple-element.39), channel_id=1, source_target_pairs={{0,16},{16,32},{32,48},{48,64},{64,80},{80,96},{96,112},{112,128},... | collective-permute-start | bytes 294920 | tf_op jit(solution)/shard_map/ppermute | solution.py:29
  86.3 9.8 %collective-permute-start.7 = (f32[12,16,128]{2,1,0:T(8,128)S(1)}, f32[12,16,128]{2,1,0:T(8,128)S(1)}, u32[]{:S(2)}, u32[]{:S(2)}) collective-permute-start(f32[12,16,128]{2,1,0:T(8,128)S(1)} %get-tuple-element.40), channel_id=1, source_target_pairs={{16,0},{32,16},{48,32},{64,48},{80,64},{96,80},{112,96},{128,112},... | collective-permute-start | bytes 294920 | tf_op jit(solution)/shard_map/ppermute | solution.py:29
  96.2 0.6 copy-start.5
  96.2 0.7 copy-start.7
  194.6 1.1 copy-start.12
  194.6 1.1 copy-start.6
  194.6 1.1 copy-start.8
  194.6 1.1 copy-start.10
  196.1 41.8 %collective-permute-start.8 = (f32[1,64,128]{2,1,0:T(8,128)S(1)}, f32[1,64,128]{2,1,0:T(8,128)S(1)}, u32[]{:S(2)}, u32[]{:S(2)}) collective-permute-start(f32[1,64,128]{2,1,0:T(8,128)S(1)} %get-tuple-element.33), channel_id=1, source_target_pairs={{0,1},{1,2},{2,3},{3,4},{4,5},{5,6},{6,7},{7,8},{8,9},{9,10},{10,1... | collective-permute-start | bytes 98312 | tf_op jit(solution)/shard_map/ppermute | solution.py:18
  198.4 39.6 %collective-permute-start.9 = (f32[1,64,128]{2,1,0:T(8,128)S(1)}, f32[1,64,128]{2,1,0:T(8,128)S(1)}, u32[]{:S(2)}, u32[]{:S(2)}) collective-permute-start(f32[1,64,128]{2,1,0:T(8,128)S(1)} %get-tuple-element.34), channel_id=1, source_target_pairs={{1,0},{2,1},{3,2},{4,3},{5,4},{6,5},{7,6},{8,7},{9,8},{10,9},{11,1... | collective-permute-start | bytes 98312 | tf_op jit(solution)/shard_map/ppermute | solution.py:21
  244.7 1.0 copy-start.9
  246.2 18.0 %collective-permute-start.10 = (f32[1,64,128]{2,1,0:T(8,128)S(1)}, f32[1,64,128]{2,1,0:T(8,128)S(1)}, u32[]{:S(2)}, u32[]{:S(2)}) collective-permute-start(f32[1,64,128]{2,1,0:T(8,128)S(1)} %get-tuple-element.31), channel_id=1, source_target_pairs={{0,1},{1,2},{2,3},{3,4},{4,5},{5,6},{6,7},{7,8},{8,9},{9,10},{10,1... | collective-permute-start | bytes 98312 | tf_op jit(solution)/shard_map/ppermute | solution.py:18
  247.5 16.7 %collective-permute-start.11 = (f32[1,64,128]{2,1,0:T(8,128)S(1)}, f32[1,64,128]{2,1,0:T(8,128)S(1)}, u32[]{:S(2)}, u32[]{:S(2)}) collective-permute-start(f32[1,64,128]{2,1,0:T(8,128)S(1)} %get-tuple-element.32), channel_id=1, source_target_pairs={{1,0},{2,1},{3,2},{4,3},{5,4},{6,5},{7,6},{8,7},{9,8},{10,9},{11,1... | collective-permute-start | bytes 98312 | tf_op jit(solution)/shard_map/ppermute | solution.py:21
  248.9 16.2 %collective-permute-start.12 = (f32[12,16,128]{2,1,0:T(8,128)S(1)}, f32[12,16,128]{2,1,0:T(8,128)S(1)}, u32[]{:S(2)}, u32[]{:S(2)}) collective-permute-start(f32[12,16,128]{2,1,0:T(8,128)S(1)} %get-tuple-element.29), channel_id=1, source_target_pairs={{0,16},{16,32},{32,48},{48,64},{64,80},{80,96},{96,112},{112,128},... | collective-permute-start | bytes 294920 | tf_op jit(solution)/shard_map/ppermute | solution.py:29
  262.4 10.4 %collective-permute-start.13 = (f32[12,16,128]{2,1,0:T(8,128)S(1)}, f32[12,16,128]{2,1,0:T(8,128)S(1)}, u32[]{:S(2)}, u32[]{:S(2)}) collective-permute-start(f32[12,16,128]{2,1,0:T(8,128)S(1)} %get-tuple-element.30), channel_id=1, source_target_pairs={{16,0},{32,16},{48,32},{64,48},{80,64},{96,80},{112,96},{128,112},... | collective-permute-start | bytes 294920 | tf_op jit(solution)/shard_map/ppermute | solution.py:29
  369.6 0.6 copy-start.13
where the time goes:
time: 372 us; the launch traced here: 371 us
  blocking collectives  272 us (73%)
  starting transfers between devices  53.5 us (14%)
  matrix products  20.1 us (5%)
  waiting for transfers between devices  14.1 us (4%)
  local copies, waits for them, and re-layouts  6.39 us (2%)
  other arithmetic  4.42 us (1%)
    psum x2, blocking collectives, step_length(): lax.psum((jnp.sum(image * residual, axis=(0, 1)), jnp.sum(image * image,...  194 us
    all_gather x2, blocking collectives, coarse_direct(): lax.all_gather(projected, 'sub', axis=0, tiled=True)  77.6 us
    ppermute x4, starting transfers between devices, from_behind(): lax.ppermute(value, axis, [(source, source + steps) for source in range(i...  33.7 us
    dot_general x24, matrix products, tile_apply(): return jnp.einsum('bij,bjc->bic', tile_set, vector, precision=PRECISE)  16.5 us
    ppermute x4, waiting for transfers between devices, from_behind(): lax.ppermute(value, axis, [(source, source + steps) for source in range(i...  14 us
    ppermute x5, starting transfers between devices, extended(): lax.ppermute(lax.slice_in_dim(block, block.shape[dim] - width, None, axis...  13.3 us
  transfers between devices with their start and end apart: 14, of which 2 were waited for; matrix products, arithmetic and copies ran while one was open for 2% of the time, Pallas kernels for 0%

commit v1 on v0

v1 whole, which is shorter than its diff:
```python
import jax
import jax.numpy as jnp
from jax import lax
from jax.sharding import PartitionSpec as P

SWEEPS = 4
SCALE = 2.0**-16

PRECISE = lax.Precision.HIGHEST


def tile_apply(tile_set, vector, precision=PRECISE):
    return jnp.einsum("bij,bjc->bic", tile_set, vector, precision=precision)


def from_neighbours(to_next, to_previous, axis):
    count = lax.axis_size(axis)
    forward = [(i, i + 1) for i in range(count - 1)]
    backward = [(i + 1, i) for i in range(count - 1)]
    return lax.ppermute(to_next, axis, forward), lax.ppermute(to_previous, axis, backward)


def swapped_sections(to_next, to_previous):
    count = lax.axis_size("sec")
    near = [(i, i ^ 1) for i in range(count)]
    low = [(i, i + 1) for i in range(1, count - 1, 2)]
    far = low + [(target, source) for source, target in low]
    even = lax.axis_index("sec") % 2 == 0
    from_far = lax.ppermute(jnp.where(even, to_previous, to_next), "sec", far)
    from_near = lax.ppermute(jnp.where(even, to_next, to_previous), "sec", near)
    return jnp.where(even, from_far, from_near), jnp.where(even, from_near, from_far)


def gather_sub(value):
    count = lax.axis_size("sub")
    spread = jnp.broadcast_to(value[None], (count, *value.shape))
    got = lax.all_to_all(spread, "sub", 0, 0, tiled=True)
    return got.reshape(count * value.shape[0], *value.shape[1:])


def total(sums):
    shape = sums.shape
    flat = sums.reshape(1, -1)
    sections, subs = lax.axis_size("sec"), lax.axis_size("sub")
    pairs = [[2 * g, 2 * g + 1] for g in range(sections // 2)]
    alike = [[2 * g + p for g in range(sections // 2)] for p in range(2)]
    flat = jnp.sum(lax.all_gather(flat, "sec", axis_index_groups=pairs), axis=0)
    spread = jnp.broadcast_to(flat[None], (sections // 2, *flat.shape))
    flat = jnp.sum(lax.all_to_all(spread, "sec", 0, 0, axis_index_groups=alike, tiled=True), axis=0)
    spread = jnp.broadcast_to(flat[None], (subs, *flat.shape))
    flat = jnp.sum(lax.all_to_all(spread, "sub", 0, 0, tiled=True), axis=0)
    return flat.reshape(shape)


def triple(before, vector, after):
    previous = jnp.concatenate([before, vector[:-1]], axis=0)
    following = jnp.concatenate([vector[1:], after], axis=0)
    return jnp.concatenate([previous, following, vector], axis=1)


def shards(forcing, coupling, diag_pair, side, basis, coarse_inverse):
    residual = forcing[0]
    sides = side[0]
    basis_rows = basis[0]
    inverse_rows = coarse_inverse[0]
    nodes, columns = residual.shape[1:]
    faces = sides.shape[1] // 2
    inverses = diag_pair[0, :, :, nodes:]
    tiles = jnp.concatenate([coupling[0], diag_pair[0, :, :, :nodes]], axis=2)
    identity = jnp.concatenate(
        [jnp.zeros((nodes, 2 * nodes), jnp.float32), jnp.eye(nodes, dtype=jnp.float32)], axis=1
    )
    sweep = identity[None] - tile_apply(inverses, tiles)
    zero = jnp.zeros_like(residual[:1])
    low_sweep, high_sweep = from_neighbours(sweep[-1:, :, nodes:], jnp.concatenate([sweep[:1, :, :nodes], sweep[:1, :, 2 * nodes :]], axis=2), "sub")
    gap = jnp.zeros((1, nodes, nodes), jnp.float32)
    low_sweep = jnp.concatenate([gap, low_sweep], axis=2)
    high_sweep = jnp.concatenate([high_sweep[:, :, :nodes], gap, high_sweep[:, :, nodes:]], axis=2)
    sweep_ext = jnp.concatenate([low_sweep, sweep, high_sweep], axis=0)

    def precondition(field):
        start = tile_apply(inverses, field)
        low, high = from_neighbours(start[-1:], start[:1], "sub")
        projected = jnp.dot(basis_rows, field.reshape(-1, columns), precision=PRECISE)
        gathered = gather_sub(projected)
        start = jnp.concatenate([low, start, high], axis=0)
        update = start
        for _ in range(SWEEPS - 1):
            update = start + tile_apply(sweep_ext, triple(zero, update, zero))
        correction = jnp.dot(inverse_rows, gathered, precision=PRECISE)
        expanded = lax.dot_general(basis_rows, correction, (((0,), (0,)), ((), ())), precision=PRECISE)
        return update[1:-1] + expanded.reshape(field.shape)

    def operate(update):
        below, above = swapped_sections(update[:, nodes - faces :], update[:, :faces])
        before, after = from_neighbours(update[-1:], update[:1], "sub")
        linear = tile_apply(tiles, triple(before, update, after))
        lower = sides[:, :faces, None] * below
        upper = sides[:, faces:, None] * above
        return jnp.concatenate(
            [linear[:, :faces] + lower, linear[:, faces : nodes - faces], linear[:, nodes - faces :] + upper],
            axis=1,
        )

    first = precondition(residual)
    image = operate(first)
    rest = residual - image
    second = precondition(rest)
    change = operate(second) * SCALE

    def inner(left, right):
        return jnp.sum(left * right, axis=(0, 1))

    sums = total(
        jnp.stack(
            [inner(image, rest), inner(image, image), inner(change, rest), inner(change, image), inner(change, change)]
        )
    )
    short = -sums[0] / sums[1]
    step = 1.0 - short
    upper = step * (sums[2] + short * sums[3])
    scaled = step / SCALE
    lower = short * short * sums[1] + 2.0 * short * scaled * sums[3] + scaled * scaled * sums[4]
    step_next = upper / SCALE / lower
    result = (step + step_next * short) * first + (step_next * step) * second
    return result[None]


def solution(mesh):
    placed = (
        P("sec", "sub", None, None),
        P("sec", "sub", None, None),
        P("sec", "sub", None, None),
        P("sec", "sub", None),
        P("sec", "sub", None),
        P("sec", "sub", None),
    )
    return jax.shard_map(
        shards, mesh=mesh, in_specs=placed, out_specs=P("sec", "sub", None, None), check_vma=False
    )
```

time: 372 us -> 152 us (0.41)
  blocking collectives: 272 us -> 39.9 us
  starting transfers between devices: 53.5 us -> 69.5 us
  waiting for transfers between devices: 14.1 us -> 7.26 us
    psum x2 -> x0, blocking collectives: 194 us -> none  [step_length(): lax.psum((jnp.sum(image * residual, axis=(0, 1)), jnp.sum(image * image,...]
    all_gather x2 -> x1, blocking collectives: 77.6 us -> 1.98 us  [total(): flat = jnp.sum(lax.all_gather(flat, 'sec', axis_index_groups=pairs), axis=0)]
    all_to_all x0 -> x2, blocking collectives: none -> 37.9 us  [the longest x1 22.3 us: total(): lax.all_to_all(spread, 'sec', 0, 0, axis_index_groups=alike, tiled=True)]
    all_to_all x0 -> x2, starting transfers between devices: none -> 20.4 us  [gather_sub(): got = lax.all_to_all(spread, 'sub', 0, 0, tiled=True)]
    ppermute x14, waiting for transfers between devices: 14.1 us -> 0.04 us  [the longest x5 0.02 us: from_neighbours(): lax.ppermute(to_next, axis, forward)]
    all_to_all x0 -> x2, waiting for transfers between devices: none -> 7.22 us  [gather_sub(): got = lax.all_to_all(spread, 'sub', 0, 0, tiled=True)]
    ppermute x14, starting transfers between devices: 53.5 us -> 49.2 us  [the longest x2 20.7 us: swapped_sections(): from_far = lax.ppermute(jnp.where(even, to_previous, to_next), 'sec', far)]
    dot_general x30 -> x17, matrix products: 20.1 us -> 23.6 us  [the longest x11 21 us: tile_apply(): return jnp.einsum('bij,bjc->bic', tile_set, vector, precision=precision)]
  transfers between devices with their start and end apart: 14 -> 16, of which waited for: 2 -> 2; matrix products, arithmetic and copies ran while one was open for 2% -> 15% of each run, Pallas kernels for 0% -> 0%
where the time goes in v1:
time: 152 us; the launch traced here: 150 us
  starting transfers between devices  69.5 us (46%)
  blocking collectives  39.9 us (26%)
  matrix products  23.6 us (16%)
  waiting for transfers between devices  7.26 us (5%)
  local copies, waits for them, and re-layouts  6.57 us (4%)
  other arithmetic  2.86 us (2%)
    all_to_all x1, blocking collectives, total(): lax.all_to_all(spread, 'sec', 0, 0, axis_index_groups=alike, tiled=True)  22.3 us
    dot_general x11, matrix products, tile_apply(): return jnp.einsum('bij,bjc->bic', tile_set, vector, precision=precision)  21 us
    ppermute x2, starting transfers between devices, swapped_sections(): from_far = lax.ppermute(jnp.where(even, to_previous, to_next), 'sec', far)  20.7 us
    all_to_all x2, starting transfers between devices, gather_sub(): got = lax.all_to_all(spread, 'sub', 0, 0, tiled=True)  20.4 us
    ppermute x5, starting transfers between devices, from_neighbours(): lax.ppermute(to_next, axis, forward)  18 us
    all_to_all x1, blocking collectives, total(): flat = jnp.sum(lax.all_to_all(spread, 'sub', 0, 0, tiled=True), axis=0)  15.5 us
    all_to_all x2, waiting for transfers between devices, gather_sub(): got = lax.all_to_all(spread, 'sub', 0, 0, tiled=True)  7.22 us
    ppermute x5, starting transfers between devices, from_neighbours(): lax.ppermute(to_previous, axis, backward)  6.58 us
  transfers between devices with their start and end apart: 16, of which 2 were waited for; matrix products, arithmetic and copies ran while one was open for 15% of the time, Pallas kernels for 0%

profile of v1, /device:TPU:1, one launch (start us, length us, event | category | flops | bytes accessed | tf_op | source)
XLA Modules:
  0.0 150.4 jit_solution(16370843868566789003)
XLA Ops:
  0.0 1.1 slice_bitcast_fusion
  1.2 0.1 copy-done.9
  1.3 0.9 fusion.49
  2.2 0.1 pad_maximum_fusion.7
  2.3 1.4 collective-permute-start.3
  3.7 0.6 fusion.97
  4.3 4.6 %collective-permute-start = (f32[1,64,128]{2,1,0:T(8,128)S(1)}, f32[1,64,128]{2,1,0:T(8,128)S(1)}, u32[]{:S(2)}, u32[]{:S(2)}) collective-permute-start(f32[1,64,128]{2,1,0:T(8,128)S(1)} %get-tuple-element.47), channel_id=1, source_target_pairs={{0,1},{1,2},{2,3},{3,4},{4,5},{5,6},{6,7},{7,8},{8,9},{9,10},{10,1... | collective-permute-start | bytes 98312 | tf_op jit(solution)/shard_map/ppermute | solution.py:20
  8.9 1.3 collective-permute-start.1
  10.2 0.1 slice.203
  10.3 4.6 %collective-permute-start.2 = (f32[1,64,128]{2,1,0:T(8,128)S(1)}, f32[1,64,128]{2,1,0:T(8,128)}, u32[]{:S(2)}, u32[]{:S(2)}) collective-permute-start(f32[1,64,128]{2,1,0:T(8,128)S(1)} %slice.203), channel_id=1, source_target_pairs={{0,1},{1,2},{2,3},{3,4},{4,5},{5,6},{6,7},{7,8},{8,9},{9,10},{10,1... | collective-permute-start | bytes 98312 | tf_op jit(solution)/shard_map/ppermute | solution.py:20
  14.9 0.4 fusion.112
  15.3 0.9 broadcast_in_dim.13
  16.1 11.3 %all-to-all-start = ((f32[16,64,128]{2,1,0:T(8,128)}), f32[16,64,128]{2,1,0:T(8,128)S(1)}, u32[]{:S(2)}, u32[]{:S(2)}) async-start(f32[16,64,128]{2,1,0:T(8,128)} %broadcast_in_dim.13), calls=%async_computation | async-start | bytes 1048576 | tf_op jit(solution)/shard_map/all_to_all | solution.py:37
  27.5 0.1 fusion.162
  27.6 0.1 pad.67.clone
  27.7 0.1 fusion.161
  27.8 0.1 pad_maximum_fusion.4
  27.9 1.0 copy-done.7
  28.9 2.4 %fusion.53 = f32[14,64,128]{2,1,0:T(8,128)S(1)} fusion(f32[1,64,128]{2,1,0:T(8,128)S(1)} %collective-permute-done.1, f32[12,64,128]{2,1,0:T(8,128)S(1)} %fusion.97, f32[1,64,128]{2,1,0:T(8,128)S(1)} %collective-permute-done, f32[14,64,128]{2,1,0:T(8,128)S(1)} %get-tuple-element.31, f32[14,64,128]{2,1,0:T(8,128)S(1)} %get-tuple-element.30, ...), kind=kOutput, calls=%fused_computation.55 | convolution fusion | flops 266993664 | bytes 2501120 | tf_op jit(solution)/shard_map/bij,bjc->bic/dot_general | solution.py:13
  31.4 0.1 fusion.154
  31.4 2.4 %fusion.56 = f32[14,64,128]{2,1,0:T(8,128)S(1)} fusion(f32[13,64,128]{2,1,0:T(8,128)S(1)} %get-tuple-element.25, f32[13,64,128]{2,1,0:T(8,128)S(1)} %get-tuple-element.24, f32[14,64,128]{2,1,0:T(8,128)S(1)} %fusion.53, f32[1,64,128]{2,1,0:T(8,128)S(1)} %collective-permute-done.1, f32[12,64,128]{2,1,0:T(8,128)S(1)} %fusion.97, ...), kind=kOutput, calls=%fused_computation.56 | convolution fusion | flops 268369920 | bytes 2894336 | tf_op jit(solution)/shard_map/bij,bjc->bic/dot_general | solution.py:13
  33.9 0.1 fusion.153
  34.0 3.2 %fusion.13 = f32[14,64,128]{2,1,0:T(8,128)} fusion(f32[13,64,128]{2,1,0:T(8,128)S(1)} %get-tuple-element.23, f32[13,64,128]{2,1,0:T(8,128)S(1)} %get-tuple-element.22, f32[14,64,128]{2,1,0:T(8,128)S(1)} %fusion.56, f32[1,64,128]{2,1,0:T(8,128)} %collective-permute-done.2, f32[1,64,64]{2,1,0:T(8,128)S(1)} %get-tuple-element.50, ...), kind=kOutput, calls=%fused_computation.16 | convolution fusion | flops 268025856 | bytes 2435584 | tf_op jit(solution)/shard_map/bij,bjc->bic/dot_general | solution.py:13
  37.2 3.1 %all-to-all-done = f32[16,64,128]{2,1,0:T(8,128)S(1)} async-done(((f32[16,64,128]{2,1,0:T(8,128)}), f32[16,64,128]{2,1,0:T(8,128)S(1)}, u32[]{:S(2)}, u32[]{:S(2)}) %all-to-all-start) | async-done | bytes 524320 | tf_op jit(solution)/shard_map/all_to_all | solution.py:37
  40.3 0.4 fusion.107
  40.8 0.5 convolution_bitcast_fusion.3
  41.3 0.2 copy.13
  41.5 1.1 fusion.96
  42.5 0.1 fusion.159
  42.6 2.2 %collective-permute-start.4 = (f32[1,64,128]{2,1,0:T(8,128)S(1)}, f32[1,64,128]{2,1,0:T(8,128)S(1)}, u32[]{:S(2)}, u32[]{:S(2)}) collective-permute-start(f32[1,64,128]{2,1,0:T(8,128)S(1)} %get-tuple-element.43), channel_id=1, source_target_pairs={{0,1},{1,2},{2,3},{3,4},{4,5},{5,6},{6,7},{7,8},{8,9},{9,10},{10,1... | collective-permute-start | bytes 98312 | tf_op jit(solution)/shard_map/ppermute | solution.py:20
  44.9 1.3 collective-permute-start.5
  46.2 12.6 %collective-permute-start.6 = (f32[12,16,128]{2,1,0:T(8,128)S(1)}, f32[12,16,128]{2,1,0:T(8,128)S(1)}, u32[]{:S(2)}, u32[]{:S(2)}) collective-permute-start(f32[12,16,128]{2,1,0:T(8,128)S(1)} %get-tuple-element.41), channel_id=1, source_target_pairs={{16,32},{48,64},{80,96},{112,128},{144,160},{176,192},{208,224},{2... | collective-permute-start | bytes 294920 | tf_op jit(solution)/shard_map/ppermute | solution.py:29
  58.8 1.9 %collective-permute-start.7 = (f32[12,16,128]{2,1,0:T(8,128)S(1)}, f32[12,16,128]{2,1,0:T(8,128)S(1)}, u32[]{:S(2)}, u32[]{:S(2)}) collective-permute-start(f32[12,16,128]{2,1,0:T(8,128)S(1)} %get-tuple-element.42), channel_id=1, source_target_pairs={{0,16},{16,0},{32,48},{48,32},{64,80},{80,64},{96,112},{112,96},{1... | collective-permute-start | bytes 294920 | tf_op jit(solution)/shard_map/ppermute | solution.py:30
  60.8 1.4 fusion.62
  62.2 0.1 slice_add_fusion.5
  62.4 0.6 convolution_bitcast_fusion.2
  63.0 4.3 %collective-permute-start.8 = (f32[1,64,128]{2,1,0:T(8,128)S(1)}, f32[1,64,128]{2,1,0:T(8,128)S(1)}, u32[]{:S(2)}, u32[]{:S(2)}) collective-permute-start(f32[1,64,128]{2,1,0:T(8,128)S(1)} %get-tuple-element.39), channel_id=1, source_target_pairs={{0,1},{1,2},{2,3},{3,4},{4,5},{5,6},{6,7},{7,8},{8,9},{9,10},{10,1... | collective-permute-start | bytes 98312 | tf_op jit(solution)/shard_map/ppermute | solution.py:20
  67.2 1.3 collective-permute-start.9
  68.5 0.4 convolution_bitcast_fusion.4
  68.9 0.9 broadcast_in_dim.14
  69.8 9.0 %all-to-all-start.1 = ((f32[16,64,128]{2,1,0:T(8,128)}), f32[16,64,128]{2,1,0:T(8,128)S(1)}, u32[]{:S(2)}, u32[]{:S(2)}) async-start(f32[16,64,128]{2,1,0:T(8,128)} %broadcast_in_dim.14), calls=%async_computation.1 | async-start | bytes 1048576 | tf_op jit(solution)/shard_map/all_to_all | solution.py:37
  78.9 0.1 pad_maximum_fusion.5
  79.0 1.0 copy-done.8
  79.9 2.4 %fusion.50 = f32[14,64,128]{2,1,0:T(8,128)S(1)} fusion(f32[1,64,128]{2,1,0:T(8,128)S(1)} %collective-permute-done.9, f32[12,64,128]{2,1,0:T(8,128)S(1)} %convolution_bitcast_fusion.2, f32[1,64,128]{2,1,0:T(8,128)S(1)} %collective-permute-done.8, f32[14,64,128]{2,1,0:T(8,128)S(1)} %get-tuple-element.28, f32[14,64,128]{2,1,0:T(8,128)S(1)} %get-tuple-element.27, ...), kind=kOutput, calls=%fused_computation.54 | convolution fusion | flops 266993664 | bytes 2501120 | tf_op jit(solution)/shard_map/bij,bjc->bic/dot_general | solution.py:13
  82.4 0.1 fusion.152
  82.5 2.4 %fusion.59 = f32[14,64,128]{2,1,0:T(8,128)S(1)} fusion(f32[13,64,128]{2,1,0:T(8,128)S(1)} %get-tuple-element.21, f32[13,64,128]{2,1,0:T(8,128)S(1)} %get-tuple-element.20, f32[14,64,128]{2,1,0:T(8,128)S(1)} %fusion.50, f32[1,64,128]{2,1,0:T(8,128)S(1)} %collective-permute-done.9, f32[12,64,128]{2,1,0:T(8,128)S(1)} %convolution_bitcast_fusion.2, ...), kind=kOutput, calls=%fused_computation.57 | convolution fusion | flops 268369920 | bytes 2894336 | tf_op jit(solution)/shard_map/bij,bjc->bic/dot_general | solution.py:13
  84.9 0.1 fusion.151
  85.0 3.2 %fusion.1 = f32[14,64,128]{2,1,0:T(8,128)} fusion(f32[13,64,128]{2,1,0:T(8,128)S(1)} %get-tuple-element.19, f32[13,64,128]{2,1,0:T(8,128)S(1)} %get-tuple-element.18, f32[14,64,128]{2,1,0:T(8,128)S(1)} %fusion.59, f32[1,64,128]{2,1,0:T(8,128)} %collective-permute-done.2, f32[1,64,64]{2,1,0:T(8,128)S(1)} %copy-done.13, ...), kind=kOutput, calls=%fused_computation.4 | convolution fusion | flops 268025856 | bytes 2435584 | tf_op jit(solution)/shard_map/bij,bjc->bic/dot_general | solution.py:13
  88.2 4.1 %all-to-all-done.1 = f32[16,64,128]{2,1,0:T(8,128)S(1)} async-done(((f32[16,64,128]{2,1,0:T(8,128)}), f32[16,64,128]{2,1,0:T(8,128)S(1)}, u32[]{:S(2)}, u32[]{:S(2)}) %all-to-all-start.1) | async-done | bytes 524320 | tf_op jit(solution)/shard_map/all_to_all | solution.py:37
  92.3 0.4 fusion.105
  92.8 0.5 convolution_bitcast_fusion.1
  93.3 0.2 copy.14
  93.5 0.3 copy-done.11
  94.0 2.3 %collective-permute-start.10 = (f32[1,64,128]{2,1,0:T(8,128)S(1)}, f32[1,64,128]{2,1,0:T(8,128)S(1)}, u32[]{:S(2)}, u32[]{:S(2)}) collective-permute-start(f32[1,64,128]{2,1,0:T(8,128)S(1)} %get-tuple-element.35), channel_id=1, source_target_pairs={{0,1},{1,2},{2,3},{3,4},{4,5},{5,6},{6,7},{7,8},{8,9},{9,10},{10,1... | collective-permute-start | bytes 98312 | tf_op jit(solution)/shard_map/ppermute | solution.py:20
  96.3 1.3 collective-permute-start.11
  97.6 8.1 %collective-permute-start.12 = (f32[12,16,128]{2,1,0:T(8,128)S(1)}, f32[12,16,128]{2,1,0:T(8,128)S(1)}, u32[]{:S(2)}, u32[]{:S(2)}) collective-permute-start(f32[12,16,128]{2,1,0:T(8,128)S(1)} %get-tuple-element.33), channel_id=1, source_target_pairs={{16,32},{48,64},{80,96},{112,128},{144,160},{176,192},{208,224},{2... | collective-permute-start | bytes 294920 | tf_op jit(solution)/shard_map/ppermute | solution.py:29
  105.8 1.9 %collective-permute-start.13 = (f32[12,16,128]{2,1,0:T(8,128)S(1)}, f32[12,16,128]{2,1,0:T(8,128)S(1)}, u32[]{:S(2)}, u32[]{:S(2)}) collective-permute-start(f32[12,16,128]{2,1,0:T(8,128)S(1)} %get-tuple-element.34), channel_id=1, source_target_pairs={{0,16},{16,0},{32,48},{48,32},{64,80},{80,64},{96,112},{112,96},{1... | collective-permute-start | bytes 294920 | tf_op jit(solution)/shard_map/ppermute | solution.py:30
  107.7 1.4 fusion.72
  109.2 0.1 slice_add_fusion.3
  109.3 0.2 multiply_reduce_fusion.1
  109.5 2.0 %all_gather.3 = f32[2,1,640]{2,1,0:T(1,128)S(1)} all-gather(f32[1,1,640]{2,1,0:T(1,128)S(1)} %all_gather_reshape.3), channel_id=1, replica_groups={{0,16},{32,48},{64,80},{96,112},{128,144},{160,176},{192,208},{224,240}..., dimensions={0}, use_global_device_ids=true | all-gather | bytes 7680 | tf_op jit(solution)/shard_map/all_gather | solution.py:47
  111.6 22.3 %all_to_all.20 = f32[16,1,640]{2,1,0:T(1,128)S(1)} all-to-all(f32[16,1,640]{2,1,0:T(1,128)S(1)} %broadcast_in_dim.15), channel_id=1, replica_groups={{0,32,64,96,128,160,192,224,256,288,320,352,384,416,448,480},{16,48,80,..., dimensions={0} | all-to-all | bytes 81920 | tf_op jit(solution)/shard_map/all_to_all | solution.py:49
  134.0 15.5 %all_to_all.21 = f32[16,1,640]{2,1,0:T(1,128)S(1)} all-to-all(f32[16,1,640]{2,1,0:T(1,128)S(1)} %broadcast_in_dim.16), channel_id=1, replica_groups=mesh['sec'=32,'sub'=16] {'sub'}, dimensions={0} | all-to-all | bytes 81920 | tf_op jit(solution)/shard_map/all_to_all | solution.py:51
  149.6 0.8 add_bitcast_fusion
  (70 shorter events, 0.6 us)
Async XLA Ops:
  0.0 40.3 %copy-start = (f32[1,64,1024]{2,1,0:T(8,128)S(1)}, f32[1,64,1024]{2,1,0:T(8,128)}, u32[]{:S(2)}) copy-start(f32[1,64,1024]{2,1,0:T(8,128)} %param.11) | copy-start | bytes 786436
  0.0 1.2 copy-start.2
  0.0 1.3 copy-start.9
  1.1 59.6 %copy-start.4 = (f32[12,64,64]{2,1,0:T(8,128)}, f32[12,64,64]{2,1,0:T(8,128)S(1)}, u32[]{:S(2)}) copy-start(f32[12,64,64]{2,1,0:T(8,128)S(1)} %slice_bitcast_fusion) | copy-start | bytes 589828
  1.3 2.5 %copy-start.1 = (f32[1,12,64,128]{3,2,1,0:T(8,128)S(1)}, f32[1,12,64,128]{3,2,1,0:T(8,128)}, u32[]{:S(2)}) copy-start(f32[1,12,64,128]{3,2,1,0:T(8,128)} %param.6) | copy-start | bytes 1179652
  2.2 8.1 %copy-start.6 = (f32[12,64,192]{2,1,0:T(8,128)}, f32[12,64,192]{2,1,0:T(8,128)S(1)}, u32[]{:S(2)}) copy-start(f32[12,64,192]{2,1,0:T(8,128)S(1)} %fusion.49) | copy-start | bytes 1769476
  2.2 12.7 %copy-start.3 = (f32[1,64,768]{2,1,0:T(8,128)S(1)}, f32[1,64,768]{2,1,0:T(8,128)}, u32[]{:S(2)}) copy-start(f32[1,64,768]{2,1,0:T(8,128)} %param.10) | copy-start | bytes 589828
  2.3 25.4 %collective-permute-start.3 = (f32[1,64,128]{2,1,0:T(8,128)S(1)}, f32[1,64,128]{2,1,0:T(8,128)S(1)}, u32[]{:S(2)}, u32[]{:S(2)}) collective-permute-start(f32[1,64,128]{2,1,0:T(8,128)S(1)} %pad_maximum_fusion.7), channel_id=1, source_target_pairs={{1,0},{2,1},{3,2},{4,3},{5,4},{6,5},{7,6},{8,7},{9,8},{10,9},{11,1... | collective-permute-start | bytes 98312 | tf_op jit(solution)/shard_map/ppermute | solution.py:20
  4.3 23.4 %collective-permute-start = (f32[1,64,128]{2,1,0:T(8,128)S(1)}, f32[1,64,128]{2,1,0:T(8,128)S(1)}, u32[]{:S(2)}, u32[]{:S(2)}) collective-permute-start(f32[1,64,128]{2,1,0:T(8,128)S(1)} %get-tuple-element.47), channel_id=1, source_target_pairs={{0,1},{1,2},{2,3},{3,4},{4,5},{5,6},{6,7},{7,8},{8,9},{9,10},{10,1... | collective-permute-start | bytes 98312 | tf_op jit(solution)/shard_map/ppermute | solution.py:20
  8.9 18.9 %collective-permute-start.1 = (f32[1,64,128]{2,1,0:T(8,128)S(1)}, f32[1,64,128]{2,1,0:T(8,128)S(1)}, u32[]{:S(2)}, u32[]{:S(2)}) collective-permute-start(f32[1,64,128]{2,1,0:T(8,128)S(1)} %get-tuple-element.48), channel_id=1, source_target_pairs={{1,0},{2,1},{3,2},{4,3},{5,4},{6,5},{7,6},{8,7},{9,8},{10,9},{11,1... | collective-permute-start | bytes 98312 | tf_op jit(solution)/shard_map/ppermute | solution.py:20
  10.3 17.6 %collective-permute-start.2 = (f32[1,64,128]{2,1,0:T(8,128)S(1)}, f32[1,64,128]{2,1,0:T(8,128)}, u32[]{:S(2)}, u32[]{:S(2)}) collective-permute-start(f32[1,64,128]{2,1,0:T(8,128)S(1)} %slice.203), channel_id=1, source_target_pairs={{0,1},{1,2},{2,3},{3,4},{4,5},{5,6},{6,7},{7,8},{8,9},{9,10},{10,1... | collective-permute-start | bytes 98312 | tf_op jit(solution)/shard_map/ppermute | solution.py:20
  15.3 12.2 %copy-start.16 = (f32[1,12,32]{2,0,1:T(1,128)S(1)}, f32[1,12,32]{2,0,1:T(1,128)}, u32[]{:S(2)}) copy-start(f32[1,12,32]{2,0,1:T(1,128)} %param.9) | copy-start | bytes 4612
  16.1 24.2 %all-to-all-start = ((f32[16,64,128]{2,1,0:T(8,128)}), f32[16,64,128]{2,1,0:T(8,128)S(1)}, u32[]{:S(2)}, u32[]{:S(2)}) async-start(f32[16,64,128]{2,1,0:T(8,128)} %broadcast_in_dim.13), calls=%async_computation | async-start | bytes 1048576 | tf_op jit(solution)/shard_map/all_to_all | solution.py:37
  27.7 6.3 %copy-start.14 = (f32[14,192]{1,0:T(8,128)}, f32[14,192]{1,0:T(8,128)S(1)}, u32[]{:S(2)}) copy-start(f32[14,192]{1,0:T(8,128)S(1)} %pad.67.clone) | copy-start | bytes 32260
  27.8 6.2 %copy-start.12 = (f32[1,64,64]{2,1,0:T(8,128)}, f32[1,64,64]{2,1,0:T(8,128)S(1)}, u32[]{:S(2)}) copy-start(f32[1,64,64]{2,1,0:T(8,128)S(1)} %get-tuple-element.50) | copy-start | bytes 49156
  27.8 1.2 copy-start.7
  42.6 18.1 %collective-permute-start.4 = (f32[1,64,128]{2,1,0:T(8,128)S(1)}, f32[1,64,128]{2,1,0:T(8,128)S(1)}, u32[]{:S(2)}, u32[]{:S(2)}) collective-permute-start(f32[1,64,128]{2,1,0:T(8,128)S(1)} %get-tuple-element.43), channel_id=1, source_target_pairs={{0,1},{1,2},{2,3},{3,4},{4,5},{5,6},{6,7},{7,8},{8,9},{9,10},{10,1... | collective-permute-start | bytes 98312 | tf_op jit(solution)/shard_map/ppermute | solution.py:20
  44.9 15.9 %collective-permute-start.5 = (f32[1,64,128]{2,1,0:T(8,128)S(1)}, f32[1,64,128]{2,1,0:T(8,128)S(1)}, u32[]{:S(2)}, u32[]{:S(2)}) collective-permute-start(f32[1,64,128]{2,1,0:T(8,128)S(1)} %get-tuple-element.44), channel_id=1, source_target_pairs={{1,0},{2,1},{3,2},{4,3},{5,4},{6,5},{7,6},{8,7},{9,8},{10,9},{11,1... | collective-permute-start | bytes 98312 | tf_op jit(solution)/shard_map/ppermute | solution.py:20
  46.2 16.0 %collective-permute-start.6 = (f32[12,16,128]{2,1,0:T(8,128)S(1)}, f32[12,16,128]{2,1,0:T(8,128)S(1)}, u32[]{:S(2)}, u32[]{:S(2)}) collective-permute-start(f32[12,16,128]{2,1,0:T(8,128)S(1)} %get-tuple-element.41), channel_id=1, source_target_pairs={{16,32},{48,64},{80,96},{112,128},{144,160},{176,192},{208,224},{2... | collective-permute-start | bytes 294920 | tf_op jit(solution)/shard_map/ppermute | solution.py:29
  58.8 3.4 %collective-permute-start.7 = (f32[12,16,128]{2,1,0:T(8,128)S(1)}, f32[12,16,128]{2,1,0:T(8,128)S(1)}, u32[]{:S(2)}, u32[]{:S(2)}) collective-permute-start(f32[12,16,128]{2,1,0:T(8,128)S(1)} %get-tuple-element.42), channel_id=1, source_target_pairs={{0,16},{16,0},{32,48},{48,32},{64,80},{80,64},{96,112},{112,96},{1... | collective-permute-start | bytes 294920 | tf_op jit(solution)/shard_map/ppermute | solution.py:30
  63.0 15.9 %collective-permute-start.8 = (f32[1,64,128]{2,1,0:T(8,128)S(1)}, f32[1,64,128]{2,1,0:T(8,128)S(1)}, u32[]{:S(2)}, u32[]{:S(2)}) collective-permute-start(f32[1,64,128]{2,1,0:T(8,128)S(1)} %get-tuple-element.39), channel_id=1, source_target_pairs={{0,1},{1,2},{2,3},{3,4},{4,5},{5,6},{6,7},{7,8},{8,9},{9,10},{10,1... | collective-permute-start | bytes 98312 | tf_op jit(solution)/shard_map/ppermute | solution.py:20
  67.2 11.6 %collective-permute-start.9 = (f32[1,64,128]{2,1,0:T(8,128)S(1)}, f32[1,64,128]{2,1,0:T(8,128)S(1)}, u32[]{:S(2)}, u32[]{:S(2)}) collective-permute-start(f32[1,64,128]{2,1,0:T(8,128)S(1)} %get-tuple-element.40), channel_id=1, source_target_pairs={{1,0},{2,1},{3,2},{4,3},{5,4},{6,5},{7,6},{8,7},{9,8},{10,9},{11,1... | collective-permute-start | bytes 98312 | tf_op jit(solution)/shard_map/ppermute | solution.py:20
  69.8 22.5 %all-to-all-start.1 = ((f32[16,64,128]{2,1,0:T(8,128)}), f32[16,64,128]{2,1,0:T(8,128)S(1)}, u32[]{:S(2)}, u32[]{:S(2)}) async-start(f32[16,64,128]{2,1,0:T(8,128)} %broadcast_in_dim.14), calls=%async_computation.1 | async-start | bytes 1048576 | tf_op jit(solution)/shard_map/all_to_all | solution.py:37
  78.8 1.1 copy-start.8
  78.8 1.1 copy-start.13
  78.8 1.1 copy-start.15
  92.8 1.0 copy-start.11
  93.9 13.9 %copy-start.5 = (f32[12,64,64]{2,1,0:T(8,128)S(1)}, f32[12,64,64]{2,1,0:T(8,128)}, u32[]{:S(2)}) copy-start(f32[12,64,64]{2,1,0:T(8,128)} %copy-done.4) | copy-start | bytes 589828
  93.9 13.9 %copy-start.10 = (f32[1,12,64,128]{3,2,1,0:T(8,128)S(1)}, f32[1,12,64,128]{3,2,1,0:T(8,128)}, u32[]{:S(2)}) copy-start(f32[1,12,64,128]{3,2,1,0:T(8,128)} %param.7) | copy-start | bytes 1179652
  94.0 13.7 %collective-permute-start.10 = (f32[1,64,128]{2,1,0:T(8,128)S(1)}, f32[1,64,128]{2,1,0:T(8,128)S(1)}, u32[]{:S(2)}, u32[]{:S(2)}) collective-permute-start(f32[1,64,128]{2,1,0:T(8,128)S(1)} %get-tuple-element.35), channel_id=1, source_target_pairs={{0,1},{1,2},{2,3},{3,4},{4,5},{5,6},{6,7},{7,8},{8,9},{9,10},{10,1... | collective-permute-start | bytes 98312 | tf_op jit(solution)/shard_map/ppermute | solution.py:20
  96.3 11.4 %collective-permute-start.11 = (f32[1,64,128]{2,1,0:T(8,128)S(1)}, f32[1,64,128]{2,1,0:T(8,128)S(1)}, u32[]{:S(2)}, u32[]{:S(2)}) collective-permute-start(f32[1,64,128]{2,1,0:T(8,128)S(1)} %get-tuple-element.36), channel_id=1, source_target_pairs={{1,0},{2,1},{3,2},{4,3},{5,4},{6,5},{7,6},{8,7},{9,8},{10,9},{11,1... | collective-permute-start | bytes 98312 | tf_op jit(solution)/shard_map/ppermute | solution.py:20
  97.6 11.5 %collective-permute-start.12 = (f32[12,16,128]{2,1,0:T(8,128)S(1)}, f32[12,16,128]{2,1,0:T(8,128)S(1)}, u32[]{:S(2)}, u32[]{:S(2)}) collective-permute-start(f32[12,16,128]{2,1,0:T(8,128)S(1)} %get-tuple-element.33), channel_id=1, source_target_pairs={{16,32},{48,64},{80,96},{112,128},{144,160},{176,192},{208,224},{2... | collective-permute-start | bytes 294920 | tf_op jit(solution)/shard_map/ppermute | solution.py:29
  105.8 3.4 %collective-permute-start.13 = (f32[12,16,128]{2,1,0:T(8,128)S(1)}, f32[12,16,128]{2,1,0:T(8,128)S(1)}, u32[]{:S(2)}, u32[]{:S(2)}) collective-permute-start(f32[12,16,128]{2,1,0:T(8,128)S(1)} %get-tuple-element.34), channel_id=1, source_target_pairs={{0,16},{16,0},{32,48},{48,32},{64,80},{80,64},{96,112},{112,96},{1... | collective-permute-start | bytes 294920 | tf_op jit(solution)/shard_map/ppermute | solution.py:30

commit v2 on v1

v2 whole, which is shorter than its diff:
```python
import jax
import jax.numpy as jnp
from jax import lax
from jax.experimental import pallas as pl
from jax.experimental.pallas import tpu as pltpu
from jax.sharding import PartitionSpec as P

SWEEPS = 4
SCALE = 2.0**-16

PRECISE = lax.Precision.HIGHEST


def dot(left, right):
    return jnp.dot(left, right, precision=PRECISE, preferred_element_type=jnp.float32)


def pairings(axis):
    count = lax.axis_size(axis)
    near = [(i, i ^ 1) for i in range(count)]
    low = [(i, i + 1) for i in range(1, count - 1, 2)]
    return near, low + [(target, source) for source, target in low]


def swap(to_near, to_far, axis):
    near, far = pairings(axis)
    from_far = lax.ppermute(to_far, axis, far)
    return lax.ppermute(to_near, axis, near), from_far


def gather_sub(spread):
    return lax.all_to_all(spread, "sub", 0, 0, tiled=True).reshape(-1, *spread.shape[2:])


def total(sums):
    shape = sums.shape
    flat = sums.reshape(1, -1)
    sections, subs = lax.axis_size("sec"), lax.axis_size("sub")
    pairs = [[2 * g, 2 * g + 1] for g in range(sections // 2)]
    alike = [[2 * g + p for g in range(sections // 2)] for p in range(2)]
    flat = jnp.sum(lax.all_gather(flat, "sec", axis_index_groups=pairs), axis=0)
    spread = jnp.broadcast_to(flat[None], (sections // 2, *flat.shape))
    flat = jnp.sum(lax.all_to_all(spread, "sec", 0, 0, axis_index_groups=alike, tiled=True), axis=0)
    spread = jnp.broadcast_to(flat[None], (subs, *flat.shape))
    flat = jnp.sum(lax.all_to_all(spread, "sub", 0, 0, tiled=True), axis=0)
    return flat.reshape(shape)


def split(value):
    high = value.astype(jnp.bfloat16)
    return high, (value - high.astype(jnp.float32)).astype(jnp.bfloat16)


def rows_split(value):
    return jnp.concatenate(split(value), axis=0)


def columns_split(value):
    return jnp.concatenate(split(value), axis=1)


def product(rows, columns):
    all_four = jnp.dot(rows, columns, preferred_element_type=jnp.float32)
    half, width = all_four.shape[0] // 2, all_four.shape[1] // 2
    top = all_four[:half, :width] + (all_four[:half, width:] + all_four[half:, :width])
    return top + all_four[half:, width:]


def prepare_kernel(odd, side, coupling_in, pair_in, residual_in, basis_in, inverse_in, sweep, tiles, start, near, far, sides, basis_rows, basis_columns, coarse_rows, coupling, pair, residual, basis, inverse_rows, sems):
    blocks, nodes, columns = residual.shape
    loads = [
        pltpu.make_async_copy(source, target, sems.at[i])
        for i, (source, target) in enumerate(
            (
                (pair_in, pair),
                (coupling_in, coupling),
                (residual_in, residual),
                (inverse_in, inverse_rows),
                (basis_in, basis),
            )
        )
    ]
    for load in loads:
        load.start()
    for load in loads[:3]:
        load.wait()
    row = lax.broadcasted_iota(jnp.int32, (nodes, nodes), 0)
    own = (row == lax.broadcasted_iota(jnp.int32, (nodes, nodes), 1)).astype(jnp.float32)
    for b in range(blocks):
        inverse = pair[b][:, nodes:]
        direct = pair[b][:, :nodes]
        start[b] = dot(inverse, residual[b])
        beside = -dot(inverse, coupling[b])
        centre = own - dot(inverse, direct)
        high, low = split(beside)
        sweep[b, :nodes, : 2 * nodes] = high
        sweep[b, nodes:, : 2 * nodes] = low
        high, low = split(centre)
        sweep[b, :nodes, 2 * nodes :] = high
        sweep[b, nodes:, 2 * nodes :] = low
        high, low = split(coupling[b])
        tiles[b, :nodes, : 2 * nodes] = high
        tiles[b, nodes:, : 2 * nodes] = low
        high, low = split(direct)
        tiles[b, :nodes, 2 * nodes :] = high
        tiles[b, nodes:, 2 * nodes :] = low
        if b == 0:
            to_previous = jnp.concatenate([beside[:, :nodes], centre], axis=1)
        if b == blocks - 1:
            to_next = jnp.concatenate([beside[:, nodes:], centre], axis=1)
        sides[b] = jnp.broadcast_to(side[b : b + 1].T, sides.shape[1:])
    even = odd[1] == 0
    near[:nodes] = jnp.where(even, start[blocks - 1], start[0])
    far[:nodes] = jnp.where(even, start[0], start[blocks - 1])
    near[nodes:] = jnp.where(even, to_next, to_previous)
    far[nodes:] = jnp.where(even, to_previous, to_next)
    for load in loads[3:]:
        load.wait()
    coarse_rows[...] = rows_split(inverse_rows[...])
    parts = rows_split(basis[...])
    basis_rows[...] = parts
    basis_columns[...] = parts.astype(jnp.float32).T.astype(jnp.bfloat16)


def first_sweep_kernel(tiles, start, out):
    blocks, nodes, _ = start.shape
    parts = [columns_split(start[b]) for b in range(blocks)]
    nothing = jnp.zeros_like(parts[0])
    for b in range(blocks):
        before = parts[b - 1] if b else nothing
        after = parts[b + 1] if b + 1 < blocks else nothing
        out[b] = start[b] + product(tiles[b], jnp.concatenate([before, after, parts[b]], axis=0))


def sweep_kernel(odd, tiles, start, partial, near, far, near_tile, far_tile, out, one, two):
    blocks, nodes, _ = start.shape
    even = odd[1] == 0
    low = jnp.where(even, far[:nodes], near[:nodes])
    high = jnp.where(even, near[:nodes], far[:nodes])
    low_tile = rows_split(jnp.where(even, far_tile[nodes:], near_tile[nodes:]))
    high_tile = rows_split(jnp.where(even, near_tile[nodes:], far_tile[nodes:]))
    low_parts, high_parts = columns_split(low), columns_split(high)
    first, last = columns_split(start[0]), columns_split(start[blocks - 1])
    one[0] = columns_split(low + product(low_tile, jnp.concatenate([first, low_parts], axis=0)))
    one[blocks + 1] = columns_split(high + product(high_tile, jnp.concatenate([last, high_parts], axis=0)))
    one[1] = columns_split(partial[0] + product(tiles[0][:, :nodes], low_parts))
    one[blocks] = columns_split(partial[blocks - 1] + product(tiles[blocks - 1][:, nodes : 2 * nodes], high_parts))
    for b in range(1, blocks - 1):
        one[b + 1] = columns_split(partial[b])
    source, target = one, two
    for sweep in range(1, SWEEPS - 1):
        final = sweep == SWEEPS - 2
        for b in range(blocks):
            near_by = jnp.concatenate([source[b], source[b + 2], source[b + 1]], axis=0)
            new = start[b] + product(tiles[b], near_by)
            if final:
                out[b] = new
            else:
                target[b + 1] = columns_split(new)
        if not final:
            target[0] = columns_split(low + product(low_tile, jnp.concatenate([source[1], source[0]], axis=0)))
            target[blocks + 1] = columns_split(
                high + product(high_tile, jnp.concatenate([source[blocks], source[blocks + 1]], axis=0))
            )
        source, target = target, source


def update_kernel(odd, coarse_rows, gathered, basis_columns, local, update, near_face, far_face, near_block, far_block):
    blocks, nodes, _ = local.shape
    faces = near_face.shape[1]
    correction = columns_split(product(coarse_rows[...], columns_split(gathered[...])))
    width = correction.shape[1] // 2
    correction = jnp.concatenate([correction, correction], axis=0)
    for b in range(blocks):
        both = jnp.dot(
            basis_columns[b * nodes : (b + 1) * nodes], correction, preferred_element_type=jnp.float32
        )
        new = local[b] + (both[:, :width] + both[:, width:])
        update[b] = new
        south, north = new[:faces], new[nodes - faces :]
        even = odd[0] == 0
        near_face[b] = jnp.where(even, north, south)
        far_face[b] = jnp.where(even, south, north)
    even = odd[1] == 0
    near_block[...] = jnp.where(even, update[blocks - 1], update[0])
    far_block[...] = jnp.where(even, update[0], update[blocks - 1])


def image_blocks(odd, tiles, sides, update, near_face, far_face, near_block, far_block):
    blocks, nodes, _ = update.shape
    faces = near_face.shape[1]
    even = odd[1] == 0
    low = jnp.where(even, far_block[...], near_block[...])
    high = jnp.where(even, near_block[...], far_block[...])
    parts = [columns_split(value) for value in (low, *(update[b] for b in range(blocks)), high)]
    even = odd[0] == 0
    for b in range(blocks):
        linear = product(tiles[b], jnp.concatenate([parts[b], parts[b + 2], parts[b + 1]], axis=0))
        below = jnp.where(even, far_face[b], near_face[b])
        above = jnp.where(even, near_face[b], far_face[b])
        yield b, jnp.concatenate(
            [
                linear[:faces] + sides[b, :faces] * below,
                linear[faces : nodes - faces],
                linear[nodes - faces :] + sides[b, faces:] * above,
            ],
            axis=0,
        )


def send_out(projected, spread, sems):
    copies = [
        pltpu.make_async_copy(projected, spread.at[i], sems.at[i]) for i in range(spread.shape[0])
    ]
    for copy in copies:
        copy.start()
    return copies


def image_kernel(odd, tiles, sides, basis_rows, pair, residual, update, far_face, near_face, far_block, near_block, image_out, rest_out, spread, start, near, far, image, rest, flat, projected, sems, stores):
    blocks, nodes, _ = update.shape
    for b, new in image_blocks(odd, tiles, sides, update, near_face, far_face, near_block, far_block):
        image[b] = new
        left = residual[b] - new
        rest[b] = left
        flat[b * nodes : (b + 1) * nodes] = columns_split(left)
    projected[...] = product(basis_rows[...], flat[...])
    copies = send_out(projected, spread, sems)
    for i, (source, target) in enumerate(((image, image_out), (rest, rest_out))):
        copies.append(pltpu.make_async_copy(source, target, stores.at[i]))
        copies[-1].start()
    for b in range(blocks):
        start[b] = product(rows_split(pair[b][:, nodes:]), flat[b * nodes : (b + 1) * nodes])
    even = odd[1] == 0
    near[...] = jnp.where(even, start[blocks - 1], start[0])
    far[...] = jnp.where(even, start[0], start[blocks - 1])
    for copy in copies:
        copy.wait()


def project_kernel(basis, field, spread, projected, sems):
    blocks, nodes, columns = field.shape
    projected[...] = dot(basis[...], field[...].reshape(blocks * nodes, columns))
    for copy in send_out(projected, spread, sems):
        copy.wait()


def sums_kernel(odd, tiles, sides, image, rest, update, far_face, near_face, far_block, near_block, sums):
    nodes, columns = update.shape[1:]
    parts = [jnp.zeros((8, columns), jnp.float32) for _ in range(5)]

    def inner(left, right):
        return jnp.sum((left * right).reshape(nodes // 8, 8, columns), axis=0)

    for b, new in image_blocks(odd, tiles, sides, update, near_face, far_face, near_block, far_block):
        change = new * SCALE
        left, right = image[b], rest[b]
        for i, (x, y) in enumerate(((left, right), (left, left), (change, right), (change, left), (change, change))):
            parts[i] = parts[i] + inner(x, y)
    for i in range(5):
        sums[i : i + 1] = jnp.sum(parts[i], axis=0, keepdims=True)


def call(kernel, outs, scratch, *operands, slow=0):
    spaces = [pltpu.VMEM] * (len(operands) - slow) + [pltpu.HBM] * slow
    spaces = [pltpu.SMEM if operand.dtype == jnp.int32 else space for operand, space in zip(operands, spaces)]
    return pl.pallas_call(
        kernel,
        out_shape=[space(shape, kind) for shape, kind, space in outs],
        in_specs=[pl.BlockSpec(memory_space=space) for space in spaces],
        out_specs=[pl.BlockSpec(memory_space=space) for _, _, space in outs],
        scratch_shapes=scratch,
        compiler_params=pltpu.CompilerParams(vmem_limit_bytes=12 << 20),
        cost_estimate=pl.CostEstimate(flops=1000, transcendentals=0, bytes_accessed=1000),
    )(
        *(
            operand if space is pltpu.SMEM else pltpu.with_memory_space_constraint(operand, space)
            for operand, space in zip(operands, spaces)
        )
    )


def shards(forcing, coupling, diag_pair, side, basis, coarse_inverse):
    residual = forcing[0]
    basis_all = basis[0]
    blocks, nodes, columns = residual.shape
    faces = side.shape[2] // 2
    coarse, own_coarse = coarse_inverse.shape[2], coarse_inverse.shape[1]
    odd = jnp.stack([lax.axis_index("sec") % 2, lax.axis_index("sub") % 2]).astype(jnp.int32)
    wide, thin, fast = jnp.float32, jnp.bfloat16, pltpu.VMEM
    subs = lax.axis_size("sub")
    block = ((nodes, columns), wide, fast)
    field = ((blocks, nodes, columns), wide, fast)
    kept = ((blocks, nodes, columns), wide, pltpu.HBM)
    face = ((blocks, faces, columns), wide, fast)
    tile = ((blocks, 2 * nodes, 3 * nodes), thin, fast)
    padded = pltpu.VMEM((blocks + 2, nodes, 2 * columns), thin)
    spread_out = ((subs, own_coarse, columns), wide, pltpu.HBM)
    spreading = [pltpu.VMEM((own_coarse, columns), wide), pltpu.SemaphoreType.DMA((subs,))]

    (spread,) = call(project_kernel, [spread_out], spreading, basis_all, residual)
    spread, odd, residual, coupling, diag_pair, side, basis_all = lax.optimization_barrier(
        (spread, odd, residual, coupling, diag_pair, side, basis_all)
    )
    pair = diag_pair[0]
    sweep, tiles, start, near, far, sides, basis_rows, basis_columns, coarse_rows = call(
        prepare_kernel,
        [
            tile,
            tile,
            field,
            ((2 * nodes, columns), wide, fast),
            ((2 * nodes, columns), wide, fast),
            ((blocks, 2 * faces, columns), wide, fast),
            ((2 * own_coarse, blocks * nodes), thin, fast),
            ((blocks * nodes, 2 * own_coarse), thin, fast),
            ((2 * own_coarse, coarse), thin, fast),
        ],
        [
            pltpu.VMEM((blocks, nodes, columns), wide),
            pltpu.VMEM((blocks, nodes, columns), wide),
            pltpu.VMEM((blocks, nodes, columns), wide),
            pltpu.VMEM(basis_all.shape, wide),
            pltpu.VMEM((own_coarse, coarse), wide),
            pltpu.SemaphoreType.DMA((5,)),
        ],
        odd, side[0], coupling[0], pair, residual, basis_all, coarse_inverse[0],
        slow=5,
    )

    def precondition(start, near, far, near_tile, far_tile, spread):
        gathered = gather_sub(spread)
        (partial,) = call(first_sweep_kernel, [field], [], sweep, start)
        (local,) = call(sweep_kernel, [field], [padded] * 2, odd, sweep, start, partial, near, far, near_tile, far_tile)
        update, near_face, far_face, near_block, far_block = call(
            update_kernel, [field, face, face, block, block], [], odd, coarse_rows, gathered, basis_columns, local
        )
        faces_in = swap(near_face, far_face, "sec")
        blocks_in = swap(near_block, far_block, "sub")
        return update, *faces_in[::-1], *blocks_in[::-1]

    halo = swap(near, far, "sub")
    first, *given = precondition(start, *halo, *halo, spread)
    image, rest, spread, start, near, far = call(
        image_kernel,
        [kept, kept, spread_out, field, block, block],
        [
            pltpu.VMEM((blocks, nodes, columns), wide),
            pltpu.VMEM((blocks, nodes, columns), wide),
            pltpu.VMEM((blocks * nodes, 2 * columns), thin),
            *spreading,
            pltpu.SemaphoreType.DMA((2,)),
        ],
        odd, tiles, sides, basis_rows, pair, residual, first, *given,
    )
    second, *given = precondition(start, *swap(near, far, "sub"), *halo, spread)
    (sums,) = call(sums_kernel, [((5, columns), wide, fast)], [], odd, tiles, sides, image, rest, second, *given)
    sums = total(sums)
    short = -sums[0] / sums[1]
    step = 1.0 - short
    upper = step * (sums[2] + short * sums[3])
    scaled = step / SCALE
    lower = short * short * sums[1] + 2.0 * short * scaled * sums[3] + scaled * scaled * sums[4]
    step_next = upper / SCALE / lower
    result = (step + step_next * short) * first + (step_next * step) * second
    return result[None]


def solution(mesh):
    placed = (
        P("sec", "sub", None, None),
        P("sec", "sub", None, None),
        P("sec", "sub", None, None),
        P("sec", "sub", None),
        P("sec", "sub", None),
        P("sec", "sub", None),
    )
    return jax.shard_map(
        shards, mesh=mesh, in_specs=placed, out_specs=P("sec", "sub", None, None), check_vma=False
    )
```

time: 152 us -> 132 us (0.87)
  matrix products: 23.6 us -> 0 us
  Pallas kernels: 0 us -> 14 us
  starting transfers between devices: 69.5 us -> 57.2 us
  waiting for transfers between devices: 7.26 us -> 13.9 us
  local copies, waits for them, and re-layouts: 6.57 us -> 3 us
  other arithmetic: 2.86 us -> 0.99 us
    dot_general x17 -> x0, matrix products: 23.6 us -> none  [the longest x11 21 us: tile_apply(): return jnp.einsum('bij,bjc->bic', tile_set, vector, precision=precision)]
    pallas_call x0 -> x10, Pallas kernels: none -> 14 us  [call(): pl.pallas_call(kernel, out_shape=[space(shape, kind) for shape, kind, spa...]
    ppermute x14 -> x12, starting transfers between devices: 49.2 us -> 38.5 us  [the longest x6 19.4 us: swap(): return (lax.ppermute(to_near, axis, near), from_far)]
    ppermute x14 -> x12, waiting for transfers between devices: 0.04 us -> 4.94 us  [the longest x6 4.93 us: swap(): return (lax.ppermute(to_near, axis, near), from_far)]
    broadcast_in_dim x3 -> x0, local copies, waits for them, and re-layouts: 1.75 us -> none  [the longest x2 1.75 us: gather_sub(): spread = jnp.broadcast_to(value[None], (count, *value.shape))]
    all_to_all x2, waiting for transfers between devices: 7.22 us -> 8.94 us  [gather_sub(): lax.all_to_all(spread, 'sub', 0, 0, tiled=True)]
    all_to_all x2, starting transfers between devices: 20.4 us -> 18.7 us  [gather_sub(): lax.all_to_all(spread, 'sub', 0, 0, tiled=True)]
  transfers between devices with their start and end apart: 16 -> 14, of which waited for: 2 -> 6; matrix products, arithmetic and copies ran while one was open for 15% -> 0% of each run, Pallas kernels for 0% -> 5%
where the time goes in v2:
time: 132 us; the launch traced here: 131 us
  starting transfers between devices  57.2 us (43%)
  blocking collectives  41.2 us (31%)
  Pallas kernels  14 us (11%)
  waiting for transfers between devices  13.9 us (11%)
  local copies, waits for them, and re-layouts  3 us (2%)
    all_to_all x1, blocking collectives, total(): lax.all_to_all(spread, 'sec', 0, 0, axis_index_groups=alike, tiled=True)  23.3 us
    ppermute x6, starting transfers between devices, swap(): return (lax.ppermute(to_near, axis, near), from_far)  19.4 us
    ppermute x6, starting transfers between devices, swap(): from_far = lax.ppermute(to_far, axis, far)  19.1 us
    all_to_all x2, starting transfers between devices, gather_sub(): lax.all_to_all(spread, 'sub', 0, 0, tiled=True)  18.7 us
    all_to_all x1, blocking collectives, total(): flat = jnp.sum(lax.all_to_all(spread, 'sub', 0, 0, tiled=True), axis=0)  14.7 us
    pallas_call x10, Pallas kernels, call(): pl.pallas_call(kernel, out_shape=[space(shape, kind) for shape, kind, spa...  14 us
    all_to_all x2, waiting for transfers between devices, gather_sub(): lax.all_to_all(spread, 'sub', 0, 0, tiled=True)  8.94 us
    ppermute x6, waiting for transfers between devices, swap(): return (lax.ppermute(to_near, axis, near), from_far)  4.93 us
  transfers between devices with their start and end apart: 14, of which 6 were waited for; matrix products, arithmetic and copies ran while one was open for 0% of the time, Pallas kernels for 5%

profile of v2, /device:TPU:1, one launch (start us, length us, event | category | flops | bytes accessed | tf_op | source)
XLA Modules:
  0.0 130.6 jit_solution(10056237354055019403)
XLA Ops:
  0.0 0.1 pad_add_fusion.odd
  0.1 1.0 copy-done
  1.1 0.9 copy-done.5
  2.0 1.3 shard_map.64
  3.3 0.0 copy-start.16
  3.3 10.4 %all-to-all-start = ((f32[16,64,128]{2,1,0:T(8,128)}), f32[16,64,128]{2,1,0:T(8,128)S(1)}, u32[]{:S(2)}, u32[]{:S(2)}) async-start(f32[16,64,128]{2,1,0:T(8,128)} %shard_map.64), calls=%async_computation | async-start | bytes 1048576 | tf_op jit(solution)/shard_map/all_to_all | solution.py:32
  13.7 0.0 copy-done.16
  13.7 3.3 %shard_map.65 = (bf16[12,128,192]{2,1,0:T(8,128)(2,1)S(1)}, bf16[12,128,192]{2,1,0:T(8,128)(2,1)S(1)}, f32[12,64,128]{2,1,0:T(8,128)S(1)}, f32[128,128]{1,0:T(8,...) custom-call(s32[2]{0:T(128)S(1)} %pad_add_fusion.odd, ...), custom_call_target="tpu_custom_call" | custom-call | flops 1000 | bytes 1000 | tf_op jit(solution)/shard_map/pallas_call | solution.py:267
  17.0 0.0 copy-start.14
  17.0 0.0 copy-start.3
  17.0 0.0 copy-start.6
  17.0 3.3 %collective-permute-start = (f32[128,128]{1,0:T(8,128)S(1)}, f32[128,128]{1,0:T(8,128)S(1)}, u32[]{:S(2)}, u32[]{:S(2)}) collective-permute-start(f32[128,128]{1,0:T(8,128)S(1)} %get-tuple-element.51), channel_id=1, source_target_pairs={{0,1},{1,0},{2,3},{3,2},{4,5},{5,4},{6,7},{7,6},{8,9},{9,8},{10,11... | collective-permute-start | bytes 196616 | tf_op jit(solution)/shard_map/ppermute | solution.py:28
  20.3 0.7 collective-permute-start.1
  21.0 0.4 shard_map.66.partial
  21.4 0.0 copy-done.14
  21.4 1.9 %collective-permute-done.near.near_tile = f32[128,128]{1,0:T(8,128)S(1)} collective-permute-done((f32[128,128]{1,0:T(8,128)S(1)}, f32[128,128]{1,0:T(8,128)S(1)}, u32[]{:S(2)}, u32[]{:S(2)}) %collective-permute-start) | collective-permute-done | bytes 65568 | tf_op jit(solution)/shard_map/ppermute | solution.py:28
  23.3 0.0 collective-permute-done.1.far.far_tile
  23.3 1.5 %shard_map.67.local = f32[12,64,128]{2,1,0:T(8,128)S(1)} custom-call(s32[2]{0:T(128)S(1)} %pad_add_fusion.odd, bf16[12,128,192]{2,1,0:T(8,128)(2,1)S(1)} %get-tuple-element.49.tiles, f32[12,64,128]{2,1,0:T(8,128)S(1)} %get-tuple-element.50.start, f32[12,64,128]{2,1,0:T(8,128)S(1)} %shard_map.66.partial, f32[128,128]{1,0:T(8,128)S(1)} %collective-permute-done.near.near_tile, ...), custom_call_target="tpu_custom_call" | custom-call | flops 1000 | bytes 1000 | tf_op jit(solution)/shard_map/pallas_call | solution.py:267
  24.8 0.0 copy-done.8
  24.8 0.0 copy-done.10
  24.8 2.6 %all-to-all-done = f32[16,64,128]{2,1,0:T(8,128)S(1)} async-done(((f32[16,64,128]{2,1,0:T(8,128)}), f32[16,64,128]{2,1,0:T(8,128)S(1)}, u32[]{:S(2)}, u32[]{:S(2)}) %all-to-all-start) | async-done | bytes 524320 | tf_op jit(solution)/shard_map/all_to_all | solution.py:32
  27.5 0.0 copy-done.3
  27.5 1.2 shard_map.68
  28.6 10.5 %collective-permute-start.2 = (f32[12,16,128]{2,1,0:T(8,128)S(1)}, f32[12,16,128]{2,1,0:T(8,128)S(1)}, u32[]{:S(2)}, u32[]{:S(2)}) collective-permute-start(f32[12,16,128]{2,1,0:T(8,128)S(1)} %get-tuple-element.54), channel_id=1, source_target_pairs={{16,32},{48,64},{80,96},{112,128},{144,160},{176,192},{208,224},{2... | collective-permute-start | bytes 294920 | tf_op jit(solution)/shard_map/ppermute | solution.py:27
  39.1 1.9 %collective-permute-start.3 = (f32[12,16,128]{2,1,0:T(8,128)S(1)}, f32[12,16,128]{2,1,0:T(8,128)S(1)}, u32[]{:S(2)}, u32[]{:S(2)}) collective-permute-start(f32[12,16,128]{2,1,0:T(8,128)S(1)} %get-tuple-element.55), channel_id=1, source_target_pairs={{0,16},{16,0},{32,48},{48,32},{64,80},{80,64},{96,112},{112,96},{1... | collective-permute-start | bytes 294920 | tf_op jit(solution)/shard_map/ppermute | solution.py:28
  41.0 0.7 collective-permute-start.4
  41.7 4.7 %collective-permute-start.5 = (f32[64,128]{1,0:T(8,128)S(1)}, f32[64,128]{1,0:T(8,128)S(1)}, u32[]{:S(2)}, u32[]{:S(2)}) collective-permute-start(f32[64,128]{1,0:T(8,128)S(1)} %get-tuple-element.57), channel_id=1, source_target_pairs={{0,1},{1,0},{2,3},{3,2},{4,5},{5,4},{6,7},{7,6},{8,9},{9,8},{10,11... | collective-permute-start | bytes 98312 | tf_op jit(solution)/shard_map/ppermute | solution.py:28
  46.4 0.0 collective-permute-done.4.far_block
  46.4 1.3 collective-permute-done.5.near_block
  47.7 0.0 collective-permute-done.2.far_face
  47.7 0.0 collective-permute-done.3.near_face
  47.7 0.0 copy-done.6
  47.7 0.0 copy-done.1
  47.7 0.0 copy-done.2
  47.7 0.0 copy-done.15
  47.7 2.4 %shard_map.69 = (f32[12,64,128]{2,1,0:T(8,128)}, f32[12,64,128]{2,1,0:T(8,128)}, f32[16,64,128]{2,1,0:T(8,128)}, f32[12,64,128]{2,1,0:T(8,128)S(1)}, f32[64,128]{1,0:T(8,128)S(1)}, /*index=5*/f32[64,128]{1,0:T(8,128)S(1)}) custom-call(s32[2]{0:T(128)S(1)} %pad_add_fusion.odd, bf16[12,128,192]{2,1,0:T(8,128)(2,1)S(1)} %get-tuple-element.43.tiles, ...), custom_call_target="tpu_custom_call" | custom-call | flops 1000 | bytes 1000 | tf_op jit(solution)/shard_map/pallas_call | solution.py:267
  50.2 8.3 %all-to-all-start.1 = ((f32[16,64,128]{2,1,0:T(8,128)}), f32[16,64,128]{2,1,0:T(8,128)S(1)}, u32[]{:S(2)}, u32[]{:S(2)}) async-start(f32[16,64,128]{2,1,0:T(8,128)} %get-tuple-element.60), calls=%async_computation.1 | async-start | bytes 1048576 | tf_op jit(solution)/shard_map/all_to_all | solution.py:32
  58.4 3.3 %collective-permute-start.6 = (f32[64,128]{1,0:T(8,128)S(1)}, f32[64,128]{1,0:T(8,128)S(1)}, u32[]{:S(2)}, u32[]{:S(2)}) collective-permute-start(f32[64,128]{1,0:T(8,128)S(1)} %get-tuple-element.62), channel_id=1, source_target_pairs={{0,1},{1,0},{2,3},{3,2},{4,5},{5,4},{6,7},{7,6},{8,9},{9,8},{10,11... | collective-permute-start | bytes 98312 | tf_op jit(solution)/shard_map/ppermute | solution.py:28
  61.7 0.7 collective-permute-start.7
  62.4 0.0 copy-start.9
  62.4 0.0 copy-start.11
  62.4 0.4 shard_map.70.partial
  62.8 0.4 collective-permute-done.6.near
  63.2 0.0 collective-permute-done.7.far
  63.2 0.0 copy-done.9
  63.2 0.0 copy-done.11
  63.3 1.5 %shard_map.71.local = f32[12,64,128]{2,1,0:T(8,128)S(1)} custom-call(s32[2]{0:T(128)S(1)} %pad_add_fusion.odd, bf16[12,128,192]{2,1,0:T(8,128)(2,1)S(1)} %get-tuple-element.49.tiles, f32[12,64,128]{2,1,0:T(8,128)S(1)} %get-tuple-element.61.start, f32[12,64,128]{2,1,0:T(8,128)S(1)} %shard_map.70.partial, f32[64,128]{1,0:T(8,128)S(1)} %collective-permute-done.6.near, ...), custom_call_target="tpu_custom_call" | custom-call | flops 1000 | bytes 1000 | tf_op jit(solution)/shard_map/pallas_call | solution.py:267
  64.7 6.3 %all-to-all-done.1 = f32[16,64,128]{2,1,0:T(8,128)S(1)} async-done(((f32[16,64,128]{2,1,0:T(8,128)}), f32[16,64,128]{2,1,0:T(8,128)S(1)}, u32[]{:S(2)}, u32[]{:S(2)}) %all-to-all-start.1) | async-done | bytes 524320 | tf_op jit(solution)/shard_map/all_to_all | solution.py:32
  71.1 0.9 copy-done.4
  72.0 1.1 shard_map.72
  73.2 6.0 %collective-permute-start.8 = (f32[12,16,128]{2,1,0:T(8,128)S(1)}, f32[12,16,128]{2,1,0:T(8,128)S(1)}, u32[]{:S(2)}, u32[]{:S(2)}) collective-permute-start(f32[12,16,128]{2,1,0:T(8,128)S(1)} %get-tuple-element.65), channel_id=1, source_target_pairs={{16,32},{48,64},{80,96},{112,128},{144,160},{176,192},{208,224},{2... | collective-permute-start | bytes 294920 | tf_op jit(solution)/shard_map/ppermute | solution.py:27
  79.1 1.9 %collective-permute-start.9 = (f32[12,16,128]{2,1,0:T(8,128)S(1)}, f32[12,16,128]{2,1,0:T(8,128)S(1)}, u32[]{:S(2)}, u32[]{:S(2)}) collective-permute-start(f32[12,16,128]{2,1,0:T(8,128)S(1)} %get-tuple-element.66), channel_id=1, source_target_pairs={{0,16},{16,0},{32,48},{48,32},{64,80},{80,64},{96,112},{112,96},{1... | collective-permute-start | bytes 294920 | tf_op jit(solution)/shard_map/ppermute | solution.py:28
  81.0 0.7 collective-permute-start.10
  81.7 4.4 %collective-permute-start.11 = (f32[64,128]{1,0:T(8,128)S(1)}, f32[64,128]{1,0:T(8,128)S(1)}, u32[]{:S(2)}, u32[]{:S(2)}) collective-permute-start(f32[64,128]{1,0:T(8,128)S(1)} %get-tuple-element.68), channel_id=1, source_target_pairs={{0,1},{1,0},{2,3},{3,2},{4,5},{5,4},{6,7},{7,6},{8,9},{9,8},{10,11... | collective-permute-start | bytes 98312 | tf_op jit(solution)/shard_map/ppermute | solution.py:28
  86.1 0.0 collective-permute-done.10.far_block
  86.1 1.3 collective-permute-done.11.near_block
  87.4 0.0 collective-permute-done.8.far_face
  87.4 0.0 collective-permute-done.9.near_face
  87.4 0.0 copy-done.7
  87.4 1.0 shard_map.73
  88.4 3.1 %all_gather.3 = f32[2,1,640]{2,1,0:T(1,128)S(1)} all-gather(f32[1,1,640]{2,1,0:T(1,128)S(1)} %all_gather_reshape.3), channel_id=1, replica_groups={{0,16},{32,48},{64,80},{96,112},{128,144},{160,176},{192,208},{224,240}..., dimensions={0}, use_global_device_ids=true | all-gather | bytes 7680 | tf_op jit(solution)/shard_map/all_gather | solution.py:41
  91.6 23.3 %all_to_all.20 = f32[16,1,640]{2,1,0:T(1,128)S(1)} all-to-all(f32[16,1,640]{2,1,0:T(1,128)S(1)} %broadcast_in_dim.6), channel_id=1, replica_groups={{0,32,64,96,128,160,192,224,256,288,320,352,384,416,448,480},{16,48,80,..., dimensions={0} | all-to-all | bytes 81920 | tf_op jit(solution)/shard_map/all_to_all | solution.py:43
  115.0 14.7 %all_to_all.21 = f32[16,1,640]{2,1,0:T(1,128)S(1)} all-to-all(f32[16,1,640]{2,1,0:T(1,128)S(1)} %broadcast_in_dim.7), channel_id=1, replica_groups=mesh['sec'=32,'sub'=16] {'sub'}, dimensions={0} | all-to-all | bytes 81920 | tf_op jit(solution)/shard_map/all_to_all | solution.py:45
  129.8 0.8 add_bitcast_fusion
  (23 shorter events, 0.2 us)
Async XLA Ops:
  0.1 1.0 copy-start
  1.1 0.9 copy-start.5
  3.3 10.4 %copy-start.16 = (f32[1,12,32]{2,0,1:T(1,128)S(1)}, f32[1,12,32]{2,0,1:T(1,128)}, u32[]{:S(2)}) copy-start(f32[1,12,32]{2,0,1:T(1,128)} %param.9) | copy-start | bytes 4612
  3.3 24.2 %all-to-all-start = ((f32[16,64,128]{2,1,0:T(8,128)}), f32[16,64,128]{2,1,0:T(8,128)S(1)}, u32[]{:S(2)}, u32[]{:S(2)}) async-start(f32[16,64,128]{2,1,0:T(8,128)} %shard_map.64), calls=%async_computation | async-start | bytes 1048576 | tf_op jit(solution)/shard_map/all_to_all | solution.py:32
  17.0 4.4 %copy-start.14 = (bf16[128,768]{1,0:T(8,128)(2,1)}, bf16[128,768]{1,0:T(8,128)(2,1)S(1)}, u32[]{:S(2)}) copy-start(bf16[128,768]{1,0:T(8,128)(2,1)S(1)} %get-tuple-element.45.basis_rows) | copy-start | bytes 589828
  17.0 10.4 %copy-start.3 = (bf16[768,128]{1,0:T(8,128)(2,1)}, bf16[768,128]{1,0:T(8,128)(2,1)S(1)}, u32[]{:S(2)}) copy-start(bf16[768,128]{1,0:T(8,128)(2,1)S(1)} %get-tuple-element.48.basis_columns) | copy-start | bytes 589828
  17.0 30.7 %copy-start.6 = (f32[12,32,128]{2,1,0:T(8,128)}, f32[12,32,128]{2,1,0:T(8,128)S(1)}, u32[]{:S(2)}) copy-start(f32[12,32,128]{2,1,0:T(8,128)S(1)} %get-tuple-element.44.sides) | copy-start | bytes 589828
  17.0 6.3 %collective-permute-start = (f32[128,128]{1,0:T(8,128)S(1)}, f32[128,128]{1,0:T(8,128)S(1)}, u32[]{:S(2)}, u32[]{:S(2)}) collective-permute-start(f32[128,128]{1,0:T(8,128)S(1)} %get-tuple-element.51), channel_id=1, source_target_pairs={{0,1},{1,0},{2,3},{3,2},{4,5},{5,4},{6,7},{7,6},{8,9},{9,8},{10,11... | collective-permute-start | bytes 196616 | tf_op jit(solution)/shard_map/ppermute | solution.py:28
  20.3 3.0 %collective-permute-start.1 = (f32[128,128]{1,0:T(8,128)S(1)}, f32[128,128]{1,0:T(8,128)S(1)}, u32[]{:S(2)}, u32[]{:S(2)}) collective-permute-start(f32[128,128]{1,0:T(8,128)S(1)} %get-tuple-element.52), channel_id=1, source_target_pairs={{1,2},{3,4},{5,6},{7,8},{9,10},{11,12},{13,14},{2,1},{4,3},{6,5},{... | collective-permute-start | bytes 196616 | tf_op jit(solution)/shard_map/ppermute | solution.py:27
  23.3 1.5 %copy-start.8 = (f32[128,128]{1,0:T(8,128)}, f32[128,128]{1,0:T(8,128)S(1)}, u32[]{:S(2)}) copy-start(f32[128,128]{1,0:T(8,128)S(1)} %collective-permute-done.near.near_tile) | copy-start | bytes 196612
  23.3 1.5 %copy-start.10 = (f32[128,128]{1,0:T(8,128)}, f32[128,128]{1,0:T(8,128)S(1)}, u32[]{:S(2)}) copy-start(f32[128,128]{1,0:T(8,128)S(1)} %collective-permute-done.1.far.far_tile) | copy-start | bytes 196612
  27.5 20.2 %copy-start.1 = (f32[1,12,64,128]{3,2,1,0:T(8,128)S(1)}, f32[1,12,64,128]{3,2,1,0:T(8,128)}, u32[]{:S(2)}) copy-start(f32[1,12,64,128]{3,2,1,0:T(8,128)} %param.6) | copy-start | bytes 1179652
  27.5 20.2 %copy-start.2 = (f32[1,12,64,128]{3,2,1,0:T(8,128)S(1)}, f32[1,12,64,128]{3,2,1,0:T(8,128)}, u32[]{:S(2)}) copy-start(f32[1,12,64,128]{3,2,1,0:T(8,128)} %param.8) | copy-start | bytes 1179652
  27.5 20.2 %copy-start.15 = (bf16[128,768]{1,0:T(8,128)(2,1)S(1)}, bf16[128,768]{1,0:T(8,128)(2,1)}, u32[]{:S(2)}) copy-start(bf16[128,768]{1,0:T(8,128)(2,1)} %copy-done.14) | copy-start | bytes 589828
  28.6 19.0 %collective-permute-start.2 = (f32[12,16,128]{2,1,0:T(8,128)S(1)}, f32[12,16,128]{2,1,0:T(8,128)S(1)}, u32[]{:S(2)}, u32[]{:S(2)}) collective-permute-start(f32[12,16,128]{2,1,0:T(8,128)S(1)} %get-tuple-element.54), channel_id=1, source_target_pairs={{16,32},{48,64},{80,96},{112,128},{144,160},{176,192},{208,224},{2... | collective-permute-start | bytes 294920 | tf_op jit(solution)/shard_map/ppermute | solution.py:27
  39.1 8.6 %collective-permute-start.3 = (f32[12,16,128]{2,1,0:T(8,128)S(1)}, f32[12,16,128]{2,1,0:T(8,128)S(1)}, u32[]{:S(2)}, u32[]{:S(2)}) collective-permute-start(f32[12,16,128]{2,1,0:T(8,128)S(1)} %get-tuple-element.55), channel_id=1, source_target_pairs={{0,16},{16,0},{32,48},{48,32},{64,80},{80,64},{96,112},{112,96},{1... | collective-permute-start | bytes 294920 | tf_op jit(solution)/shard_map/ppermute | solution.py:28
  41.0 5.4 %collective-permute-start.4 = (f32[64,128]{1,0:T(8,128)S(1)}, f32[64,128]{1,0:T(8,128)S(1)}, u32[]{:S(2)}, u32[]{:S(2)}) collective-permute-start(f32[64,128]{1,0:T(8,128)S(1)} %get-tuple-element.56), channel_id=1, source_target_pairs={{1,2},{3,4},{5,6},{7,8},{9,10},{11,12},{13,14},{2,1},{4,3},{6,5},{... | collective-permute-start | bytes 98312 | tf_op jit(solution)/shard_map/ppermute | solution.py:27
  41.7 6.0 %collective-permute-start.5 = (f32[64,128]{1,0:T(8,128)S(1)}, f32[64,128]{1,0:T(8,128)S(1)}, u32[]{:S(2)}, u32[]{:S(2)}) collective-permute-start(f32[64,128]{1,0:T(8,128)S(1)} %get-tuple-element.57), channel_id=1, source_target_pairs={{0,1},{1,0},{2,3},{3,2},{4,5},{5,4},{6,7},{7,6},{8,9},{9,8},{10,11... | collective-permute-start | bytes 98312 | tf_op jit(solution)/shard_map/ppermute | solution.py:28
  50.2 20.9 %all-to-all-start.1 = ((f32[16,64,128]{2,1,0:T(8,128)}), f32[16,64,128]{2,1,0:T(8,128)S(1)}, u32[]{:S(2)}, u32[]{:S(2)}) async-start(f32[16,64,128]{2,1,0:T(8,128)} %get-tuple-element.60), calls=%async_computation.1 | async-start | bytes 1048576 | tf_op jit(solution)/shard_map/all_to_all | solution.py:32
  58.4 4.8 %collective-permute-start.6 = (f32[64,128]{1,0:T(8,128)S(1)}, f32[64,128]{1,0:T(8,128)S(1)}, u32[]{:S(2)}, u32[]{:S(2)}) collective-permute-start(f32[64,128]{1,0:T(8,128)S(1)} %get-tuple-element.62), channel_id=1, source_target_pairs={{0,1},{1,0},{2,3},{3,2},{4,5},{5,4},{6,7},{7,6},{8,9},{9,8},{10,11... | collective-permute-start | bytes 98312 | tf_op jit(solution)/shard_map/ppermute | solution.py:28
  61.7 1.5 %collective-permute-start.7 = (f32[64,128]{1,0:T(8,128)S(1)}, f32[64,128]{1,0:T(8,128)S(1)}, u32[]{:S(2)}, u32[]{:S(2)}) collective-permute-start(f32[64,128]{1,0:T(8,128)S(1)} %get-tuple-element.63), channel_id=1, source_target_pairs={{1,2},{3,4},{5,6},{7,8},{9,10},{11,12},{13,14},{2,1},{4,3},{6,5},{... | collective-permute-start | bytes 98312 | tf_op jit(solution)/shard_map/ppermute | solution.py:27
  62.4 0.8 copy-start.9
  62.4 0.9 copy-start.11
  71.1 0.9 copy-start.4
  72.0 15.4 %copy-start.7 = (f32[12,32,128]{2,1,0:T(8,128)S(1)}, f32[12,32,128]{2,1,0:T(8,128)}, u32[]{:S(2)}) copy-start(f32[12,32,128]{2,1,0:T(8,128)} %copy-done.6) | copy-start | bytes 589828
  72.0 15.4 %copy-start.12 = (f32[12,64,128]{2,1,0:T(8,128)S(1)}, f32[12,64,128]{2,1,0:T(8,128)}, u32[]{:S(2)}) copy-start(f32[12,64,128]{2,1,0:T(8,128)} %get-tuple-element.58.image) | copy-start | bytes 1179652
  72.0 15.4 %copy-start.13 = (f32[12,64,128]{2,1,0:T(8,128)S(1)}, f32[12,64,128]{2,1,0:T(8,128)}, u32[]{:S(2)}) copy-start(f32[12,64,128]{2,1,0:T(8,128)} %get-tuple-element.59.rest) | copy-start | bytes 1179652
  73.2 14.2 %collective-permute-start.8 = (f32[12,16,128]{2,1,0:T(8,128)S(1)}, f32[12,16,128]{2,1,0:T(8,128)S(1)}, u32[]{:S(2)}, u32[]{:S(2)}) collective-permute-start(f32[12,16,128]{2,1,0:T(8,128)S(1)} %get-tuple-element.65), channel_id=1, source_target_pairs={{16,32},{48,64},{80,96},{112,128},{144,160},{176,192},{208,224},{2... | collective-permute-start | bytes 294920 | tf_op jit(solution)/shard_map/ppermute | solution.py:27
  79.1 8.3 %collective-permute-start.9 = (f32[12,16,128]{2,1,0:T(8,128)S(1)}, f32[12,16,128]{2,1,0:T(8,128)S(1)}, u32[]{:S(2)}, u32[]{:S(2)}) collective-permute-start(f32[12,16,128]{2,1,0:T(8,128)S(1)} %get-tuple-element.66), channel_id=1, source_target_pairs={{0,16},{16,0},{32,48},{48,32},{64,80},{80,64},{96,112},{112,96},{1... | collective-permute-start | bytes 294920 | tf_op jit(solution)/shard_map/ppermute | solution.py:28
  81.0 5.0 %collective-permute-start.10 = (f32[64,128]{1,0:T(8,128)S(1)}, f32[64,128]{1,0:T(8,128)S(1)}, u32[]{:S(2)}, u32[]{:S(2)}) collective-permute-start(f32[64,128]{1,0:T(8,128)S(1)} %get-tuple-element.67), channel_id=1, source_target_pairs={{1,2},{3,4},{5,6},{7,8},{9,10},{11,12},{13,14},{2,1},{4,3},{6,5},{... | collective-permute-start | bytes 98312 | tf_op jit(solution)/shard_map/ppermute | solution.py:27
  81.7 5.7 %collective-permute-start.11 = (f32[64,128]{1,0:T(8,128)S(1)}, f32[64,128]{1,0:T(8,128)S(1)}, u32[]{:S(2)}, u32[]{:S(2)}) collective-permute-start(f32[64,128]{1,0:T(8,128)S(1)} %get-tuple-element.68), channel_id=1, source_target_pairs={{0,1},{1,0},{2,3},{3,2},{4,5},{5,4},{6,7},{7,6},{8,9},{9,8},{10,11... | collective-permute-start | bytes 98312 | tf_op jit(solution)/shard_map/ppermute | solution.py:28

commit v3 on v2

v3 whole, which is shorter than its diff:
```python
import jax
import jax.numpy as jnp
from jax import lax
from jax.experimental import pallas as pl
from jax.experimental.pallas import tpu as pltpu
from jax.sharding import PartitionSpec as P

SWEEPS = 4
SCALE = 2.0**-16

PRECISE = lax.Precision.HIGHEST


def dot(left, right):
    return jnp.dot(left, right, precision=PRECISE, preferred_element_type=jnp.float32)


def pairings(axis):
    count = lax.axis_size(axis)
    near = [(i, i ^ 1) for i in range(count)]
    low = [(i, i + 1) for i in range(1, count - 1, 2)]
    return near, low + [(target, source) for source, target in low]


def swap(to_near, to_far, axis):
    near, far = pairings(axis)
    from_far = lax.ppermute(to_far, axis, far)
    return lax.ppermute(to_near, axis, near), from_far


def gather_sub(spread):
    return lax.all_to_all(spread, "sub", 0, 0, tiled=True).reshape(-1, *spread.shape[2:])


def total(sums):
    sections, subs = lax.axis_size("sec"), lax.axis_size("sub")
    planes = sections // 4
    within = [
        [(4 * p + 2 * run + core) * subs + sub for run in range(2) for sub in range(subs)]
        for p in range(planes)
        for core in range(2)
    ]
    across = [[4 * p + 2 * run + core for p in range(planes) for core in range(2)] for run in range(2)]
    flat = sums.reshape(1, -1)
    for axes, groups in ((("sec", "sub"), within), ("sec", across)):
        spread = jnp.broadcast_to(flat[None], (len(groups[0]), *flat.shape))
        flat = jnp.sum(lax.all_to_all(spread, axes, 0, 0, axis_index_groups=groups, tiled=True), axis=0)
    return flat.reshape(sums.shape)


def split(value):
    high = value.astype(jnp.bfloat16)
    return high, (value - high.astype(jnp.float32)).astype(jnp.bfloat16)


def rows_split(value):
    return jnp.concatenate(split(value), axis=0)


def columns_split(value):
    return jnp.concatenate(split(value), axis=1)


def product(rows, columns):
    all_four = jnp.dot(rows, columns, preferred_element_type=jnp.float32)
    half, width = all_four.shape[0] // 2, all_four.shape[1] // 2
    top = all_four[:half, :width] + (all_four[:half, width:] + all_four[half:, :width])
    return top + all_four[half:, width:]


def pair_split(value):
    high, low = split(value)
    both = jnp.concatenate([high.astype(jnp.float32), low.astype(jnp.float32)], axis=1)
    return both.astype(jnp.bfloat16)


def pair_product(pairs, columns):
    both = jnp.dot(pairs, jnp.concatenate([columns, columns], axis=0), preferred_element_type=jnp.float32)
    width = both.shape[1] // 2
    return both[:, :width] + both[:, width:]


def tile_product(beside, centre, before, after, own):
    return product(beside, jnp.concatenate([before, after], axis=0)) + pair_product(centre, own)


def block_sweep(pair, coupling, field):
    nodes = pair.shape[0]
    inverse = rows_split(pair[:, nodes:])
    row = lax.broadcasted_iota(jnp.int32, (nodes, nodes), 0)
    unit = (row == lax.broadcasted_iota(jnp.int32, (nodes, nodes), 1)).astype(jnp.float32)
    beside = -product(inverse, columns_split(coupling))
    own = unit - product(inverse, columns_split(pair))[:, :nodes]
    return product(inverse, columns_split(field)), beside, own


def start_all(pairs, sems):
    loads = [pltpu.make_async_copy(source, target, sems.at[i]) for i, (source, target) in enumerate(pairs)]
    for load in loads:
        load.start()
    return loads


def edge_kernel(odd, coupling_in, pair_in, residual_in, near, far, coupling, pair, residual, sems):
    blocks, nodes = pair_in.shape[:2]
    loads = start_all(
        [
            (source.at[b], target.at[i])
            for source, target in ((pair_in, pair), (coupling_in, coupling), (residual_in, residual))
            for i, b in enumerate((0, blocks - 1))
        ],
        sems,
    )
    for load in loads:
        load.wait()
    even = odd[1] == 0
    start, beside, own = block_sweep(pair[0], coupling[0], residual[0])
    last, beyond, own_last = block_sweep(pair[1], coupling[1], residual[1])
    to_previous = jnp.concatenate([beside[:, :nodes], own], axis=1)
    to_next = jnp.concatenate([beyond[:, nodes:], own_last], axis=1)
    near[:nodes] = jnp.where(even, last, start)
    far[:nodes] = jnp.where(even, start, last)
    near[nodes:] = jnp.where(even, to_next, to_previous)
    far[nodes:] = jnp.where(even, to_previous, to_next)


def prepare_kernel(side, coupling_in, pair_in, residual_in, basis_in, inverse_in, sweep, sweep_own, tiles_out, tiles_own_out, start, sides_out, basis_rows_out, basis_columns, coarse_rows, coupling, pair, residual, basis, inverse_rows, tiles, tiles_own, sides, basis_rows, sems, stores):
    blocks, nodes, columns = residual.shape
    loads = start_all(
        [
            (pair_in, pair),
            (coupling_in, coupling),
            (residual_in, residual),
            (inverse_in, inverse_rows),
            (basis_in, basis),
        ],
        sems,
    )
    for load in loads[:3]:
        load.wait()
    for b in range(blocks):
        start[b], beside, own = block_sweep(pair[b], coupling[b], residual[b])
        sweep[b] = rows_split(beside)
        sweep_own[b] = pair_split(own)
        tiles[b] = rows_split(coupling[b])
        tiles_own[b] = pair_split(pair[b][:, :nodes])
        sides[b] = jnp.broadcast_to(side[b : b + 1].T, sides.shape[1:])
    for load in loads[3:]:
        load.wait()
    parts = rows_split(basis[...])
    basis_rows[...] = parts
    copies = start_all(
        [(tiles, tiles_out), (tiles_own, tiles_own_out), (sides, sides_out), (basis_rows, basis_rows_out)], stores
    )
    coarse_rows[...] = rows_split(inverse_rows[...])
    basis_columns[...] = parts.astype(jnp.float32).T.astype(jnp.bfloat16)
    for copy in copies:
        copy.wait()


def first_sweep_kernel(tiles, tiles_own, start, out):
    blocks, nodes, _ = start.shape
    parts = [columns_split(start[b]) for b in range(blocks)]
    nothing = jnp.zeros_like(parts[0])
    for b in range(blocks):
        before = parts[b - 1] if b else nothing
        after = parts[b + 1] if b + 1 < blocks else nothing
        out[b] = start[b] + tile_product(tiles[b], tiles_own[b], before, after, parts[b])


def sweep_kernel(odd, tiles, tiles_own, start, partial, far, near, far_tile, near_tile, out, one, two):
    blocks, nodes, _ = start.shape
    even = odd[1] == 0
    low = jnp.where(even, far[...], near[...])
    high = jnp.where(even, near[...], far[...])
    low_tile = rows_split(jnp.where(even, far_tile[...], near_tile[...]))
    high_tile = rows_split(jnp.where(even, near_tile[...], far_tile[...]))
    low_parts, high_parts = columns_split(low), columns_split(high)
    first, last = columns_split(start[0]), columns_split(start[blocks - 1])
    one[0] = columns_split(low + product(low_tile, jnp.concatenate([first, low_parts], axis=0)))
    one[blocks + 1] = columns_split(high + product(high_tile, jnp.concatenate([last, high_parts], axis=0)))
    one[1] = columns_split(partial[0] + product(tiles[0][:, :nodes], low_parts))
    one[blocks] = columns_split(partial[blocks - 1] + product(tiles[blocks - 1][:, nodes : 2 * nodes], high_parts))
    for b in range(1, blocks - 1):
        one[b + 1] = columns_split(partial[b])
    source, target = one, two
    for sweep in range(1, SWEEPS - 1):
        final = sweep == SWEEPS - 2
        for b in range(blocks):
            new = start[b] + tile_product(tiles[b], tiles_own[b], source[b], source[b + 2], source[b + 1])
            if final:
                out[b] = new
            else:
                target[b + 1] = columns_split(new)
        if not final:
            target[0] = columns_split(low + product(low_tile, jnp.concatenate([source[1], source[0]], axis=0)))
            target[blocks + 1] = columns_split(
                high + product(high_tile, jnp.concatenate([source[blocks], source[blocks + 1]], axis=0))
            )
        source, target = target, source


def keeping_sweep_kernel(odd, tiles, tiles_own, start, partial, far, near, out, far_kept, near_kept, one, two, sems):
    nodes = start.shape[1]
    far_tile, near_tile = far.at[nodes : 2 * nodes], near.at[nodes : 2 * nodes]
    copies = start_all([(far_tile, far_kept), (near_tile, near_kept)], sems)
    sweep_kernel(
        odd, tiles, tiles_own, start, partial, far.at[:nodes], near.at[:nodes], far_tile, near_tile, out, one, two
    )
    for copy in copies:
        copy.wait()


def update_kernel(odd, coarse_rows, gathered, basis_columns, local, update, near_face, far_face, near_block, far_block):
    blocks, nodes, _ = local.shape
    faces = near_face.shape[1]
    correction = columns_split(product(coarse_rows[...], columns_split(gathered[...])))
    for b in range(blocks):
        new = local[b] + pair_product(basis_columns[b * nodes : (b + 1) * nodes], correction)
        update[b] = new
        south, north = new[:faces], new[nodes - faces :]
        even = odd[0] == 0
        near_face[b] = jnp.where(even, north, south)
        far_face[b] = jnp.where(even, south, north)
    even = odd[1] == 0
    near_block[...] = jnp.where(even, update[blocks - 1], update[0])
    far_block[...] = jnp.where(even, update[0], update[blocks - 1])


def image_blocks(odd, tiles, tiles_own, sides, update, near_face, far_face, near_block, far_block):
    blocks, nodes, _ = update.shape
    faces = near_face.shape[1]
    even = odd[1] == 0
    low = jnp.where(even, far_block[...], near_block[...])
    high = jnp.where(even, near_block[...], far_block[...])
    parts = [columns_split(value) for value in (low, *(update[b] for b in range(blocks)), high)]
    even = odd[0] == 0
    for b in range(blocks):
        linear = tile_product(tiles[b], tiles_own[b], parts[b], parts[b + 2], parts[b + 1])
        below = jnp.where(even, far_face[b], near_face[b])
        above = jnp.where(even, near_face[b], far_face[b])
        yield b, jnp.concatenate(
            [
                linear[:faces] + sides[b, :faces] * below,
                linear[faces : nodes - faces],
                linear[nodes - faces :] + sides[b, faces:] * above,
            ],
            axis=0,
        )


def send_out(projected, spread, sems):
    return start_all([(projected, spread.at[i]) for i in range(spread.shape[0])], sems)


def image_kernel(odd, tiles, tiles_own, sides, basis_rows, pair, residual, update, near_face, near_block, far_block, far_face, image_out, rest_out, spread, start, near, far, image, rest, flat, projected, edges, sems, stores):
    blocks, nodes, _ = update.shape
    for b, new in image_blocks(odd, tiles, tiles_own, sides, update, near_face, far_face, near_block, far_block):
        image[b] = new
        left = residual[b] - new
        rest[b] = left
        flat[b * nodes : (b + 1) * nodes] = columns_split(left)
    projected[...] = product(basis_rows[...], flat[...])
    copies = send_out(projected, spread, sems)
    for b in (0, blocks - 1, *range(1, blocks - 1)):
        start[b] = product(rows_split(pair[b][:, nodes:]), flat[b * nodes : (b + 1) * nodes])
        if b == blocks - 1:
            even = odd[1] == 0
            edges[0] = jnp.where(even, start[blocks - 1], start[0])
            edges[1] = jnp.where(even, start[0], start[blocks - 1])
            copies += start_all(
                [(edges.at[0], near), (edges.at[1], far), (image, image_out), (rest, rest_out)], stores
            )
    for copy in copies:
        copy.wait()


def project_kernel(basis_in, field_in, spread, basis, field, projected, sems, arrived):
    blocks, nodes, columns = field.shape
    for load in start_all([(basis_in, basis), (field_in, field)], arrived):
        load.wait()
    projected[...] = dot(basis[...], field[...].reshape(blocks * nodes, columns))
    for copy in send_out(projected, spread, sems):
        copy.wait()


def sums_kernel(odd, tiles, tiles_own, sides, image, rest, update, near_face, near_block, far_block, far_face, sums):
    nodes, columns = update.shape[1:]
    parts = [jnp.zeros((8, columns), jnp.float32) for _ in range(5)]

    def inner(left, right):
        return jnp.sum((left * right).reshape(nodes // 8, 8, columns), axis=0)

    for b, new in image_blocks(odd, tiles, tiles_own, sides, update, near_face, far_face, near_block, far_block):
        change = new * SCALE
        left, right = image[b], rest[b]
        for i, (x, y) in enumerate(((left, right), (left, left), (change, right), (change, left), (change, change))):
            parts[i] = parts[i] + inner(x, y)
    for i in range(5):
        sums[i : i + 1] = jnp.sum(parts[i], axis=0, keepdims=True)


def call(kernel, outs, scratch, *operands, slow=0):
    specs, given = [], []
    for at, operand in enumerate(operands):
        space = pltpu.HBM if at >= len(operands) - slow else pltpu.VMEM
        if operand.dtype == jnp.int32:
            space = pltpu.SMEM
        elif operand.size > 2 * operand.shape[-1] ** 2 or space is pltpu.HBM:
            operand = pltpu.with_memory_space_constraint(operand, space)
        specs.append(pl.BlockSpec(memory_space=space))
        given.append(operand)
    return pl.pallas_call(
        kernel,
        out_shape=[(space or jax.ShapeDtypeStruct)(shape, kind) for shape, kind, space in outs],
        in_specs=specs,
        out_specs=[pl.BlockSpec(memory_space=space or pltpu.VMEM) for _, _, space in outs],
        scratch_shapes=scratch,
        compiler_params=pltpu.CompilerParams(vmem_limit_bytes=12 << 20),
        cost_estimate=pl.CostEstimate(flops=1000, transcendentals=0, bytes_accessed=1000),
    )(*given)


def shards(forcing, coupling, diag_pair, side, basis, coarse_inverse):
    residual = forcing[0]
    basis_all = basis[0]
    blocks, nodes, columns = residual.shape
    faces = side.shape[2] // 2
    coarse, own_coarse = coarse_inverse.shape[2], coarse_inverse.shape[1]
    odd = jnp.stack([lax.axis_index("sec") % 2, lax.axis_index("sub") % 2]).astype(jnp.int32)
    wide, thin, fast = jnp.float32, jnp.bfloat16, pltpu.VMEM
    subs = lax.axis_size("sub")
    block = ((nodes, columns), wide, None)
    edge = ((nodes, columns), wide, pltpu.HBM)
    small = ((2 * nodes, columns), wide, None)
    field = ((blocks, nodes, columns), wide, fast)
    kept = ((blocks, nodes, columns), wide, pltpu.HBM)
    face = ((blocks, faces, columns), wide, fast)
    tile = ((blocks, 2 * nodes, 2 * nodes), thin)
    tile_own = ((blocks, nodes, 2 * nodes), thin)
    padded = pltpu.VMEM((blocks + 2, nodes, 2 * columns), thin)
    spread_out = ((subs, own_coarse, columns), wide, pltpu.HBM)
    spreading = [pltpu.VMEM((own_coarse, columns), wide), pltpu.SemaphoreType.DMA((subs,))]

    (spread,) = call(
        project_kernel,
        [spread_out],
        [
            pltpu.VMEM(basis_all.shape, wide),
            pltpu.VMEM((blocks, nodes, columns), wide),
            *spreading,
            pltpu.SemaphoreType.DMA((2,)),
        ],
        basis_all, residual,
        slow=2,
    )
    spread, odd, residual, coupling, diag_pair, side, basis_all = lax.optimization_barrier(
        (spread, odd, residual, coupling, diag_pair, side, basis_all)
    )
    pair = diag_pair[0]
    near, far = call(
        edge_kernel,
        [small, small],
        [pltpu.VMEM((2, nodes, columns), wide)] * 3 + [pltpu.SemaphoreType.DMA((6,))],
        odd, coupling[0], pair, residual,
        slow=3,
    )
    halo = swap(near, far, "sub")
    sweep, sweep_own, tiles, tiles_own, start, sides, basis_rows, basis_columns, coarse_rows = call(
        prepare_kernel,
        [
            (*tile, fast),
            (*tile_own, fast),
            (*tile, pltpu.HBM),
            (*tile_own, pltpu.HBM),
            field,
            ((blocks, 2 * faces, columns), wide, pltpu.HBM),
            ((2 * own_coarse, blocks * nodes), thin, pltpu.HBM),
            ((blocks * nodes, 2 * own_coarse), thin, fast),
            ((2 * own_coarse, coarse), thin, fast),
        ],
        [
            pltpu.VMEM((blocks, nodes, columns), wide),
            pltpu.VMEM((blocks, nodes, columns), wide),
            pltpu.VMEM((blocks, nodes, columns), wide),
            pltpu.VMEM(basis_all.shape, wide),
            pltpu.VMEM((own_coarse, coarse), wide),
            pltpu.VMEM(*tile),
            pltpu.VMEM(*tile_own),
            pltpu.VMEM((blocks, 2 * faces, columns), wide),
            pltpu.VMEM((2 * own_coarse, blocks * nodes), thin),
            pltpu.SemaphoreType.DMA((5,)),
            pltpu.SemaphoreType.DMA((4,)),
        ],
        side[0], coupling[0], pair, residual, basis_all, coarse_inverse[0],
        slow=5,
    )

    def precondition(start, near, far, kept, spread):
        gathered = gather_sub(spread)
        (partial,) = call(first_sweep_kernel, [field], [], sweep, sweep_own, start)
        given = (odd, sweep, sweep_own, start, partial, far, near)
        if kept:
            (local,) = call(sweep_kernel, [field], [padded] * 2, *given, *kept)
        else:
            local, *kept = call(
                keeping_sweep_kernel,
                [field, edge, edge],
                [padded, padded, pltpu.SemaphoreType.DMA((2,))],
                *given,
            )
        update, near_face, far_face, near_block, far_block = call(
            update_kernel, [field, face, face, block, block], [], odd, coarse_rows, gathered, basis_columns, local
        )
        faces_in = swap(near_face, far_face, "sec")
        blocks_in = swap(near_block, far_block, "sub")
        return kept, update, faces_in[0], blocks_in[0], blocks_in[1], faces_in[1]

    kept_tiles, first, *given = precondition(start, *halo, None, spread)
    image, rest, spread, start, near, far = call(
        image_kernel,
        [kept, kept, spread_out, field, edge, edge],
        [
            pltpu.VMEM((blocks, nodes, columns), wide),
            pltpu.VMEM((blocks, nodes, columns), wide),
            pltpu.VMEM((blocks * nodes, 2 * columns), thin),
            pltpu.VMEM((own_coarse, columns), wide),
            pltpu.VMEM((2, nodes, columns), wide),
            pltpu.SemaphoreType.DMA((subs,)),
            pltpu.SemaphoreType.DMA((4,)),
        ],
        odd, tiles, tiles_own, sides, basis_rows, pair, residual, first, *given,
    )
    _, second, *given = precondition(start, *swap(near, far, "sub"), kept_tiles, spread)
    (sums,) = call(sums_kernel, [((5, columns), wide, fast)], [], odd, tiles, tiles_own, sides, image, rest, second, *given)
    sums = total(sums)
    short = -sums[0] / sums[1]
    step = 1.0 - short
    upper = step * (sums[2] + short * sums[3])
    scaled = step / SCALE
    lower = short * short * sums[1] + 2.0 * short * scaled * sums[3] + scaled * scaled * sums[4]
    step_next = upper / SCALE / lower
    result = (step + step_next * short) * first + (step_next * step) * second
    return result[None]


def solution(mesh):
    placed = (
        P("sec", "sub", None, None),
        P("sec", "sub", None, None),
        P("sec", "sub", None, None),
        P("sec", "sub", None),
        P("sec", "sub", None),
        P("sec", "sub", None),
    )
    return jax.shard_map(
        shards, mesh=mesh, in_specs=placed, out_specs=P("sec", "sub", None, None), check_vma=False
    )
```

time: 132 us -> 127 us (0.962)
  waiting for transfers between devices: 13.9 us -> 6.86 us
  Pallas kernels: 14 us -> 18 us
  starting transfers between devices: 57.2 us -> 60.6 us
  local copies, waits for them, and re-layouts: 3 us -> 0.14 us
  blocking collectives: 41.2 us -> 38.9 us
    all_to_all x2, waiting for transfers between devices: 8.94 us -> 1.75 us  [gather_sub(): lax.all_to_all(spread, 'sub', 0, 0, tiled=True)]
    pallas_call x10 -> x11, Pallas kernels: 14 us -> 18 us  [call(): pl.pallas_call(kernel, out_shape=[(space or jax.ShapeDtypeStruct)(shape,...]
    all_gather x1 -> x0, blocking collectives: 3.13 us -> none  [total(): flat = jnp.sum(lax.all_gather(flat, 'sec', axis_index_groups=pairs), axis=0)]
    unnamed x35 -> x27, local copies, waits for them, and re-layouts: 2.94 us -> 0.06 us
    all_to_all x2, starting transfers between devices: 18.7 us -> 21 us  [gather_sub(): lax.all_to_all(spread, 'sub', 0, 0, tiled=True)]
    ppermute x6, starting transfers between devices: 19.4 us -> 21.4 us  [swap(): return (lax.ppermute(to_near, axis, near), from_far)]
  transfers between devices with their start and end apart: 14 -> 14, of which waited for: 6 -> 4; matrix products, arithmetic and copies ran while one was open for 0% -> 0% of each run, Pallas kernels for 5% -> 8%
where the time goes in v3:
time: 127 us; the launch traced here: 126 us
  starting transfers between devices  60.6 us (48%)
  blocking collectives  38.9 us (31%)
  Pallas kernels  18 us (14%)
  waiting for transfers between devices  6.86 us (5%)
    all_to_all x2, blocking collectives, total(): lax.all_to_all(spread, axes, 0, 0, axis_index_groups=groups, tiled=True)  38.9 us
    ppermute x6, starting transfers between devices, swap(): return (lax.ppermute(to_near, axis, near), from_far)  21.4 us
    all_to_all x2, starting transfers between devices, gather_sub(): lax.all_to_all(spread, 'sub', 0, 0, tiled=True)  21 us
    ppermute x6, starting transfers between devices, swap(): from_far = lax.ppermute(to_far, axis, far)  18.2 us
    pallas_call x11, Pallas kernels, call(): pl.pallas_call(kernel, out_shape=[(space or jax.ShapeDtypeStruct)(shape,...  18 us
    ppermute x6, waiting for transfers between devices, swap(): return (lax.ppermute(to_near, axis, near), from_far)  5.09 us
  transfers between devices with their start and end apart: 14, of which 4 were waited for; matrix products, arithmetic and copies ran while one was open for 0% of the time, Pallas kernels for 8%

profile of v3, /device:TPU:1, one launch (start us, length us, event | category | flops | bytes accessed | tf_op | source)
XLA Modules:
  0.0 126.0 jit_solution(13294707156708339348)
XLA Ops:
  0.0 0.1 pad_add_fusion.odd
  0.1 2.4 %shard_map.64 = f32[16,64,128]{2,1,0:T(8,128)} custom-call(f32[64,768]{1,0:T(8,128)} %bitcast.64, f32[12,64,128]{2,1,0:T(8,128)} %bitcast.51), custom_call_target="tpu_custom_call" | custom-call | flops 1000 | bytes 1000 | tf_op jit(solution)/shard_map/pallas_call | solution.py:313
  2.5 10.4 %all-to-all-start = ((f32[16,64,128]{2,1,0:T(8,128)}), f32[16,64,128]{2,1,0:T(8,128)S(1)}, u32[]{:S(2)}, u32[]{:S(2)}) async-start(f32[16,64,128]{2,1,0:T(8,128)} %shard_map.64), calls=%async_computation | async-start | bytes 1048576 | tf_op jit(solution)/shard_map/all_to_all | solution.py:32
  12.9 0.0 copy-start.10
  12.9 1.8 %shard_map.67 = (f32[128,128]{1,0:T(8,128)S(1)}, f32[128,128]{1,0:T(8,128)S(1)}) custom-call(s32[2]{0:T(128)S(1)} %pad_add_fusion.odd, f32[12,64,128]{2,1,0:T(8,128)} %bitcast.62, f32[12,64,128]{2,1,0:T(8,128)} %bitcast.55, f32[12,64,128]{2,1,0:T(8,128)} %bitcast.52), custom_call_target="tpu_custom_call" | custom-call | flops 1000 | bytes 1000 | tf_op jit(solution)/shard_map/pallas_call | solution.py:313
  14.7 0.7 collective-permute-start
  15.4 5.7 %collective-permute-start.1 = (f32[128,128]{1,0:T(8,128)S(1)}, f32[128,128]{1,0:T(8,128)S(1)}, u32[]{:S(2)}, u32[]{:S(2)}) collective-permute-start(f32[128,128]{1,0:T(8,128)S(1)} %get-tuple-element.59), channel_id=1, source_target_pairs={{0,1},{1,0},{2,3},{3,2},{4,5},{5,4},{6,7},{7,6},{8,9},{9,8},{10,11... | collective-permute-start | bytes 196616 | tf_op jit(solution)/shard_map/ppermute | solution.py:28
  21.1 0.0 copy-done.10
  21.1 3.3 %shard_map.65 = (bf16[12,128,128]{2,1,0:T(8,128)(2,1)S(1)}, bf16[12,64,128]{2,1,0:T(8,128)(2,1)S(1)}, bf16[12,128,128]{2,1,0:T(8,128)(2,1)}, bf16[12,64,128]{2,1...) custom-call(f32[12,32]{1,0:T(8,128)S(1)} %bitcast.60, ...), custom_call_target="tpu_custom_call" | custom-call | flops 1000 | bytes 1000 | tf_op jit(solution)/shard_map/pallas_call | solution.py:313
  24.4 0.5 shard_map.66.partial
  24.9 0.0 collective-permute-done.far
  24.9 0.0 collective-permute-done.1.near
  24.9 0.0 copy-start.4
  24.9 0.0 copy-start.7
  24.9 2.2 %shard_map.68 = (f32[12,64,128]{2,1,0:T(8,128)S(1)}, f32[64,128]{1,0:T(8,128)}, f32[64,128]{1,0:T(8,128)}) custom-call(s32[2]{0:T(128)S(1)} %pad_add_fusion.odd, bf16[12,128,128]{2,1,0:T(8,128)(2,1)S(1)} %get-tuple-element.55.tiles, bf16[12,64,128]{2,1,0:T(8,128)(2,1)S(1)} %get-tuple-element.56.tiles_own, f32[12,64,128]{2,1,0:T(8,128)S(1)} %get-tuple-element.57.start, ...), custom_call_target="tpu_custom_call" | custom-call | flops 1000 | bytes 1000 | tf_op jit(solution)/shard_map/pallas_call | solution.py:313
  27.1 0.0 all-to-all-done
  27.1 0.0 copy-start
  27.1 0.0 copy-start.1
  27.1 0.0 copy-start.2
  27.1 0.0 copy-start.3
  27.1 1.2 shard_map.69
  28.3 4.1 %collective-permute-start.2 = (f32[12,16,128]{2,1,0:T(8,128)S(1)}, f32[12,16,128]{2,1,0:T(8,128)S(1)}, u32[]{:S(2)}, u32[]{:S(2)}) collective-permute-start(f32[12,16,128]{2,1,0:T(8,128)S(1)} %get-tuple-element.62), channel_id=1, source_target_pairs={{0,16},{16,0},{32,48},{48,32},{64,80},{80,64},{96,112},{112,96},{1... | collective-permute-start | bytes 294920 | tf_op jit(solution)/shard_map/ppermute | solution.py:28
  32.4 7.8 %collective-permute-start.5 = (f32[12,16,128]{2,1,0:T(8,128)S(1)}, f32[12,16,128]{2,1,0:T(8,128)S(1)}, u32[]{:S(2)}, u32[]{:S(2)}) collective-permute-start(f32[12,16,128]{2,1,0:T(8,128)S(1)} %get-tuple-element.65), channel_id=1, source_target_pairs={{16,32},{48,64},{80,96},{112,128},{144,160},{176,192},{208,224},{2... | collective-permute-start | bytes 294920 | tf_op jit(solution)/shard_map/ppermute | solution.py:27
  40.2 2.0 %collective-permute-start.3 = (f32[64,128]{1,0:T(8,128)S(1)}, f32[64,128]{1,0:T(8,128)S(1)}, u32[]{:S(2)}, u32[]{:S(2)}) collective-permute-start(f32[64,128]{1,0:T(8,128)S(1)} %get-tuple-element.63), channel_id=1, source_target_pairs={{0,1},{1,0},{2,3},{3,2},{4,5},{5,4},{6,7},{7,6},{8,9},{9,8},{10,11... | collective-permute-start | bytes 98312 | tf_op jit(solution)/shard_map/ppermute | solution.py:28
  42.2 0.7 collective-permute-start.4
  42.9 2.0 %collective-permute-done.3.near_block = f32[64,128]{1,0:T(8,128)S(1)} collective-permute-done((f32[64,128]{1,0:T(8,128)S(1)}, f32[64,128]{1,0:T(8,128)S(1)}, u32[]{:S(2)}, u32[]{:S(2)}) %collective-permute-start.3) | collective-permute-done | bytes 32800 | tf_op jit(solution)/shard_map/ppermute | solution.py:28
  44.9 0.0 collective-permute-done.4.far_block
  44.9 0.0 collective-permute-done.2.near_face
  44.9 0.0 collective-permute-done.5.far_face
  44.9 0.0 copy-done.4
  44.9 0.0 copy-done.7
  44.9 0.0 copy-done
  44.9 0.0 copy-done.1
  44.9 0.0 copy-done.2
  44.9 0.0 copy-done.3
  45.0 2.5 %shard_map.70 = (f32[12,64,128]{2,1,0:T(8,128)}, f32[12,64,128]{2,1,0:T(8,128)}, f32[16,64,128]{2,1,0:T(8,128)}, f32[12,64,128]{2,1,0:T(8,128)S(1)}, f32[64,128]{1,0:T(8,128)}, /*index=5*/f32[64,128]{1,0:T(8,128)}) custom-call(s32[2]{0:T(128)S(1)} %pad_add_fusion.odd, bf16[12,128,128]{2,1,0:T(8,128)(2,1)S(1)} %copy-done.2, ...), custom_call_target="tpu_custom_call" | custom-call | flops 1000 | bytes 1000 | tf_op jit(solution)/shard_map/pallas_call | solution.py:313
  47.4 0.0 copy-start.12
  47.4 0.0 copy-start.11
  47.5 10.6 %all-to-all-start.1 = ((f32[16,64,128]{2,1,0:T(8,128)}), f32[16,64,128]{2,1,0:T(8,128)S(1)}, u32[]{:S(2)}, u32[]{:S(2)}) async-start(f32[16,64,128]{2,1,0:T(8,128)} %get-tuple-element.68), calls=%async_computation.1 | async-start | bytes 1048576 | tf_op jit(solution)/shard_map/all_to_all | solution.py:32
  58.0 0.0 copy-done.12
  58.1 0.7 collective-permute-start.6
  58.7 5.7 %collective-permute-start.7 = (f32[64,128]{1,0:T(8,128)S(1)}, f32[64,128]{1,0:T(8,128)S(1)}, u32[]{:S(2)}, u32[]{:S(2)}) collective-permute-start(f32[64,128]{1,0:T(8,128)S(1)} %copy-done.11), channel_id=1, source_target_pairs={{0,1},{1,0},{2,3},{3,2},{4,5},{5,4},{6,7},{7,6},{8,9},{9,8},{10,11... | collective-permute-start | bytes 98312 | tf_op jit(solution)/shard_map/ppermute | solution.py:28
  64.4 0.0 copy-start.8
  64.5 0.0 copy-start.9
  64.5 0.5 shard_map.71.partial
  64.9 0.0 collective-permute-done.6.far
  64.9 1.1 collective-permute-done.7.near
  66.1 0.0 copy-done.9
  66.1 1.6 %shard_map.72.local = f32[12,64,128]{2,1,0:T(8,128)S(1)} custom-call(s32[2]{0:T(128)S(1)} %pad_add_fusion.odd, bf16[12,128,128]{2,1,0:T(8,128)(2,1)S(1)} %get-tuple-element.55.tiles, bf16[12,64,128]{2,1,0:T(8,128)(2,1)S(1)} %get-tuple-element.56.tiles_own, f32[12,64,128]{2,1,0:T(8,128)S(1)} %get-tuple-element.69.start, ...), custom_call_target="tpu_custom_call" | custom-call | flops 1000 | bytes 1000 | tf_op jit(solution)/shard_map/pallas_call | solution.py:313
  67.7 1.7 %all-to-all-done.1 = f32[16,64,128]{2,1,0:T(8,128)S(1)} async-done(((f32[16,64,128]{2,1,0:T(8,128)}), f32[16,64,128]{2,1,0:T(8,128)S(1)}, u32[]{:S(2)}, u32[]{:S(2)}) %all-to-all-start.1) | async-done | bytes 524320 | tf_op jit(solution)/shard_map/all_to_all | solution.py:32
  69.5 1.1 shard_map.73
  70.6 1.9 %collective-permute-start.8 = (f32[12,16,128]{2,1,0:T(8,128)S(1)}, f32[12,16,128]{2,1,0:T(8,128)S(1)}, u32[]{:S(2)}, u32[]{:S(2)}) collective-permute-start(f32[12,16,128]{2,1,0:T(8,128)S(1)} %get-tuple-element.75), channel_id=1, source_target_pairs={{0,16},{16,0},{32,48},{48,32},{64,80},{80,64},{96,112},{112,96},{1... | collective-permute-start | bytes 294920 | tf_op jit(solution)/shard_map/ppermute | solution.py:28
  72.6 7.7 %collective-permute-start.11 = (f32[12,16,128]{2,1,0:T(8,128)S(1)}, f32[12,16,128]{2,1,0:T(8,128)S(1)}, u32[]{:S(2)}, u32[]{:S(2)}) collective-permute-start(f32[12,16,128]{2,1,0:T(8,128)S(1)} %get-tuple-element.78), channel_id=1, source_target_pairs={{16,32},{48,64},{80,96},{112,128},{144,160},{176,192},{208,224},{2... | collective-permute-start | bytes 294920 | tf_op jit(solution)/shard_map/ppermute | solution.py:27
  80.3 2.0 %collective-permute-start.9 = (f32[64,128]{1,0:T(8,128)S(1)}, f32[64,128]{1,0:T(8,128)S(1)}, u32[]{:S(2)}, u32[]{:S(2)}) collective-permute-start(f32[64,128]{1,0:T(8,128)S(1)} %get-tuple-element.76), channel_id=1, source_target_pairs={{0,1},{1,0},{2,3},{3,2},{4,5},{5,4},{6,7},{7,6},{8,9},{9,8},{10,11... | collective-permute-start | bytes 98312 | tf_op jit(solution)/shard_map/ppermute | solution.py:28
  82.3 0.7 collective-permute-start.10
  83.0 2.0 %collective-permute-done.9.near_block = f32[64,128]{1,0:T(8,128)S(1)} collective-permute-done((f32[64,128]{1,0:T(8,128)S(1)}, f32[64,128]{1,0:T(8,128)S(1)}, u32[]{:S(2)}, u32[]{:S(2)}) %collective-permute-start.9) | collective-permute-done | bytes 32800 | tf_op jit(solution)/shard_map/ppermute | solution.py:28
  85.0 0.0 collective-permute-done.10.far_block
  85.0 0.0 collective-permute-done.8.near_face
  85.0 0.0 collective-permute-done.11.far_face
  85.0 1.0 shard_map.74
  86.1 22.4 %all_to_all.20 = f32[32,1,640]{2,1,0:T(1,128)S(1)} all-to-all(f32[32,1,640]{2,1,0:T(1,128)S(1)} %broadcast_in_dim.9), channel_id=1, replica_groups={{0,1,2,3,4,5,6,7,8,9,10,11,12,13,14,15,32,33,34,35,36,37,38,39,40,41,42..., dimensions={0} | all-to-all | bytes 163840 | tf_op jit(solution)/shard_map/all_to_all | solution.py:47
  108.5 0.1 reduce_sum.20
  108.6 16.5 %all_to_all.21 = f32[16,1,640]{2,1,0:T(1,128)S(1)} all-to-all(f32[16,1,640]{2,1,0:T(1,128)S(1)} %broadcast_in_dim.20), channel_id=1, replica_groups={{0,16,64,80,128,144,192,208,256,272,320,336,384,400,448,464},{32,48,96,..., dimensions={0} | all-to-all | bytes 81920 | tf_op jit(solution)/shard_map/all_to_all | solution.py:47
  125.2 0.8 add_bitcast_fusion
  (13 shorter events, 0.1 us)
Async XLA Ops:
  2.5 24.6 %all-to-all-start = ((f32[16,64,128]{2,1,0:T(8,128)}), f32[16,64,128]{2,1,0:T(8,128)S(1)}, u32[]{:S(2)}, u32[]{:S(2)}) async-start(f32[16,64,128]{2,1,0:T(8,128)} %shard_map.64), calls=%async_computation | async-start | bytes 1048576 | tf_op jit(solution)/shard_map/all_to_all | solution.py:32
  12.9 8.2 %copy-start.10 = (f32[1,12,32]{2,0,1:T(1,128)S(1)}, f32[1,12,32]{2,0,1:T(1,128)}, u32[]{:S(2)}) copy-start(f32[1,12,32]{2,0,1:T(1,128)} %param.9) | copy-start | bytes 4612
  14.7 10.2 %collective-permute-start = (f32[128,128]{1,0:T(8,128)S(1)}, f32[128,128]{1,0:T(8,128)S(1)}, u32[]{:S(2)}, u32[]{:S(2)}) collective-permute-start(f32[128,128]{1,0:T(8,128)S(1)} %get-tuple-element.58), channel_id=1, source_target_pairs={{1,2},{3,4},{5,6},{7,8},{9,10},{11,12},{13,14},{2,1},{4,3},{6,5},{... | collective-permute-start | bytes 196616 | tf_op jit(solution)/shard_map/ppermute | solution.py:27
  15.4 9.5 %collective-permute-start.1 = (f32[128,128]{1,0:T(8,128)S(1)}, f32[128,128]{1,0:T(8,128)S(1)}, u32[]{:S(2)}, u32[]{:S(2)}) collective-permute-start(f32[128,128]{1,0:T(8,128)S(1)} %get-tuple-element.59), channel_id=1, source_target_pairs={{0,1},{1,0},{2,3},{3,2},{4,5},{5,4},{6,7},{7,6},{8,9},{9,8},{10,11... | collective-permute-start | bytes 196616 | tf_op jit(solution)/shard_map/ppermute | solution.py:28
  24.9 20.0 %copy-start.4 = (f32[12,32,128]{2,1,0:T(8,128)S(1)}, f32[12,32,128]{2,1,0:T(8,128)}, u32[]{:S(2)}) copy-start(f32[12,32,128]{2,1,0:T(8,128)} %get-tuple-element.50.sides) | copy-start | bytes 589828
  24.9 20.0 %copy-start.7 = (bf16[128,768]{1,0:T(8,128)(2,1)S(1)}, bf16[128,768]{1,0:T(8,128)(2,1)}, u32[]{:S(2)}) copy-start(bf16[128,768]{1,0:T(8,128)(2,1)} %get-tuple-element.51.basis_rows) | copy-start | bytes 589828
  27.1 17.8 %copy-start = (f32[1,12,64,128]{3,2,1,0:T(8,128)S(1)}, f32[1,12,64,128]{3,2,1,0:T(8,128)}, u32[]{:S(2)}) copy-start(f32[1,12,64,128]{3,2,1,0:T(8,128)} %param.6) | copy-start | bytes 1179652
  27.1 17.8 %copy-start.1 = (f32[1,12,64,128]{3,2,1,0:T(8,128)S(1)}, f32[1,12,64,128]{3,2,1,0:T(8,128)}, u32[]{:S(2)}) copy-start(f32[1,12,64,128]{3,2,1,0:T(8,128)} %param.8) | copy-start | bytes 1179652
  27.1 17.8 %copy-start.2 = (bf16[12,128,128]{2,1,0:T(8,128)(2,1)S(1)}, bf16[12,128,128]{2,1,0:T(8,128)(2,1)}, u32[]{:S(2)}) copy-start(bf16[12,128,128]{2,1,0:T(8,128)(2,1)} %get-tuple-element.48.tiles) | copy-start | bytes 1179652
  27.1 17.8 %copy-start.3 = (bf16[12,64,128]{2,1,0:T(8,128)(2,1)S(1)}, bf16[12,64,128]{2,1,0:T(8,128)(2,1)}, u32[]{:S(2)}) copy-start(bf16[12,64,128]{2,1,0:T(8,128)(2,1)} %get-tuple-element.49.tiles_own) | copy-start | bytes 589828
  28.3 16.6 %collective-permute-start.2 = (f32[12,16,128]{2,1,0:T(8,128)S(1)}, f32[12,16,128]{2,1,0:T(8,128)S(1)}, u32[]{:S(2)}, u32[]{:S(2)}) collective-permute-start(f32[12,16,128]{2,1,0:T(8,128)S(1)} %get-tuple-element.62), channel_id=1, source_target_pairs={{0,16},{16,0},{32,48},{48,32},{64,80},{80,64},{96,112},{112,96},{1... | collective-permute-start | bytes 294920 | tf_op jit(solution)/shard_map/ppermute | solution.py:28
  32.4 12.5 %collective-permute-start.5 = (f32[12,16,128]{2,1,0:T(8,128)S(1)}, f32[12,16,128]{2,1,0:T(8,128)S(1)}, u32[]{:S(2)}, u32[]{:S(2)}) collective-permute-start(f32[12,16,128]{2,1,0:T(8,128)S(1)} %get-tuple-element.65), channel_id=1, source_target_pairs={{16,32},{48,64},{80,96},{112,128},{144,160},{176,192},{208,224},{2... | collective-permute-start | bytes 294920 | tf_op jit(solution)/shard_map/ppermute | solution.py:27
  40.2 4.7 %collective-permute-start.3 = (f32[64,128]{1,0:T(8,128)S(1)}, f32[64,128]{1,0:T(8,128)S(1)}, u32[]{:S(2)}, u32[]{:S(2)}) collective-permute-start(f32[64,128]{1,0:T(8,128)S(1)} %get-tuple-element.63), channel_id=1, source_target_pairs={{0,1},{1,0},{2,3},{3,2},{4,5},{5,4},{6,7},{7,6},{8,9},{9,8},{10,11... | collective-permute-start | bytes 98312 | tf_op jit(solution)/shard_map/ppermute | solution.py:28
  42.2 2.7 %collective-permute-start.4 = (f32[64,128]{1,0:T(8,128)S(1)}, f32[64,128]{1,0:T(8,128)S(1)}, u32[]{:S(2)}, u32[]{:S(2)}) collective-permute-start(f32[64,128]{1,0:T(8,128)S(1)} %get-tuple-element.64), channel_id=1, source_target_pairs={{1,2},{3,4},{5,6},{7,8},{9,10},{11,12},{13,14},{2,1},{4,3},{6,5},{... | collective-permute-start | bytes 98312 | tf_op jit(solution)/shard_map/ppermute | solution.py:27
  47.4 10.6 %copy-start.12 = (f32[64,128]{1,0:T(8,128)S(1)}, f32[64,128]{1,0:T(8,128)}, u32[]{:S(2)}) copy-start(f32[64,128]{1,0:T(8,128)} %get-tuple-element.70) | copy-start | bytes 98308
  47.4 11.3 %copy-start.11 = (f32[64,128]{1,0:T(8,128)S(1)}, f32[64,128]{1,0:T(8,128)}, u32[]{:S(2)}) copy-start(f32[64,128]{1,0:T(8,128)} %get-tuple-element.71) | copy-start | bytes 98308
  47.5 22.0 %all-to-all-start.1 = ((f32[16,64,128]{2,1,0:T(8,128)}), f32[16,64,128]{2,1,0:T(8,128)S(1)}, u32[]{:S(2)}, u32[]{:S(2)}) async-start(f32[16,64,128]{2,1,0:T(8,128)} %get-tuple-element.68), calls=%async_computation.1 | async-start | bytes 1048576 | tf_op jit(solution)/shard_map/all_to_all | solution.py:32
  58.1 6.9 %collective-permute-start.6 = (f32[64,128]{1,0:T(8,128)S(1)}, f32[64,128]{1,0:T(8,128)S(1)}, u32[]{:S(2)}, u32[]{:S(2)}) collective-permute-start(f32[64,128]{1,0:T(8,128)S(1)} %copy-done.12), channel_id=1, source_target_pairs={{1,2},{3,4},{5,6},{7,8},{9,10},{11,12},{13,14},{2,1},{4,3},{6,5},{... | collective-permute-start | bytes 98312 | tf_op jit(solution)/shard_map/ppermute | solution.py:27
  58.7 7.3 %collective-permute-start.7 = (f32[64,128]{1,0:T(8,128)S(1)}, f32[64,128]{1,0:T(8,128)S(1)}, u32[]{:S(2)}, u32[]{:S(2)}) collective-permute-start(f32[64,128]{1,0:T(8,128)S(1)} %copy-done.11), channel_id=1, source_target_pairs={{0,1},{1,0},{2,3},{3,2},{4,5},{5,4},{6,7},{7,6},{8,9},{9,8},{10,11... | collective-permute-start | bytes 98312 | tf_op jit(solution)/shard_map/ppermute | solution.py:28
  64.4 1.6 %copy-start.8 = (f32[64,128]{1,0:T(8,128)S(1)}, f32[64,128]{1,0:T(8,128)}, u32[]{:S(2)}) copy-start(f32[64,128]{1,0:T(8,128)} %get-tuple-element.72.far_tile) | copy-start | bytes 98308
  64.5 1.6 %copy-start.9 = (f32[64,128]{1,0:T(8,128)S(1)}, f32[64,128]{1,0:T(8,128)}, u32[]{:S(2)}) copy-start(f32[64,128]{1,0:T(8,128)} %get-tuple-element.73.near_tile) | copy-start | bytes 98308
  69.5 15.5 %copy-start.5 = (f32[12,64,128]{2,1,0:T(8,128)S(1)}, f32[12,64,128]{2,1,0:T(8,128)}, u32[]{:S(2)}) copy-start(f32[12,64,128]{2,1,0:T(8,128)} %get-tuple-element.66.image) | copy-start | bytes 1179652
  69.5 15.5 %copy-start.6 = (f32[12,64,128]{2,1,0:T(8,128)S(1)}, f32[12,64,128]{2,1,0:T(8,128)}, u32[]{:S(2)}) copy-start(f32[12,64,128]{2,1,0:T(8,128)} %get-tuple-element.67.rest) | copy-start | bytes 1179652
  70.6 14.3 %collective-permute-start.8 = (f32[12,16,128]{2,1,0:T(8,128)S(1)}, f32[12,16,128]{2,1,0:T(8,128)S(1)}, u32[]{:S(2)}, u32[]{:S(2)}) collective-permute-start(f32[12,16,128]{2,1,0:T(8,128)S(1)} %get-tuple-element.75), channel_id=1, source_target_pairs={{0,16},{16,0},{32,48},{48,32},{64,80},{80,64},{96,112},{112,96},{1... | collective-permute-start | bytes 294920 | tf_op jit(solution)/shard_map/ppermute | solution.py:28
  72.6 12.4 %collective-permute-start.11 = (f32[12,16,128]{2,1,0:T(8,128)S(1)}, f32[12,16,128]{2,1,0:T(8,128)S(1)}, u32[]{:S(2)}, u32[]{:S(2)}) collective-permute-start(f32[12,16,128]{2,1,0:T(8,128)S(1)} %get-tuple-element.78), channel_id=1, source_target_pairs={{16,32},{48,64},{80,96},{112,128},{144,160},{176,192},{208,224},{2... | collective-permute-start | bytes 294920 | tf_op jit(solution)/shard_map/ppermute | solution.py:27
  80.3 4.7 %collective-permute-start.9 = (f32[64,128]{1,0:T(8,128)S(1)}, f32[64,128]{1,0:T(8,128)S(1)}, u32[]{:S(2)}, u32[]{:S(2)}) collective-permute-start(f32[64,128]{1,0:T(8,128)S(1)} %get-tuple-element.76), channel_id=1, source_target_pairs={{0,1},{1,0},{2,3},{3,2},{4,5},{5,4},{6,7},{7,6},{8,9},{9,8},{10,11... | collective-permute-start | bytes 98312 | tf_op jit(solution)/shard_map/ppermute | solution.py:28
  82.3 2.6 %collective-permute-start.10 = (f32[64,128]{1,0:T(8,128)S(1)}, f32[64,128]{1,0:T(8,128)S(1)}, u32[]{:S(2)}, u32[]{:S(2)}) collective-permute-start(f32[64,128]{1,0:T(8,128)S(1)} %get-tuple-element.77), channel_id=1, source_target_pairs={{1,2},{3,4},{5,6},{7,8},{9,10},{11,12},{13,14},{2,1},{4,3},{6,5},{... | collective-permute-start | bytes 98312 | tf_op jit(solution)/shard_map/ppermute | solution.py:27

commit v4 on v3

--- a/solution.py
+++ b/solution.py
@@ -101,30 +101,7 @@
     return loads
 
 
-def edge_kernel(odd, coupling_in, pair_in, residual_in, near, far, coupling, pair, residual, sems):
-    blocks, nodes = pair_in.shape[:2]
-    loads = start_all(
-        [
-            (source.at[b], target.at[i])
-            for source, target in ((pair_in, pair), (coupling_in, coupling), (residual_in, residual))
-            for i, b in enumerate((0, blocks - 1))
-        ],
-        sems,
-    )
-    for load in loads:
-        load.wait()
-    even = odd[1] == 0
-    start, beside, own = block_sweep(pair[0], coupling[0], residual[0])
-    last, beyond, own_last = block_sweep(pair[1], coupling[1], residual[1])
-    to_previous = jnp.concatenate([beside[:, :nodes], own], axis=1)
-    to_next = jnp.concatenate([beyond[:, nodes:], own_last], axis=1)
-    near[:nodes] = jnp.where(even, last, start)
-    far[:nodes] = jnp.where(even, start, last)
-    near[nodes:] = jnp.where(even, to_next, to_previous)
-    far[nodes:] = jnp.where(even, to_previous, to_next)
-
-
-def prepare_kernel(side, coupling_in, pair_in, residual_in, basis_in, inverse_in, sweep, sweep_own, tiles_out, tiles_own_out, start, sides_out, basis_rows_out, basis_columns, coarse_rows, coupling, pair, residual, basis, inverse_rows, tiles, tiles_own, sides, basis_rows, sems, stores):
+def prepare_kernel(side, coupling_in, pair_in, residual_in, basis_in, inverse_in, sweep, sweep_own, tiles_out, tiles_own_out, edge_tiles_out, start, sides_out, basis_rows_out, basis_columns, coarse_rows, coupling, pair, residual, basis, inverse_rows, tiles, tiles_own, sides, basis_rows, sems, stores):
     blocks, nodes, columns = residual.shape
     loads = start_all(
         [
@@ -150,7 +127,15 @@
     parts = rows_split(basis[...])
     basis_rows[...] = parts
     copies = start_all(
-        [(tiles, tiles_out), (tiles_own, tiles_own_out), (sides, sides_out), (basis_rows, basis_rows_out)], stores
+        [
+            (tiles, tiles_out),
+            (tiles_own, tiles_own_out),
+            (sides, sides_out),
+            (basis_rows, basis_rows_out),
+            (tiles.at[0], edge_tiles_out.at[0]),
+            (tiles.at[blocks - 1], edge_tiles_out.at[1]),
+        ],
+        stores,
     )
     coarse_rows[...] = rows_split(inverse_rows[...])
     basis_columns[...] = parts.astype(jnp.float32).T.astype(jnp.bfloat16)
@@ -227,23 +212,36 @@
     far_block[...] = jnp.where(even, update[0], update[blocks - 1])
 
 
-def image_blocks(odd, tiles, tiles_own, sides, update, near_face, far_face, near_block, far_block):
-    blocks, nodes, _ = update.shape
-    faces = near_face.shape[1]
+def linear_kernel(tiles, tiles_own, update, out):
+    blocks = update.shape[0]
+    parts = [columns_split(update[b]) for b in range(blocks)]
+    nothing = jnp.zeros_like(parts[0])
+    for b in range(blocks):
+        before = parts[b - 1] if b else nothing
+        after = parts[b + 1] if b + 1 < blocks else nothing
+        out[b] = tile_product(tiles[b], tiles_own[b], before, after, parts[b])
+
+
+def image_blocks(odd, edge_tiles, sides, linear, near_face, far_face, near_block, far_block):
+    blocks, nodes, _ = linear.shape
+    faces = near_face.shape[2]
     even = odd[1] == 0
-    low = jnp.where(even, far_block[...], near_block[...])
-    high = jnp.where(even, near_block[...], far_block[...])
-    parts = [columns_split(value) for value in (low, *(update[b] for b in range(blocks)), high)]
+    low = columns_split(jnp.where(even, far_block[...], near_block[...]))
+    high = columns_split(jnp.where(even, near_block[...], far_block[...]))
     even = odd[0] == 0
     for b in range(blocks):
-        linear = tile_product(tiles[b], tiles_own[b], parts[b], parts[b + 2], parts[b + 1])
-        below = jnp.where(even, far_face[b], near_face[b])
-        above = jnp.where(even, near_face[b], far_face[b])
+        new = linear[b]
+        if b == 0:
+            new = new + product(edge_tiles[0][:, :nodes], low)
+        if b == blocks - 1:
+            new = new + product(edge_tiles[1][:, nodes:], high)
+        below = jnp.where(even, far_face[b], near_face[0, b])
+        above = jnp.where(even, near_face[1, b], far_face[b])
         yield b, jnp.concatenate(
             [
-                linear[:faces] + sides[b, :faces] * below,
-                linear[faces : nodes - faces],
-                linear[nodes - faces :] + sides[b, faces:] * above,
+                new[:faces] + sides[b, :faces] * below,
+                new[faces : nodes - faces],
+                new[nodes - faces :] + sides[b, faces:] * above,
             ],
             axis=0,
         )
@@ -253,9 +251,9 @@
     return start_all([(projected, spread.at[i]) for i in range(spread.shape[0])], sems)
 
 
-def image_kernel(odd, tiles, tiles_own, sides, basis_rows, pair, residual, update, near_face, near_block, far_block, far_face, image_out, rest_out, spread, start, near, far, image, rest, flat, projected, edges, sems, stores):
-    blocks, nodes, _ = update.shape
-    for b, new in image_blocks(odd, tiles, tiles_own, sides, update, near_face, far_face, near_block, far_block):
+def image_kernel(odd, edge_tiles, sides, basis_rows, pair, residual, linear, far_face, near_face, near_block, far_block, image_out, rest_out, spread, start, near, far, image, rest, flat, projected, edges, sems, stores):
+    blocks, nodes, _ = linear.shape
+    for b, new in image_blocks(odd, edge_tiles, sides, linear, near_face, far_face, near_block, far_block):
         image[b] = new
         left = residual[b] - new
         rest[b] = left
@@ -275,23 +273,44 @@
         copy.wait()
 
 
-def project_kernel(basis_in, field_in, spread, basis, field, projected, sems, arrived):
+def first_kernel(odd, basis_in, coupling_in, pair_in, field_in, spread, near, far, basis, field, coupling, pair, residual, projected, sems, arrived, edges_arrived):
     blocks, nodes, columns = field.shape
-    for load in start_all([(basis_in, basis), (field_in, field)], arrived):
+    loads = start_all([(basis_in, basis), (field_in, field)], arrived)
+    edge_loads = start_all(
+        [
+            (source.at[b], target.at[i])
+            for source, target in ((pair_in, pair), (coupling_in, coupling), (field_in, residual))
+            for i, b in enumerate((0, blocks - 1))
+        ],
+        edges_arrived,
+    )
+    for load in loads:
         load.wait()
     projected[...] = dot(basis[...], field[...].reshape(blocks * nodes, columns))
-    for copy in send_out(projected, spread, sems):
+    copies = send_out(projected, spread, sems)
+    for load in edge_loads:
+        load.wait()
+    even = odd[1] == 0
+    start, beside, own = block_sweep(pair[0], coupling[0], residual[0])
+    last, beyond, own_last = block_sweep(pair[1], coupling[1], residual[1])
+    to_previous = jnp.concatenate([beside[:, :nodes], own], axis=1)
+    to_next = jnp.concatenate([beyond[:, nodes:], own_last], axis=1)
+    near[:nodes] = jnp.where(even, last, start)
+    far[:nodes] = jnp.where(even, start, last)
+    near[nodes:] = jnp.where(even, to_next, to_previous)
+    far[nodes:] = jnp.where(even, to_previous, to_next)
+    for copy in copies:
         copy.wait()
 
 
-def sums_kernel(odd, tiles, tiles_own, sides, image, rest, update, near_face, near_block, far_block, far_face, sums):
-    nodes, columns = update.shape[1:]
+def sums_kernel(odd, edge_tiles, sides, image, rest, linear, far_face, near_face, near_block, far_block, sums):
+    nodes, columns = linear.shape[1:]
     parts = [jnp.zeros((8, columns), jnp.float32) for _ in range(5)]
 
     def inner(left, right):
         return jnp.sum((left * right).reshape(nodes // 8, 8, columns), axis=0)
 
-    for b, new in image_blocks(odd, tiles, tiles_own, sides, update, near_face, far_face, near_block, far_block):
+    for b, new in image_blocks(odd, edge_tiles, sides, linear, near_face, far_face, near_block, far_block):
         change = new * SCALE
         left, right = image[b], rest[b]
         for i, (x, y) in enumerate(((left, right), (left, left), (change, right), (change, left), (change, change))):
@@ -342,37 +361,33 @@
     spread_out = ((subs, own_coarse, columns), wide, pltpu.HBM)
     spreading = [pltpu.VMEM((own_coarse, columns), wide), pltpu.SemaphoreType.DMA((subs,))]
 
-    (spread,) = call(
-        project_kernel,
-        [spread_out],
+    spread, near, far = call(
+        first_kernel,
+        [spread_out, small, small],
         [
             pltpu.VMEM(basis_all.shape, wide),
             pltpu.VMEM((blocks, nodes, columns), wide),
+            *[pltpu.VMEM((2, nodes, columns), wide)] * 3,
             *spreading,
             pltpu.SemaphoreType.DMA((2,)),
-        ],
-        basis_all, residual,
-        slow=2,
+            pltpu.SemaphoreType.DMA((6,)),
+        ],
+        odd, basis_all, coupling[0], diag_pair[0], residual,
+        slow=4,
     )
     spread, odd, residual, coupling, diag_pair, side, basis_all = lax.optimization_barrier(
         (spread, odd, residual, coupling, diag_pair, side, basis_all)
     )
     pair = diag_pair[0]
-    near, far = call(
-        edge_kernel,
-        [small, small],
-        [pltpu.VMEM((2, nodes, columns), wide)] * 3 + [pltpu.SemaphoreType.DMA((6,))],
-        odd, coupling[0], pair, residual,
-        slow=3,
-    )
     halo = swap(near, far, "sub")
-    sweep, sweep_own, tiles, tiles_own, start, sides, basis_rows, basis_columns, coarse_rows = call(
+    sweep, sweep_own, tiles, tiles_own, edge_tiles, start, sides, basis_rows, basis_columns, coarse_rows = call(
         prepare_kernel,
         [
             (*tile, fast),
             (*tile_own, fast),
             (*tile, pltpu.HBM),
             (*tile_own, pltpu.HBM),
+            ((2, 2 * nodes, 2 * nodes), thin, pltpu.HBM),
             field,
             ((blocks, 2 * faces, columns), wide, pltpu.HBM),
             ((2 * own_coarse, blocks * nodes), thin, pltpu.HBM),
@@ -390,7 +405,7 @@
             pltpu.VMEM((blocks, 2 * faces, columns), wide),
             pltpu.VMEM((2 * own_coarse, blocks * nodes), thin),
             pltpu.SemaphoreType.DMA((5,)),
-            pltpu.SemaphoreType.DMA((4,)),
+            pltpu.SemaphoreType.DMA((6,)),
         ],
         side[0], coupling[0], pair, residual, basis_all, coarse_inverse[0],
         slow=5,
@@ -412,11 +427,17 @@
         update, near_face, far_face, near_block, far_block = call(
             update_kernel, [field, face, face, block, block], [], odd, coarse_rows, gathered, basis_columns, local
         )
-        faces_in = swap(near_face, far_face, "sec")
+        sections = lax.axis_size("sec")
+        pairs = [[i, i + 1] for i in range(0, sections, 2)]
+        faces_in = (
+            lax.all_gather(near_face, "sec", axis_index_groups=pairs),
+            lax.ppermute(far_face, "sec", pairings("sec")[1]),
+        )
         blocks_in = swap(near_block, far_block, "sub")
-        return kept, update, faces_in[0], blocks_in[0], blocks_in[1], faces_in[1]
-
-    kept_tiles, first, *given = precondition(start, *halo, None, spread)
+        (linear,) = call(linear_kernel, [field], [], tiles, tiles_own, update)
+        return kept, update, linear, faces_in[1], faces_in[0], *blocks_in
+
+    kept_tiles, first, linear, *given = precondition(start, *halo, None, spread)
     image, rest, spread, start, near, far = call(
         image_kernel,
         [kept, kept, spread_out, field, edge, edge],
@@ -429,10 +450,10 @@
             pltpu.SemaphoreType.DMA((subs,)),
             pltpu.SemaphoreType.DMA((4,)),
         ],
-        odd, tiles, tiles_own, sides, basis_rows, pair, residual, first, *given,
-    )
-    _, second, *given = precondition(start, *swap(near, far, "sub"), kept_tiles, spread)
-    (sums,) = call(sums_kernel, [((5, columns), wide, fast)], [], odd, tiles, tiles_own, sides, image, rest, second, *given)
+        odd, edge_tiles, sides, basis_rows, pair, residual, linear, *given,
+    )
+    _, second, linear, *given = precondition(start, *swap(near, far, "sub"), kept_tiles, spread)
+    (sums,) = call(sums_kernel, [((5, columns), wide, fast)], [], odd, edge_tiles, sides, image, rest, linear, *given)
     sums = total(sums)
     short = -sums[0] / sums[1]
     step = 1.0 - short

time: 127 us -> 123 us (0.969)
  starting transfers between devices: 60.6 us -> 53.8 us
  blocking collectives: 38.9 us -> 42.3 us
    ppermute x6 -> x4, starting transfers between devices: 18.2 us -> 2.65 us  [swap(): from_far = lax.ppermute(to_far, axis, far)]
    ppermute x0 -> x2, starting transfers between devices: none -> 14.7 us  [precondition(): lax.ppermute(far_face, 'sec', pairings('sec')[1])]
    ppermute x6 -> x4, starting transfers between devices: 21.4 us -> 15.4 us  [swap(): return (lax.ppermute(to_near, axis, near), from_far)]
    all_gather x0 -> x2, blocking collectives: none -> 4.16 us  [precondition(): lax.all_gather(near_face, 'sec', axis_index_groups=pairs)]
    all_to_all x2, waiting for transfers between devices: 1.75 us -> 5.4 us  [gather_sub(): lax.all_to_all(spread, 'sub', 0, 0, tiled=True)]
    ppermute x6 -> x4, waiting for transfers between devices: 5.09 us -> 1.77 us  [swap(): return (lax.ppermute(to_near, axis, near), from_far)]
    pallas_call x11 -> x12, Pallas kernels: 18 us -> 17.4 us  [call(): pl.pallas_call(kernel, out_shape=[(space or jax.ShapeDtypeStruct)(shape,...]
  transfers between devices with their start and end apart: 14 -> 12, of which waited for: 4 -> 4; matrix products, arithmetic and copies ran while one was open for 0% -> 0% of each run, Pallas kernels for 8% -> 7%
where the time goes in v4:
time: 123 us
  starting transfers between devices  53.8 us (44%)
  blocking collectives  42.3 us (34%)
  Pallas kernels  17.4 us (14%)
  waiting for transfers between devices  7.52 us (6%)
    all_to_all x2, blocking collectives, total(): lax.all_to_all(spread, axes, 0, 0, axis_index_groups=groups, tiled=True)  38.1 us
    all_to_all x2, starting transfers between devices, gather_sub(): lax.all_to_all(spread, 'sub', 0, 0, tiled=True)  21 us
    pallas_call x12, Pallas kernels, call(): pl.pallas_call(kernel, out_shape=[(space or jax.ShapeDtypeStruct)(shape,...  17.4 us
    ppermute x4, starting transfers between devices, swap(): return (lax.ppermute(to_near, axis, near), from_far)  15.4 us
    ppermute x2, starting transfers between devices, precondition(): lax.ppermute(far_face, 'sec', pairings('sec')[1])  14.7 us
    all_to_all x2, waiting for transfers between devices, gather_sub(): lax.all_to_all(spread, 'sub', 0, 0, tiled=True)  5.4 us
    all_gather x2, blocking collectives, precondition(): lax.all_gather(near_face, 'sec', axis_index_groups=pairs)  4.16 us
    ppermute x4, starting transfers between devices, swap(): from_far = lax.ppermute(to_far, axis, far)  2.65 us
  transfers between devices with their start and end apart: 12, of which 4 were waited for; matrix products, arithmetic and copies ran while one was open for 0% of the time, Pallas kernels for 7%

profile of v4, /device:TPU:1, one launch (start us, length us, event | category | flops | bytes accessed | tf_op | source)
XLA Modules:
  0.0 122.5 jit_solution(5104743015769697777)
XLA Ops:
  0.0 0.1 pad_add_fusion.odd
  0.1 3.1 %shard_map.64 = (f32[16,64,128]{2,1,0:T(8,128)}, f32[128,128]{1,0:T(8,128)S(1)}, f32[128,128]{1,0:T(8,128)S(1)}) custom-call(s32[2]{0:T(128)S(1)} %pad_add_fusion.odd, f32[64,768]{1,0:T(8,128)} %bitcast.69, f32[12,64,128]{2,1,0:T(8,128)} %bitcast.67, f32[12,64,128]{2,1,0:T(8,128)} %bitcast.55, f32[12,64,128]{2,1,0:T(8,128)} %bitcast.58), custom_call_target="tpu_custom_call" | custom-call | flops 1000 | bytes 1000 | tf_op jit(solution)/shard_map/pallas_call | solution.py:332
  3.2 0.0 copy-start.12
  3.2 10.4 %all-to-all-start = ((f32[16,64,128]{2,1,0:T(8,128)}), f32[16,64,128]{2,1,0:T(8,128)S(1)}, u32[]{:S(2)}, u32[]{:S(2)}) async-start(f32[16,64,128]{2,1,0:T(8,128)} %get-tuple-element.57), calls=%async_computation | async-start | bytes 1048576 | tf_op jit(solution)/shard_map/all_to_all | solution.py:32
  13.6 0.7 collective-permute-start
  14.3 5.7 %collective-permute-start.1 = (f32[128,128]{1,0:T(8,128)S(1)}, f32[128,128]{1,0:T(8,128)S(1)}, u32[]{:S(2)}, u32[]{:S(2)}) collective-permute-start(f32[128,128]{1,0:T(8,128)S(1)} %get-tuple-element.63), channel_id=1, source_target_pairs={{0,1},{1,0},{2,3},{3,2},{4,5},{5,4},{6,7},{7,6},{8,9},{9,8},{10,11... | collective-permute-start | bytes 196616 | tf_op jit(solution)/shard_map/ppermute | solution.py:28
  19.9 0.0 copy-done.12
  20.0 3.3 %shard_map.65 = (bf16[12,128,128]{2,1,0:T(8,128)(2,1)S(1)}, bf16[12,64,128]{2,1,0:T(8,128)(2,1)S(1)}, bf16[12,128,128]{2,1,0:T(8,128)(2,1)}, bf16[12,64,128]{2,1...) custom-call(f32[12,32]{1,0:T(8,128)S(1)} %bitcast.65, ...), custom_call_target="tpu_custom_call" | custom-call | flops 1000 | bytes 1000 | tf_op jit(solution)/shard_map/pallas_call | solution.py:332
  23.3 0.5 shard_map.66.partial
  23.8 0.0 collective-permute-done.far
  23.8 0.0 collective-permute-done.1.near
  23.8 2.1 %shard_map.67 = (f32[12,64,128]{2,1,0:T(8,128)S(1)}, f32[64,128]{1,0:T(8,128)}, f32[64,128]{1,0:T(8,128)}) custom-call(s32[2]{0:T(128)S(1)} %pad_add_fusion.odd, bf16[12,128,128]{2,1,0:T(8,128)(2,1)S(1)} %get-tuple-element.59.tiles, bf16[12,64,128]{2,1,0:T(8,128)(2,1)S(1)} %get-tuple-element.60.tiles_own, f32[12,64,128]{2,1,0:T(8,128)S(1)} %get-tuple-element.61.start, ...), custom_call_target="tpu_custom_call" | custom-call | flops 1000 | bytes 1000 | tf_op jit(solution)/shard_map/pallas_call | solution.py:332
  25.9 1.4 %all-to-all-done = f32[16,64,128]{2,1,0:T(8,128)S(1)} async-done(((f32[16,64,128]{2,1,0:T(8,128)}), f32[16,64,128]{2,1,0:T(8,128)S(1)}, u32[]{:S(2)}, u32[]{:S(2)}) %all-to-all-start) | async-done | bytes 524320 | tf_op jit(solution)/shard_map/all_to_all | solution.py:32
  27.4 1.1 shard_map.68
  28.5 10.5 %collective-permute-start.2 = (f32[12,16,128]{2,1,0:T(8,128)S(1)}, f32[12,16,128]{2,1,0:T(8,128)S(1)}, u32[]{:S(2)}, u32[]{:S(2)}) collective-permute-start(f32[12,16,128]{2,1,0:T(8,128)S(1)} %get-tuple-element.66), channel_id=1, source_target_pairs={{16,32},{48,64},{80,96},{112,128},{144,160},{176,192},{208,224},{2... | collective-permute-start | bytes 294920 | tf_op jit(solution)/shard_map/ppermute | solution.py:434
  39.0 2.0 %collective-permute-start.3 = (f32[64,128]{1,0:T(8,128)S(1)}, f32[64,128]{1,0:T(8,128)S(1)}, u32[]{:S(2)}, u32[]{:S(2)}) collective-permute-start(f32[64,128]{1,0:T(8,128)S(1)} %get-tuple-element.68), channel_id=1, source_target_pairs={{0,1},{1,0},{2,3},{3,2},{4,5},{5,4},{6,7},{7,6},{8,9},{9,8},{10,11... | collective-permute-start | bytes 98312 | tf_op jit(solution)/shard_map/ppermute | solution.py:28
  41.0 0.7 collective-permute-start.4
  41.7 0.0 copy-done.2
  41.7 0.0 copy-done.4
  41.7 0.0 copy-start
  41.7 0.0 copy-start.1
  41.7 0.0 copy-start.9
  41.7 0.5 shard_map.69.linear
  42.2 0.0 copy-start.3
  42.2 0.0 copy-start.7
  42.2 2.1 %all-gather = f32[24,16,128]{2,1,0:T(8,128)S(1)} all-gather(f32[12,16,128]{2,1,0:T(8,128)S(1)} %get-tuple-element.67), channel_id=2, replica_groups={{0,16},{32,48},{64,80},{96,112},{128,144},{160,176},{192,208},{224,240}..., dimensions={0}, use_global_device_ids=true | all-gather | bytes 294912 | tf_op jit(solution)/shard_map/all_gather | solution.py:433
  44.3 0.0 collective-permute-done.3.near_block
  44.3 0.0 collective-permute-done.4.far_block
  44.3 0.0 collective-permute-done.2.far_face
  44.3 0.0 copy-done
  44.3 0.0 copy-done.1
  44.3 0.0 copy-done.9
  44.3 0.0 copy-done.3
  44.3 0.0 copy-done.7
  44.3 2.2 %shard_map.70 = (f32[12,64,128]{2,1,0:T(8,128)}, f32[12,64,128]{2,1,0:T(8,128)}, f32[16,64,128]{2,1,0:T(8,128)}, f32[12,64,128]{2,1,0:T(8,128)S(1)}, f32[64,128]{1,0:T(8,128)}, /*index=5*/f32[64,128]{1,0:T(8,128)}) custom-call(s32[2]{0:T(128)S(1)} %pad_add_fusion.odd, bf16[2,128,128]{2,1,0:T(8,128)(2,1)S(1)} %copy-done.7, f32[12,32,128]{2,1,0:T(8,128)S(1)} %copy-done.3, ...), custom_call_target="tpu_custom_call" | custom-call | flops 1000 | bytes 1000 | tf_op jit(solution)/shard_map/pallas_call | solution.py:332
  46.6 0.0 copy-start.14
  46.6 10.6 %all-to-all-start.1 = ((f32[16,64,128]{2,1,0:T(8,128)}), f32[16,64,128]{2,1,0:T(8,128)S(1)}, u32[]{:S(2)}, u32[]{:S(2)}) async-start(f32[16,64,128]{2,1,0:T(8,128)} %get-tuple-element.72), calls=%async_computation.1 | async-start | bytes 1048576 | tf_op jit(solution)/shard_map/all_to_all | solution.py:32
  57.2 0.7 collective-permute-start.5
  57.9 5.7 %collective-permute-start.6 = (f32[64,128]{1,0:T(8,128)S(1)}, f32[64,128]{1,0:T(8,128)S(1)}, u32[]{:S(2)}, u32[]{:S(2)}) collective-permute-start(f32[64,128]{1,0:T(8,128)S(1)} %copy-done.13), channel_id=1, source_target_pairs={{0,1},{1,0},{2,3},{3,2},{4,5},{5,4},{6,7},{7,6},{8,9},{9,8},{10,11... | collective-permute-start | bytes 98312 | tf_op jit(solution)/shard_map/ppermute | solution.py:28
  63.6 0.0 copy-start.10
  63.6 0.0 copy-start.11
  63.7 0.5 shard_map.71.partial
  64.1 0.0 collective-permute-done.5.far
  64.1 1.8 %collective-permute-done.6.near = f32[64,128]{1,0:T(8,128)S(1)} collective-permute-done((f32[64,128]{1,0:T(8,128)S(1)}, f32[64,128]{1,0:T(8,128)S(1)}, u32[]{:S(2)}, u32[]{:S(2)}) %collective-permute-start.6) | collective-permute-done | bytes 32800 | tf_op jit(solution)/shard_map/ppermute | solution.py:28
  65.9 1.7 %shard_map.72.local = f32[12,64,128]{2,1,0:T(8,128)S(1)} custom-call(s32[2]{0:T(128)S(1)} %pad_add_fusion.odd, bf16[12,128,128]{2,1,0:T(8,128)(2,1)S(1)} %get-tuple-element.59.tiles, bf16[12,64,128]{2,1,0:T(8,128)(2,1)S(1)} %get-tuple-element.60.tiles_own, f32[12,64,128]{2,1,0:T(8,128)S(1)} %get-tuple-element.73.start, ...), custom_call_target="tpu_custom_call" | custom-call | flops 1000 | bytes 1000 | tf_op jit(solution)/shard_map/pallas_call | solution.py:332
  67.6 4.0 %all-to-all-done.1 = f32[16,64,128]{2,1,0:T(8,128)S(1)} async-done(((f32[16,64,128]{2,1,0:T(8,128)}), f32[16,64,128]{2,1,0:T(8,128)S(1)}, u32[]{:S(2)}, u32[]{:S(2)}) %all-to-all-start.1) | async-done | bytes 524320 | tf_op jit(solution)/shard_map/all_to_all | solution.py:32
  71.5 1.1 shard_map.73
  72.7 4.2 %collective-permute-start.7 = (f32[12,16,128]{2,1,0:T(8,128)S(1)}, f32[12,16,128]{2,1,0:T(8,128)S(1)}, u32[]{:S(2)}, u32[]{:S(2)}) collective-permute-start(f32[12,16,128]{2,1,0:T(8,128)S(1)} %get-tuple-element.79), channel_id=1, source_target_pairs={{16,32},{48,64},{80,96},{112,128},{144,160},{176,192},{208,224},{2... | collective-permute-start | bytes 294920 | tf_op jit(solution)/shard_map/ppermute | solution.py:434
  76.9 0.0 copy-start.5
  76.9 0.0 copy-start.6
  76.9 0.5 shard_map.74.linear
  77.4 2.0 %collective-permute-start.8 = (f32[64,128]{1,0:T(8,128)S(1)}, f32[64,128]{1,0:T(8,128)S(1)}, u32[]{:S(2)}, u32[]{:S(2)}) collective-permute-start(f32[64,128]{1,0:T(8,128)S(1)} %get-tuple-element.81), channel_id=1, source_target_pairs={{0,1},{1,0},{2,3},{3,2},{4,5},{5,4},{6,7},{7,6},{8,9},{9,8},{10,11... | collective-permute-start | bytes 98312 | tf_op jit(solution)/shard_map/ppermute | solution.py:28
  79.4 0.7 collective-permute-start.9
  80.1 0.0 copy-start.8
  80.1 2.1 %all-gather.1 = f32[24,16,128]{2,1,0:T(8,128)S(1)} all-gather(f32[12,16,128]{2,1,0:T(8,128)S(1)} %get-tuple-element.80), channel_id=3, replica_groups={{0,16},{32,48},{64,80},{96,112},{128,144},{160,176},{192,208},{224,240}..., dimensions={0}, use_global_device_ids=true | all-gather | bytes 294912 | tf_op jit(solution)/shard_map/all_gather | solution.py:433
  82.2 0.0 collective-permute-done.8.near_block
  82.2 0.0 collective-permute-done.9.far_block
  82.2 0.3 collective-permute-done.7.far_face
  82.5 0.0 copy-done.6
  82.6 0.8 shard_map.75
  83.5 23.0 %all_to_all.20 = f32[32,1,640]{2,1,0:T(1,128)S(1)} all-to-all(f32[32,1,640]{2,1,0:T(1,128)S(1)} %broadcast_in_dim.9), channel_id=1, replica_groups={{0,1,2,3,4,5,6,7,8,9,10,11,12,13,14,15,32,33,34,35,36,37,38,39,40,41,42..., dimensions={0} | all-to-all | bytes 163840 | tf_op jit(solution)/shard_map/all_to_all | solution.py:47
  106.5 0.1 reduce_sum.20
  106.6 15.1 %all_to_all.21 = f32[16,1,640]{2,1,0:T(1,128)S(1)} all-to-all(f32[16,1,640]{2,1,0:T(1,128)S(1)} %broadcast_in_dim.20), channel_id=1, replica_groups={{0,16,64,80,128,144,192,208,256,272,320,336,384,400,448,464},{32,48,96,..., dimensions={0} | all-to-all | bytes 81920 | tf_op jit(solution)/shard_map/all_to_all | solution.py:47
  121.7 0.8 add_bitcast_fusion
  (16 shorter events, 0.2 us)
Async XLA Ops:
  3.2 16.8 %copy-start.12 = (f32[1,12,32]{2,0,1:T(1,128)S(1)}, f32[1,12,32]{2,0,1:T(1,128)}, u32[]{:S(2)}) copy-start(f32[1,12,32]{2,0,1:T(1,128)} %param.9) | copy-start | bytes 4612
  3.2 24.2 %all-to-all-start = ((f32[16,64,128]{2,1,0:T(8,128)}), f32[16,64,128]{2,1,0:T(8,128)S(1)}, u32[]{:S(2)}, u32[]{:S(2)}) async-start(f32[16,64,128]{2,1,0:T(8,128)} %get-tuple-element.57), calls=%async_computation | async-start | bytes 1048576 | tf_op jit(solution)/shard_map/all_to_all | solution.py:32
  13.6 10.2 %collective-permute-start = (f32[128,128]{1,0:T(8,128)S(1)}, f32[128,128]{1,0:T(8,128)S(1)}, u32[]{:S(2)}, u32[]{:S(2)}) collective-permute-start(f32[128,128]{1,0:T(8,128)S(1)} %get-tuple-element.62), channel_id=1, source_target_pairs={{1,2},{3,4},{5,6},{7,8},{9,10},{11,12},{13,14},{2,1},{4,3},{6,5},{... | collective-permute-start | bytes 196616 | tf_op jit(solution)/shard_map/ppermute | solution.py:27
  14.3 9.5 %collective-permute-start.1 = (f32[128,128]{1,0:T(8,128)S(1)}, f32[128,128]{1,0:T(8,128)S(1)}, u32[]{:S(2)}, u32[]{:S(2)}) collective-permute-start(f32[128,128]{1,0:T(8,128)S(1)} %get-tuple-element.63), channel_id=1, source_target_pairs={{0,1},{1,0},{2,3},{3,2},{4,5},{5,4},{6,7},{7,6},{8,9},{9,8},{10,11... | collective-permute-start | bytes 196616 | tf_op jit(solution)/shard_map/ppermute | solution.py:28
  27.4 14.3 %copy-start.2 = (bf16[12,128,128]{2,1,0:T(8,128)(2,1)S(1)}, bf16[12,128,128]{2,1,0:T(8,128)(2,1)}, u32[]{:S(2)}) copy-start(bf16[12,128,128]{2,1,0:T(8,128)(2,1)} %get-tuple-element.54.tiles) | copy-start | bytes 1179652
  27.4 14.3 %copy-start.4 = (bf16[12,64,128]{2,1,0:T(8,128)(2,1)S(1)}, bf16[12,64,128]{2,1,0:T(8,128)(2,1)}, u32[]{:S(2)}) copy-start(bf16[12,64,128]{2,1,0:T(8,128)(2,1)} %get-tuple-element.55.tiles_own) | copy-start | bytes 589828
  28.5 15.8 %collective-permute-start.2 = (f32[12,16,128]{2,1,0:T(8,128)S(1)}, f32[12,16,128]{2,1,0:T(8,128)S(1)}, u32[]{:S(2)}, u32[]{:S(2)}) collective-permute-start(f32[12,16,128]{2,1,0:T(8,128)S(1)} %get-tuple-element.66), channel_id=1, source_target_pairs={{16,32},{48,64},{80,96},{112,128},{144,160},{176,192},{208,224},{2... | collective-permute-start | bytes 294920 | tf_op jit(solution)/shard_map/ppermute | solution.py:434
  39.0 5.3 %collective-permute-start.3 = (f32[64,128]{1,0:T(8,128)S(1)}, f32[64,128]{1,0:T(8,128)S(1)}, u32[]{:S(2)}, u32[]{:S(2)}) collective-permute-start(f32[64,128]{1,0:T(8,128)S(1)} %get-tuple-element.68), channel_id=1, source_target_pairs={{0,1},{1,0},{2,3},{3,2},{4,5},{5,4},{6,7},{7,6},{8,9},{9,8},{10,11... | collective-permute-start | bytes 98312 | tf_op jit(solution)/shard_map/ppermute | solution.py:28
  41.0 3.3 %collective-permute-start.4 = (f32[64,128]{1,0:T(8,128)S(1)}, f32[64,128]{1,0:T(8,128)S(1)}, u32[]{:S(2)}, u32[]{:S(2)}) collective-permute-start(f32[64,128]{1,0:T(8,128)S(1)} %get-tuple-element.69), channel_id=1, source_target_pairs={{1,2},{3,4},{5,6},{7,8},{9,10},{11,12},{13,14},{2,1},{4,3},{6,5},{... | collective-permute-start | bytes 98312 | tf_op jit(solution)/shard_map/ppermute | solution.py:27
  41.7 2.6 %copy-start = (f32[1,12,64,128]{3,2,1,0:T(8,128)S(1)}, f32[1,12,64,128]{3,2,1,0:T(8,128)}, u32[]{:S(2)}) copy-start(f32[1,12,64,128]{3,2,1,0:T(8,128)} %param.8) | copy-start | bytes 1179652
  41.7 2.6 %copy-start.1 = (f32[1,12,64,128]{3,2,1,0:T(8,128)S(1)}, f32[1,12,64,128]{3,2,1,0:T(8,128)}, u32[]{:S(2)}) copy-start(f32[1,12,64,128]{3,2,1,0:T(8,128)} %param.6) | copy-start | bytes 1179652
  41.7 2.6 %copy-start.9 = (bf16[128,768]{1,0:T(8,128)(2,1)S(1)}, bf16[128,768]{1,0:T(8,128)(2,1)}, u32[]{:S(2)}) copy-start(bf16[128,768]{1,0:T(8,128)(2,1)} %get-tuple-element.53.basis_rows) | copy-start | bytes 589828
  42.2 2.1 %copy-start.3 = (f32[12,32,128]{2,1,0:T(8,128)S(1)}, f32[12,32,128]{2,1,0:T(8,128)}, u32[]{:S(2)}) copy-start(f32[12,32,128]{2,1,0:T(8,128)} %get-tuple-element.52.sides) | copy-start | bytes 589828
  42.2 2.1 %copy-start.7 = (bf16[2,128,128]{2,1,0:T(8,128)(2,1)S(1)}, bf16[2,128,128]{2,1,0:T(8,128)(2,1)}, u32[]{:S(2)}) copy-start(bf16[2,128,128]{2,1,0:T(8,128)(2,1)} %get-tuple-element.51.edge_tiles) | copy-start | bytes 196612
  46.6 10.7 %copy-start.14 = (f32[64,128]{1,0:T(8,128)S(1)}, f32[64,128]{1,0:T(8,128)}, u32[]{:S(2)}) copy-start(f32[64,128]{1,0:T(8,128)} %get-tuple-element.74) | copy-start | bytes 98308
  46.6 11.3 %copy-start.13 = (f32[64,128]{1,0:T(8,128)S(1)}, f32[64,128]{1,0:T(8,128)}, u32[]{:S(2)}) copy-start(f32[64,128]{1,0:T(8,128)} %get-tuple-element.75) | copy-start | bytes 98308
  46.6 25.0 %all-to-all-start.1 = ((f32[16,64,128]{2,1,0:T(8,128)}), f32[16,64,128]{2,1,0:T(8,128)S(1)}, u32[]{:S(2)}, u32[]{:S(2)}) async-start(f32[16,64,128]{2,1,0:T(8,128)} %get-tuple-element.72), calls=%async_computation.1 | async-start | bytes 1048576 | tf_op jit(solution)/shard_map/all_to_all | solution.py:32
  57.2 6.9 %collective-permute-start.5 = (f32[64,128]{1,0:T(8,128)S(1)}, f32[64,128]{1,0:T(8,128)S(1)}, u32[]{:S(2)}, u32[]{:S(2)}) collective-permute-start(f32[64,128]{1,0:T(8,128)S(1)} %copy-done.14), channel_id=1, source_target_pairs={{1,2},{3,4},{5,6},{7,8},{9,10},{11,12},{13,14},{2,1},{4,3},{6,5},{... | collective-permute-start | bytes 98312 | tf_op jit(solution)/shard_map/ppermute | solution.py:27
  57.9 8.0 %collective-permute-start.6 = (f32[64,128]{1,0:T(8,128)S(1)}, f32[64,128]{1,0:T(8,128)S(1)}, u32[]{:S(2)}, u32[]{:S(2)}) collective-permute-start(f32[64,128]{1,0:T(8,128)S(1)} %copy-done.13), channel_id=1, source_target_pairs={{0,1},{1,0},{2,3},{3,2},{4,5},{5,4},{6,7},{7,6},{8,9},{9,8},{10,11... | collective-permute-start | bytes 98312 | tf_op jit(solution)/shard_map/ppermute | solution.py:28
  63.6 2.3 %copy-start.10 = (f32[64,128]{1,0:T(8,128)S(1)}, f32[64,128]{1,0:T(8,128)}, u32[]{:S(2)}) copy-start(f32[64,128]{1,0:T(8,128)} %get-tuple-element.76.far_tile) | copy-start | bytes 98308
  63.6 2.3 %copy-start.11 = (f32[64,128]{1,0:T(8,128)S(1)}, f32[64,128]{1,0:T(8,128)}, u32[]{:S(2)}) copy-start(f32[64,128]{1,0:T(8,128)} %get-tuple-element.77.near_tile) | copy-start | bytes 98308
  72.7 9.8 %collective-permute-start.7 = (f32[12,16,128]{2,1,0:T(8,128)S(1)}, f32[12,16,128]{2,1,0:T(8,128)S(1)}, u32[]{:S(2)}, u32[]{:S(2)}) collective-permute-start(f32[12,16,128]{2,1,0:T(8,128)S(1)} %get-tuple-element.79), channel_id=1, source_target_pairs={{16,32},{48,64},{80,96},{112,128},{144,160},{176,192},{208,224},{2... | collective-permute-start | bytes 294920 | tf_op jit(solution)/shard_map/ppermute | solution.py:434
  76.9 5.6 %copy-start.5 = (f32[12,64,128]{2,1,0:T(8,128)S(1)}, f32[12,64,128]{2,1,0:T(8,128)}, u32[]{:S(2)}) copy-start(f32[12,64,128]{2,1,0:T(8,128)} %get-tuple-element.70.image) | copy-start | bytes 1179652
  76.9 5.6 %copy-start.6 = (f32[12,64,128]{2,1,0:T(8,128)S(1)}, f32[12,64,128]{2,1,0:T(8,128)}, u32[]{:S(2)}) copy-start(f32[12,64,128]{2,1,0:T(8,128)} %get-tuple-element.71.rest) | copy-start | bytes 1179652
  77.4 4.8 %collective-permute-start.8 = (f32[64,128]{1,0:T(8,128)S(1)}, f32[64,128]{1,0:T(8,128)S(1)}, u32[]{:S(2)}, u32[]{:S(2)}) collective-permute-start(f32[64,128]{1,0:T(8,128)S(1)} %get-tuple-element.81), channel_id=1, source_target_pairs={{0,1},{1,0},{2,3},{3,2},{4,5},{5,4},{6,7},{7,6},{8,9},{9,8},{10,11... | collective-permute-start | bytes 98312 | tf_op jit(solution)/shard_map/ppermute | solution.py:28
  79.4 2.8 %collective-permute-start.9 = (f32[64,128]{1,0:T(8,128)S(1)}, f32[64,128]{1,0:T(8,128)S(1)}, u32[]{:S(2)}, u32[]{:S(2)}) collective-permute-start(f32[64,128]{1,0:T(8,128)S(1)} %get-tuple-element.82), channel_id=1, source_target_pairs={{1,2},{3,4},{5,6},{7,8},{9,10},{11,12},{13,14},{2,1},{4,3},{6,5},{... | collective-permute-start | bytes 98312 | tf_op jit(solution)/shard_map/ppermute | solution.py:27
  80.1 2.4 %copy-start.8 = (bf16[2,128,128]{2,1,0:T(8,128)(2,1)S(1)}, bf16[2,128,128]{2,1,0:T(8,128)(2,1)}, u32[]{:S(2)}) copy-start(bf16[2,128,128]{2,1,0:T(8,128)(2,1)} %get-tuple-element.51.edge_tiles) | copy-start | bytes 196612

commit v5 on v4

--- a/solution.py
+++ b/solution.py
@@ -42,7 +42,7 @@
     ]
     across = [[4 * p + 2 * run + core for p in range(planes) for core in range(2)] for run in range(2)]
     flat = sums.reshape(1, -1)
-    for axes, groups in ((("sec", "sub"), within), ("sec", across)):
+    for axes, groups in (("sec", across), (("sec", "sub"), within)):
         spread = jnp.broadcast_to(flat[None], (len(groups[0]), *flat.shape))
         flat = jnp.sum(lax.all_to_all(spread, axes, 0, 0, axis_index_groups=groups, tiled=True), axis=0)
     return flat.reshape(sums.shape)
@@ -143,57 +143,66 @@
         copy.wait()
 
 
-def first_sweep_kernel(tiles, tiles_own, start, out):
+def inner_sweeps_kernel(tiles, tiles_own, start, out, first_ends):
     blocks, nodes, _ = start.shape
     parts = [columns_split(start[b]) for b in range(blocks)]
     nothing = jnp.zeros_like(parts[0])
+    for sweep in range(SWEEPS - 1):
+        new = [
+            start[b]
+            + tile_product(
+                tiles[b],
+                tiles_own[b],
+                parts[b - 1] if b else nothing,
+                parts[b + 1] if b + 1 < blocks else nothing,
+                parts[b],
+            )
+            for b in range(blocks)
+        ]
+        if sweep == 0:
+            first_ends[0], first_ends[1] = new[0], new[-1]
+        if sweep < SWEEPS - 2:
+            parts = [columns_split(value) for value in new]
     for b in range(blocks):
-        before = parts[b - 1] if b else nothing
-        after = parts[b + 1] if b + 1 < blocks else nothing
-        out[b] = start[b] + tile_product(tiles[b], tiles_own[b], before, after, parts[b])
-
-
-def sweep_kernel(odd, tiles, tiles_own, start, partial, far, near, far_tile, near_tile, out, one, two):
+        out[b] = new[b]
+
+
+def outer_sweeps_kernel(odd, tiles, tiles_own, start, inner, first_ends, far, near, far_tile, near_tile, out):
     blocks, nodes, _ = start.shape
     even = odd[1] == 0
-    low = jnp.where(even, far[...], near[...])
-    high = jnp.where(even, near[...], far[...])
-    low_tile = rows_split(jnp.where(even, far_tile[...], near_tile[...]))
-    high_tile = rows_split(jnp.where(even, near_tile[...], far_tile[...]))
-    low_parts, high_parts = columns_split(low), columns_split(high)
-    first, last = columns_split(start[0]), columns_split(start[blocks - 1])
-    one[0] = columns_split(low + product(low_tile, jnp.concatenate([first, low_parts], axis=0)))
-    one[blocks + 1] = columns_split(high + product(high_tile, jnp.concatenate([last, high_parts], axis=0)))
-    one[1] = columns_split(partial[0] + product(tiles[0][:, :nodes], low_parts))
-    one[blocks] = columns_split(partial[blocks - 1] + product(tiles[blocks - 1][:, nodes : 2 * nodes], high_parts))
-    for b in range(1, blocks - 1):
-        one[b + 1] = columns_split(partial[b])
-    source, target = one, two
-    for sweep in range(1, SWEEPS - 1):
-        final = sweep == SWEEPS - 2
-        for b in range(blocks):
-            new = start[b] + tile_product(tiles[b], tiles_own[b], source[b], source[b + 2], source[b + 1])
-            if final:
-                out[b] = new
-            else:
-                target[b + 1] = columns_split(new)
-        if not final:
-            target[0] = columns_split(low + product(low_tile, jnp.concatenate([source[1], source[0]], axis=0)))
-            target[blocks + 1] = columns_split(
-                high + product(high_tile, jnp.concatenate([source[blocks], source[blocks + 1]], axis=0))
-            )
-        source, target = target, source
-
-
-def keeping_sweep_kernel(odd, tiles, tiles_own, start, partial, far, near, out, far_kept, near_kept, one, two, sems):
-    nodes = start.shape[1]
-    far_tile, near_tile = far.at[nodes : 2 * nodes], near.at[nodes : 2 * nodes]
-    copies = start_all([(far_tile, far_kept), (near_tile, near_kept)], sems)
-    sweep_kernel(
-        odd, tiles, tiles_own, start, partial, far.at[:nodes], near.at[:nodes], far_tile, near_tile, out, one, two
-    )
-    for copy in copies:
-        copy.wait()
+    far_tile, near_tile = far_tile[-nodes:], near_tile[-nodes:]
+    ends = (
+        (0, 1, jnp.where(even, far[:nodes], near[:nodes]), jnp.where(even, far_tile, near_tile)),
+        (blocks - 1, -1, jnp.where(even, near[:nodes], far[:nodes]), jnp.where(even, near_tile, far_tile)),
+    )
+    for at, (end, inward, beside, tile) in enumerate(ends):
+        tile = rows_split(tile)
+
+        def of_block(b, outer, own=None, deeper=None):
+            lower, upper = tiles[b][:, :nodes], tiles[b][:, nodes:]
+            total = product(lower if inward == 1 else upper, outer)
+            if own is not None:
+                total = total + pair_product(tiles_own[b], own)
+            if deeper is not None:
+                total = total + product(upper if inward == 1 else lower, deeper)
+            return total
+
+        def of_beside(edge, last):
+            return beside + product(tile, jnp.concatenate([columns_split(edge), last], axis=0))
+
+        one, two, three = end, end + inward, end + 2 * inward
+        beside_0 = columns_split(beside)
+        first = of_block(one, beside_0)
+        beside_1 = columns_split(of_beside(start[one], beside_0))
+        beside_2 = columns_split(of_beside(first_ends[at] + first, beside_1))
+        first = columns_split(first)
+        second = columns_split(of_block(one, beside_1, first))
+        second_two = columns_split(of_block(two, first))
+        out[one] = inner[one] + of_block(one, beside_2, second, second_two)
+        out[two] = inner[two] + of_block(two, second, second_two)
+        out[three] = inner[three] + of_block(three, second_two)
+    for b in range(3, blocks - 3):
+        out[b] = inner[b]
 
 
 def update_kernel(odd, coarse_rows, gathered, basis_columns, local, update, near_face, far_face, near_block, far_block):
@@ -210,6 +219,16 @@
     even = odd[1] == 0
     near_block[...] = jnp.where(even, update[blocks - 1], update[0])
     far_block[...] = jnp.where(even, update[0], update[blocks - 1])
+
+
+def keeping_update_kernel(odd, coarse_rows, gathered, basis_columns, local, far, near, update, near_face, far_face, near_block, far_block, far_kept, near_kept, sems):
+    nodes = local.shape[1]
+    copies = start_all([(far.at[nodes : 2 * nodes], far_kept), (near.at[nodes : 2 * nodes], near_kept)], sems)
+    update_kernel(
+        odd, coarse_rows, gathered, basis_columns, local, update, near_face, far_face, near_block, far_block
+    )
+    for copy in copies:
+        copy.wait()
 
 
 def linear_kernel(tiles, tiles_own, update, out):
@@ -275,7 +294,6 @@
 
 def first_kernel(odd, basis_in, coupling_in, pair_in, field_in, spread, near, far, basis, field, coupling, pair, residual, projected, sems, arrived, edges_arrived):
     blocks, nodes, columns = field.shape
-    loads = start_all([(basis_in, basis), (field_in, field)], arrived)
     edge_loads = start_all(
         [
             (source.at[b], target.at[i])
@@ -284,10 +302,7 @@
         ],
         edges_arrived,
     )
-    for load in loads:
-        load.wait()
-    projected[...] = dot(basis[...], field[...].reshape(blocks * nodes, columns))
-    copies = send_out(projected, spread, sems)
+    loads = start_all([(basis_in, basis), (field_in, field)], arrived)
     for load in edge_loads:
         load.wait()
     even = odd[1] == 0
@@ -299,7 +314,10 @@
     far[:nodes] = jnp.where(even, start, last)
     near[nodes:] = jnp.where(even, to_next, to_previous)
     far[nodes:] = jnp.where(even, to_previous, to_next)
-    for copy in copies:
+    for load in loads:
+        load.wait()
+    projected[...] = dot(basis[...], field[...].reshape(blocks * nodes, columns))
+    for copy in send_out(projected, spread, sems):
         copy.wait()
 
 
@@ -357,7 +375,6 @@
     face = ((blocks, faces, columns), wide, fast)
     tile = ((blocks, 2 * nodes, 2 * nodes), thin)
     tile_own = ((blocks, nodes, 2 * nodes), thin)
-    padded = pltpu.VMEM((blocks + 2, nodes, 2 * columns), thin)
     spread_out = ((subs, own_coarse, columns), wide, pltpu.HBM)
     spreading = [pltpu.VMEM((own_coarse, columns), wide), pltpu.SemaphoreType.DMA((subs,))]
 
@@ -413,20 +430,20 @@
 
     def precondition(start, near, far, kept, spread):
         gathered = gather_sub(spread)
-        (partial,) = call(first_sweep_kernel, [field], [], sweep, sweep_own, start)
-        given = (odd, sweep, sweep_own, start, partial, far, near)
+        inner, first_ends = call(
+            inner_sweeps_kernel, [field, ((2, nodes, columns), wide, None)], [], sweep, sweep_own, start
+        )
+        (local,) = call(
+            outer_sweeps_kernel, [field], [], odd, sweep, sweep_own, start, inner, first_ends, far, near, *(kept or (far, near))
+        )
+        outs = [field, face, face, block, block]
+        given = (odd, coarse_rows, gathered, basis_columns, local)
         if kept:
-            (local,) = call(sweep_kernel, [field], [padded] * 2, *given, *kept)
+            update, near_face, far_face, near_block, far_block = call(update_kernel, outs, [], *given)
         else:
-            local, *kept = call(
-                keeping_sweep_kernel,
-                [field, edge, edge],
-                [padded, padded, pltpu.SemaphoreType.DMA((2,))],
-                *given,
+            update, near_face, far_face, near_block, far_block, *kept = call(
+                keeping_update_kernel, [*outs, edge, edge], [pltpu.SemaphoreType.DMA((2,))], *given, far, near
             )
-        update, near_face, far_face, near_block, far_block = call(
-            update_kernel, [field, face, face, block, block], [], odd, coarse_rows, gathered, basis_columns, local
-        )
         sections = lax.axis_size("sec")
         pairs = [[i, i + 1] for i in range(0, sections, 2)]
         faces_in = (

time: 123 us -> 121 us (0.984)
  blocking collectives: 42.3 us -> 40.8 us
    all_to_all x2, blocking collectives: 38.1 us -> 36.6 us  [total(): lax.all_to_all(spread, axes, 0, 0, axis_index_groups=groups, tiled=True)]
  transfers between devices with their start and end apart: 12 -> 12, of which waited for: 4 -> 4; matrix products, arithmetic and copies ran while one was open for 0% -> 0% of each run, Pallas kernels for 7% -> 8%
where the time goes in v5:
time: 121 us
  starting transfers between devices  53.3 us (44%)
  blocking collectives  40.8 us (34%)
  Pallas kernels  18.2 us (15%)
  waiting for transfers between devices  6.81 us (6%)
    all_to_all x2, blocking collectives, total(): lax.all_to_all(spread, axes, 0, 0, axis_index_groups=groups, tiled=True)  36.6 us
    all_to_all x2, starting transfers between devices, gather_sub(): lax.all_to_all(spread, 'sub', 0, 0, tiled=True)  20.5 us
    pallas_call x12, Pallas kernels, call(): pl.pallas_call(kernel, out_shape=[(space or jax.ShapeDtypeStruct)(shape,...  18.2 us
    ppermute x4, starting transfers between devices, swap(): return (lax.ppermute(to_near, axis, near), from_far)  15.4 us
    ppermute x2, starting transfers between devices, precondition(): lax.ppermute(far_face, 'sec', pairings('sec')[1])  14.8 us
    all_to_all x2, waiting for transfers between devices, gather_sub(): lax.all_to_all(spread, 'sub', 0, 0, tiled=True)  5.43 us
    all_gather x2, blocking collectives, precondition(): lax.all_gather(near_face, 'sec', axis_index_groups=pairs)  4.16 us
    ppermute x4, starting transfers between devices, swap(): from_far = lax.ppermute(to_far, axis, far)  2.65 us
  transfers between devices with their start and end apart: 12, of which 4 were waited for; matrix products, arithmetic and copies ran while one was open for 0% of the time, Pallas kernels for 8%

profile of v5, /device:TPU:1, one launch (start us, length us, event | category | flops | bytes accessed | tf_op | source)
XLA Modules:
  0.0 120.6 jit_solution(15032828369663194893)
XLA Ops:
  0.0 0.1 pad_add_fusion.odd
  0.1 3.2 %shard_map.64 = (f32[16,64,128]{2,1,0:T(8,128)}, f32[128,128]{1,0:T(8,128)S(1)}, f32[128,128]{1,0:T(8,128)S(1)}) custom-call(s32[2]{0:T(128)S(1)} %pad_add_fusion.odd, f32[64,768]{1,0:T(8,128)} %bitcast.69, f32[12,64,128]{2,1,0:T(8,128)} %bitcast.67, f32[12,64,128]{2,1,0:T(8,128)} %bitcast.55, f32[12,64,128]{2,1,0:T(8,128)} %bitcast.58), custom_call_target="tpu_custom_call" | custom-call | flops 1000 | bytes 1000 | tf_op jit(solution)/shard_map/pallas_call | solution.py:350
  3.3 0.0 copy-start.12
  3.3 10.4 %all-to-all-start = ((f32[16,64,128]{2,1,0:T(8,128)}), f32[16,64,128]{2,1,0:T(8,128)S(1)}, u32[]{:S(2)}, u32[]{:S(2)}) async-start(f32[16,64,128]{2,1,0:T(8,128)} %get-tuple-element.60), calls=%async_computation | async-start | bytes 1048576 | tf_op jit(solution)/shard_map/all_to_all | solution.py:32
  13.7 0.7 collective-permute-start
  14.4 5.7 %collective-permute-start.1 = (f32[128,128]{1,0:T(8,128)S(1)}, f32[128,128]{1,0:T(8,128)S(1)}, u32[]{:S(2)}, u32[]{:S(2)}) collective-permute-start(f32[128,128]{1,0:T(8,128)S(1)} %get-tuple-element.68), channel_id=1, source_target_pairs={{0,1},{1,0},{2,3},{3,2},{4,5},{5,4},{6,7},{7,6},{8,9},{9,8},{10,11... | collective-permute-start | bytes 196616 | tf_op jit(solution)/shard_map/ppermute | solution.py:28
  20.1 0.0 copy-done.12
  20.1 3.3 %shard_map.65 = (bf16[12,128,128]{2,1,0:T(8,128)(2,1)S(1)}, bf16[12,64,128]{2,1,0:T(8,128)(2,1)S(1)}, bf16[12,128,128]{2,1,0:T(8,128)(2,1)}, bf16[12,64,128]{2,1...) custom-call(f32[12,32]{1,0:T(8,128)S(1)} %bitcast.65, ...), custom_call_target="tpu_custom_call" | custom-call | flops 1000 | bytes 1000 | tf_op jit(solution)/shard_map/pallas_call | solution.py:350
  23.4 1.1 shard_map.66
  24.5 0.0 collective-permute-done.far.far_tile
  24.5 0.0 collective-permute-done.1.near.near_tile
  24.5 1.6 %shard_map.67.local = f32[12,64,128]{2,1,0:T(8,128)S(1)} custom-call(s32[2]{0:T(128)S(1)} %pad_add_fusion.odd, bf16[12,128,128]{2,1,0:T(8,128)(2,1)S(1)} %get-tuple-element.62.tiles, bf16[12,64,128]{2,1,0:T(8,128)(2,1)S(1)} %get-tuple-element.63.tiles_own, f32[12,64,128]{2,1,0:T(8,128)S(1)} %get-tuple-element.64.start, ...), custom_call_target="tpu_custom_call" | custom-call | flops 1000 | bytes 1000 | tf_op jit(solution)/shard_map/pallas_call | solution.py:350
  26.1 1.4 %all-to-all-done = f32[16,64,128]{2,1,0:T(8,128)S(1)} async-done(((f32[16,64,128]{2,1,0:T(8,128)}), f32[16,64,128]{2,1,0:T(8,128)S(1)}, u32[]{:S(2)}, u32[]{:S(2)}) %all-to-all-start) | async-done | bytes 524320 | tf_op jit(solution)/shard_map/all_to_all | solution.py:32
  27.5 1.2 shard_map.68
  28.7 10.4 %collective-permute-start.2 = (f32[12,16,128]{2,1,0:T(8,128)S(1)}, f32[12,16,128]{2,1,0:T(8,128)S(1)}, u32[]{:S(2)}, u32[]{:S(2)}) collective-permute-start(f32[12,16,128]{2,1,0:T(8,128)S(1)} %get-tuple-element.70), channel_id=1, source_target_pairs={{16,32},{48,64},{80,96},{112,128},{144,160},{176,192},{208,224},{2... | collective-permute-start | bytes 294920 | tf_op jit(solution)/shard_map/ppermute | solution.py:451
  39.1 2.0 %collective-permute-start.3 = (f32[64,128]{1,0:T(8,128)S(1)}, f32[64,128]{1,0:T(8,128)S(1)}, u32[]{:S(2)}, u32[]{:S(2)}) collective-permute-start(f32[64,128]{1,0:T(8,128)S(1)} %get-tuple-element.72), channel_id=1, source_target_pairs={{0,1},{1,0},{2,3},{3,2},{4,5},{5,4},{6,7},{7,6},{8,9},{9,8},{10,11... | collective-permute-start | bytes 98312 | tf_op jit(solution)/shard_map/ppermute | solution.py:28
  41.1 0.7 collective-permute-start.4
  41.8 0.0 copy-done.2
  41.8 0.0 copy-done.4
  41.8 0.0 copy-start
  41.8 0.0 copy-start.1
  41.8 0.0 copy-start.9
  41.8 0.5 shard_map.69.linear
  42.3 0.0 copy-start.3
  42.3 0.0 copy-start.7
  42.3 2.1 %all-gather = f32[24,16,128]{2,1,0:T(8,128)S(1)} all-gather(f32[12,16,128]{2,1,0:T(8,128)S(1)} %get-tuple-element.71), channel_id=2, replica_groups={{0,16},{32,48},{64,80},{96,112},{128,144},{160,176},{192,208},{224,240}..., dimensions={0}, use_global_device_ids=true | all-gather | bytes 294912 | tf_op jit(solution)/shard_map/all_gather | solution.py:450
  44.4 0.0 collective-permute-done.3.near_block
  44.4 0.0 collective-permute-done.4.far_block
  44.4 0.0 collective-permute-done.2.far_face
  44.4 0.0 copy-done
  44.4 0.0 copy-done.1
  44.5 0.0 copy-done.9
  44.5 0.0 copy-done.3
  44.5 0.0 copy-done.7
  44.5 2.2 %shard_map.70 = (f32[12,64,128]{2,1,0:T(8,128)}, f32[12,64,128]{2,1,0:T(8,128)}, f32[16,64,128]{2,1,0:T(8,128)}, f32[12,64,128]{2,1,0:T(8,128)S(1)}, f32[64,128]{1,0:T(8,128)}, /*index=5*/f32[64,128]{1,0:T(8,128)}) custom-call(s32[2]{0:T(128)S(1)} %pad_add_fusion.odd, bf16[2,128,128]{2,1,0:T(8,128)(2,1)S(1)} %copy-done.7, f32[12,32,128]{2,1,0:T(8,128)S(1)} %copy-done.3, ...), custom_call_target="tpu_custom_call" | custom-call | flops 1000 | bytes 1000 | tf_op jit(solution)/shard_map/pallas_call | solution.py:350
  46.7 0.0 copy-start.14
  46.7 0.0 copy-start.13
  46.7 10.1 %all-to-all-start.1 = ((f32[16,64,128]{2,1,0:T(8,128)}), f32[16,64,128]{2,1,0:T(8,128)S(1)}, u32[]{:S(2)}, u32[]{:S(2)}) async-start(f32[16,64,128]{2,1,0:T(8,128)} %get-tuple-element.76), calls=%async_computation.1 | async-start | bytes 1048576 | tf_op jit(solution)/shard_map/all_to_all | solution.py:32
  56.8 0.0 copy-done.14
  56.8 0.7 collective-permute-start.5
  57.5 0.0 copy-done.13
  57.5 5.7 %collective-permute-start.6 = (f32[64,128]{1,0:T(8,128)S(1)}, f32[64,128]{1,0:T(8,128)S(1)}, u32[]{:S(2)}, u32[]{:S(2)}) collective-permute-start(f32[64,128]{1,0:T(8,128)S(1)} %copy-done.13), channel_id=1, source_target_pairs={{0,1},{1,0},{2,3},{3,2},{4,5},{5,4},{6,7},{7,6},{8,9},{9,8},{10,11... | collective-permute-start | bytes 98312 | tf_op jit(solution)/shard_map/ppermute | solution.py:28
  63.2 1.1 shard_map.71
  64.3 0.0 collective-permute-done.5.far
  64.3 1.1 collective-permute-done.6.near
  65.5 0.0 copy-done.11
  65.5 1.6 %shard_map.72.local = f32[12,64,128]{2,1,0:T(8,128)S(1)} custom-call(s32[2]{0:T(128)S(1)} %pad_add_fusion.odd, bf16[12,128,128]{2,1,0:T(8,128)(2,1)S(1)} %get-tuple-element.62.tiles, bf16[12,64,128]{2,1,0:T(8,128)(2,1)S(1)} %get-tuple-element.63.tiles_own, f32[12,64,128]{2,1,0:T(8,128)S(1)} %get-tuple-element.77.start, ...), custom_call_target="tpu_custom_call" | custom-call | flops 1000 | bytes 1000 | tf_op jit(solution)/shard_map/pallas_call | solution.py:350
  67.1 4.1 %all-to-all-done.1 = f32[16,64,128]{2,1,0:T(8,128)S(1)} async-done(((f32[16,64,128]{2,1,0:T(8,128)}), f32[16,64,128]{2,1,0:T(8,128)S(1)}, u32[]{:S(2)}, u32[]{:S(2)}) %all-to-all-start.1) | async-done | bytes 524320 | tf_op jit(solution)/shard_map/all_to_all | solution.py:32
  71.1 1.1 shard_map.73
  72.3 4.3 %collective-permute-start.7 = (f32[12,16,128]{2,1,0:T(8,128)S(1)}, f32[12,16,128]{2,1,0:T(8,128)S(1)}, u32[]{:S(2)}, u32[]{:S(2)}) collective-permute-start(f32[12,16,128]{2,1,0:T(8,128)S(1)} %get-tuple-element.85), channel_id=1, source_target_pairs={{16,32},{48,64},{80,96},{112,128},{144,160},{176,192},{208,224},{2... | collective-permute-start | bytes 294920 | tf_op jit(solution)/shard_map/ppermute | solution.py:451
  76.6 0.0 copy-start.5
  76.6 0.5 shard_map.74.linear
  77.1 2.0 %collective-permute-start.8 = (f32[64,128]{1,0:T(8,128)S(1)}, f32[64,128]{1,0:T(8,128)S(1)}, u32[]{:S(2)}, u32[]{:S(2)}) collective-permute-start(f32[64,128]{1,0:T(8,128)S(1)} %get-tuple-element.87), channel_id=1, source_target_pairs={{0,1},{1,0},{2,3},{3,2},{4,5},{5,4},{6,7},{7,6},{8,9},{9,8},{10,11... | collective-permute-start | bytes 98312 | tf_op jit(solution)/shard_map/ppermute | solution.py:28
  79.1 0.7 collective-permute-start.9
  79.8 2.1 %all-gather.1 = f32[24,16,128]{2,1,0:T(8,128)S(1)} all-gather(f32[12,16,128]{2,1,0:T(8,128)S(1)} %get-tuple-element.86), channel_id=3, replica_groups={{0,16},{32,48},{64,80},{96,112},{128,144},{160,176},{192,208},{224,240}..., dimensions={0}, use_global_device_ids=true | all-gather | bytes 294912 | tf_op jit(solution)/shard_map/all_gather | solution.py:450
  81.9 0.0 collective-permute-done.8.near_block
  81.9 0.0 collective-permute-done.9.far_block
  81.9 0.2 collective-permute-done.7.far_face
  82.1 0.0 copy-done.6
  82.1 0.8 shard_map.75
  83.0 19.3 %all_to_all.20 = f32[16,1,640]{2,1,0:T(1,128)S(1)} all-to-all(f32[16,1,640]{2,1,0:T(1,128)S(1)} %broadcast_in_dim.9), channel_id=1, replica_groups={{0,16,64,80,128,144,192,208,256,272,320,336,384,400,448,464},{32,48,96,..., dimensions={0} | all-to-all | bytes 81920 | tf_op jit(solution)/shard_map/all_to_all | solution.py:47
  102.4 17.3 %all_to_all.21 = f32[32,1,640]{2,1,0:T(1,128)S(1)} all-to-all(f32[32,1,640]{2,1,0:T(1,128)S(1)} %broadcast_in_dim.20), channel_id=1, replica_groups={{0,1,2,3,4,5,6,7,8,9,10,11,12,13,14,15,32,33,34,35,36,37,38,39,40,41,42..., dimensions={0} | all-to-all | bytes 163840 | tf_op jit(solution)/shard_map/all_to_all | solution.py:47
  119.7 0.1 reduce_sum.21
  119.8 0.8 add_bitcast_fusion
  (16 shorter events, 0.2 us)
Async XLA Ops:
  3.3 16.8 %copy-start.12 = (f32[1,12,32]{2,0,1:T(1,128)S(1)}, f32[1,12,32]{2,0,1:T(1,128)}, u32[]{:S(2)}) copy-start(f32[1,12,32]{2,0,1:T(1,128)} %param.9) | copy-start | bytes 4612
  3.3 24.2 %all-to-all-start = ((f32[16,64,128]{2,1,0:T(8,128)}), f32[16,64,128]{2,1,0:T(8,128)S(1)}, u32[]{:S(2)}, u32[]{:S(2)}) async-start(f32[16,64,128]{2,1,0:T(8,128)} %get-tuple-element.60), calls=%async_computation | async-start | bytes 1048576 | tf_op jit(solution)/shard_map/all_to_all | solution.py:32
  13.7 10.8 %collective-permute-start = (f32[128,128]{1,0:T(8,128)S(1)}, f32[128,128]{1,0:T(8,128)S(1)}, u32[]{:S(2)}, u32[]{:S(2)}) collective-permute-start(f32[128,128]{1,0:T(8,128)S(1)} %get-tuple-element.67), channel_id=1, source_target_pairs={{1,2},{3,4},{5,6},{7,8},{9,10},{11,12},{13,14},{2,1},{4,3},{6,5},{... | collective-permute-start | bytes 196616 | tf_op jit(solution)/shard_map/ppermute | solution.py:27
  14.4 10.1 %collective-permute-start.1 = (f32[128,128]{1,0:T(8,128)S(1)}, f32[128,128]{1,0:T(8,128)S(1)}, u32[]{:S(2)}, u32[]{:S(2)}) collective-permute-start(f32[128,128]{1,0:T(8,128)S(1)} %get-tuple-element.68), channel_id=1, source_target_pairs={{0,1},{1,0},{2,3},{3,2},{4,5},{5,4},{6,7},{7,6},{8,9},{9,8},{10,11... | collective-permute-start | bytes 196616 | tf_op jit(solution)/shard_map/ppermute | solution.py:28
  27.5 14.3 %copy-start.2 = (bf16[12,128,128]{2,1,0:T(8,128)(2,1)S(1)}, bf16[12,128,128]{2,1,0:T(8,128)(2,1)}, u32[]{:S(2)}) copy-start(bf16[12,128,128]{2,1,0:T(8,128)(2,1)} %get-tuple-element.57.tiles) | copy-start | bytes 1179652
  27.5 14.3 %copy-start.4 = (bf16[12,64,128]{2,1,0:T(8,128)(2,1)S(1)}, bf16[12,64,128]{2,1,0:T(8,128)(2,1)}, u32[]{:S(2)}) copy-start(bf16[12,64,128]{2,1,0:T(8,128)(2,1)} %get-tuple-element.58.tiles_own) | copy-start | bytes 589828
  28.7 15.8 %collective-permute-start.2 = (f32[12,16,128]{2,1,0:T(8,128)S(1)}, f32[12,16,128]{2,1,0:T(8,128)S(1)}, u32[]{:S(2)}, u32[]{:S(2)}) collective-permute-start(f32[12,16,128]{2,1,0:T(8,128)S(1)} %get-tuple-element.70), channel_id=1, source_target_pairs={{16,32},{48,64},{80,96},{112,128},{144,160},{176,192},{208,224},{2... | collective-permute-start | bytes 294920 | tf_op jit(solution)/shard_map/ppermute | solution.py:451
  39.1 5.3 %collective-permute-start.3 = (f32[64,128]{1,0:T(8,128)S(1)}, f32[64,128]{1,0:T(8,128)S(1)}, u32[]{:S(2)}, u32[]{:S(2)}) collective-permute-start(f32[64,128]{1,0:T(8,128)S(1)} %get-tuple-element.72), channel_id=1, source_target_pairs={{0,1},{1,0},{2,3},{3,2},{4,5},{5,4},{6,7},{7,6},{8,9},{9,8},{10,11... | collective-permute-start | bytes 98312 | tf_op jit(solution)/shard_map/ppermute | solution.py:28
  41.1 3.3 %collective-permute-start.4 = (f32[64,128]{1,0:T(8,128)S(1)}, f32[64,128]{1,0:T(8,128)S(1)}, u32[]{:S(2)}, u32[]{:S(2)}) collective-permute-start(f32[64,128]{1,0:T(8,128)S(1)} %get-tuple-element.73), channel_id=1, source_target_pairs={{1,2},{3,4},{5,6},{7,8},{9,10},{11,12},{13,14},{2,1},{4,3},{6,5},{... | collective-permute-start | bytes 98312 | tf_op jit(solution)/shard_map/ppermute | solution.py:27
  41.8 2.6 %copy-start = (f32[1,12,64,128]{3,2,1,0:T(8,128)S(1)}, f32[1,12,64,128]{3,2,1,0:T(8,128)}, u32[]{:S(2)}) copy-start(f32[1,12,64,128]{3,2,1,0:T(8,128)} %param.8) | copy-start | bytes 1179652
  41.8 2.6 %copy-start.1 = (f32[1,12,64,128]{3,2,1,0:T(8,128)S(1)}, f32[1,12,64,128]{3,2,1,0:T(8,128)}, u32[]{:S(2)}) copy-start(f32[1,12,64,128]{3,2,1,0:T(8,128)} %param.6) | copy-start | bytes 1179652
  41.8 2.6 %copy-start.9 = (bf16[128,768]{1,0:T(8,128)(2,1)S(1)}, bf16[128,768]{1,0:T(8,128)(2,1)}, u32[]{:S(2)}) copy-start(bf16[128,768]{1,0:T(8,128)(2,1)} %get-tuple-element.56.basis_rows) | copy-start | bytes 589828
  42.3 2.1 %copy-start.3 = (f32[12,32,128]{2,1,0:T(8,128)S(1)}, f32[12,32,128]{2,1,0:T(8,128)}, u32[]{:S(2)}) copy-start(f32[12,32,128]{2,1,0:T(8,128)} %get-tuple-element.55.sides) | copy-start | bytes 589828
  42.3 2.1 %copy-start.7 = (bf16[2,128,128]{2,1,0:T(8,128)(2,1)S(1)}, bf16[2,128,128]{2,1,0:T(8,128)(2,1)}, u32[]{:S(2)}) copy-start(bf16[2,128,128]{2,1,0:T(8,128)(2,1)} %get-tuple-element.54.edge_tiles) | copy-start | bytes 196612
  46.7 10.1 %copy-start.14 = (f32[64,128]{1,0:T(8,128)S(1)}, f32[64,128]{1,0:T(8,128)}, u32[]{:S(2)}) copy-start(f32[64,128]{1,0:T(8,128)} %get-tuple-element.80) | copy-start | bytes 98308
  46.7 10.8 %copy-start.13 = (f32[64,128]{1,0:T(8,128)S(1)}, f32[64,128]{1,0:T(8,128)}, u32[]{:S(2)}) copy-start(f32[64,128]{1,0:T(8,128)} %get-tuple-element.81) | copy-start | bytes 98308
  46.7 24.4 %all-to-all-start.1 = ((f32[16,64,128]{2,1,0:T(8,128)}), f32[16,64,128]{2,1,0:T(8,128)S(1)}, u32[]{:S(2)}, u32[]{:S(2)}) async-start(f32[16,64,128]{2,1,0:T(8,128)} %get-tuple-element.76), calls=%async_computation.1 | async-start | bytes 1048576 | tf_op jit(solution)/shard_map/all_to_all | solution.py:32
  56.8 7.5 %collective-permute-start.5 = (f32[64,128]{1,0:T(8,128)S(1)}, f32[64,128]{1,0:T(8,128)S(1)}, u32[]{:S(2)}, u32[]{:S(2)}) collective-permute-start(f32[64,128]{1,0:T(8,128)S(1)} %copy-done.14), channel_id=1, source_target_pairs={{1,2},{3,4},{5,6},{7,8},{9,10},{11,12},{13,14},{2,1},{4,3},{6,5},{... | collective-permute-start | bytes 98312 | tf_op jit(solution)/shard_map/ppermute | solution.py:27
  57.5 8.0 %collective-permute-start.6 = (f32[64,128]{1,0:T(8,128)S(1)}, f32[64,128]{1,0:T(8,128)S(1)}, u32[]{:S(2)}, u32[]{:S(2)}) collective-permute-start(f32[64,128]{1,0:T(8,128)S(1)} %copy-done.13), channel_id=1, source_target_pairs={{0,1},{1,0},{2,3},{3,2},{4,5},{5,4},{6,7},{7,6},{8,9},{9,8},{10,11... | collective-permute-start | bytes 98312 | tf_op jit(solution)/shard_map/ppermute | solution.py:28
  63.2 2.3 %copy-start.10 = (f32[64,128]{1,0:T(8,128)S(1)}, f32[64,128]{1,0:T(8,128)}, u32[]{:S(2)}) copy-start(f32[64,128]{1,0:T(8,128)} %get-tuple-element.82.far_tile) | copy-start | bytes 98308
  63.2 2.3 %copy-start.11 = (f32[64,128]{1,0:T(8,128)S(1)}, f32[64,128]{1,0:T(8,128)}, u32[]{:S(2)}) copy-start(f32[64,128]{1,0:T(8,128)} %get-tuple-element.83.near_tile) | copy-start | bytes 98308
  72.3 9.8 %collective-permute-start.7 = (f32[12,16,128]{2,1,0:T(8,128)S(1)}, f32[12,16,128]{2,1,0:T(8,128)S(1)}, u32[]{:S(2)}, u32[]{:S(2)}) collective-permute-start(f32[12,16,128]{2,1,0:T(8,128)S(1)} %get-tuple-element.85), channel_id=1, source_target_pairs={{16,32},{48,64},{80,96},{112,128},{144,160},{176,192},{208,224},{2... | collective-permute-start | bytes 294920 | tf_op jit(solution)/shard_map/ppermute | solution.py:451
  76.6 5.5 %copy-start.5 = (f32[12,64,128]{2,1,0:T(8,128)S(1)}, f32[12,64,128]{2,1,0:T(8,128)}, u32[]{:S(2)}) copy-start(f32[12,64,128]{2,1,0:T(8,128)} %get-tuple-element.74.image) | copy-start | bytes 1179652
  76.6 5.5 %copy-start.6 = (f32[12,64,128]{2,1,0:T(8,128)S(1)}, f32[12,64,128]{2,1,0:T(8,128)}, u32[]{:S(2)}) copy-start(f32[12,64,128]{2,1,0:T(8,128)} %get-tuple-element.75.rest) | copy-start | bytes 1179652
  77.1 4.8 %collective-permute-start.8 = (f32[64,128]{1,0:T(8,128)S(1)}, f32[64,128]{1,0:T(8,128)S(1)}, u32[]{:S(2)}, u32[]{:S(2)}) collective-permute-start(f32[64,128]{1,0:T(8,128)S(1)} %get-tuple-element.87), channel_id=1, source_target_pairs={{0,1},{1,0},{2,3},{3,2},{4,5},{5,4},{6,7},{7,6},{8,9},{9,8},{10,11... | collective-permute-start | bytes 98312 | tf_op jit(solution)/shard_map/ppermute | solution.py:28
  79.1 2.8 %collective-permute-start.9 = (f32[64,128]{1,0:T(8,128)S(1)}, f32[64,128]{1,0:T(8,128)S(1)}, u32[]{:S(2)}, u32[]{:S(2)}) collective-permute-start(f32[64,128]{1,0:T(8,128)S(1)} %get-tuple-element.88), channel_id=1, source_target_pairs={{1,2},{3,4},{5,6},{7,8},{9,10},{11,12},{13,14},{2,1},{4,3},{6,5},{... | collective-permute-start | bytes 98312 | tf_op jit(solution)/shard_map/ppermute | solution.py:27
  79.8 2.3 %copy-start.8 = (bf16[2,128,128]{2,1,0:T(8,128)(2,1)S(1)}, bf16[2,128,128]{2,1,0:T(8,128)(2,1)}, u32[]{:S(2)}) copy-start(bf16[2,128,128]{2,1,0:T(8,128)(2,1)} %get-tuple-element.54.edge_tiles) | copy-start | bytes 196612

commit v6 on v5

--- a/solution.py
+++ b/solution.py
@@ -99,6 +99,29 @@
     for load in loads:
         load.start()
     return loads
+
+
+def edge_kernel(odd, coupling_in, pair_in, residual_in, near, far, coupling, pair, residual, sems):
+    blocks, nodes = pair_in.shape[:2]
+    loads = start_all(
+        [
+            (source.at[b], target.at[i])
+            for source, target in ((pair_in, pair), (coupling_in, coupling), (residual_in, residual))
+            for i, b in enumerate((0, blocks - 1))
+        ],
+        sems,
+    )
+    for load in loads:
+        load.wait()
+    even = odd[1] == 0
+    start, beside, own = block_sweep(pair[0], coupling[0], residual[0])
+    last, beyond, own_last = block_sweep(pair[1], coupling[1], residual[1])
+    to_previous = jnp.concatenate([beside[:, :nodes], own], axis=1)
+    to_next = jnp.concatenate([beyond[:, nodes:], own_last], axis=1)
+    near[:nodes] = jnp.where(even, last, start)
+    far[:nodes] = jnp.where(even, start, last)
+    near[nodes:] = jnp.where(even, to_next, to_previous)
+    far[nodes:] = jnp.where(even, to_previous, to_next)
 
 
 def prepare_kernel(side, coupling_in, pair_in, residual_in, basis_in, inverse_in, sweep, sweep_own, tiles_out, tiles_own_out, edge_tiles_out, start, sides_out, basis_rows_out, basis_columns, coarse_rows, coupling, pair, residual, basis, inverse_rows, tiles, tiles_own, sides, basis_rows, sems, stores):
@@ -292,29 +315,9 @@
         copy.wait()
 
 
-def first_kernel(odd, basis_in, coupling_in, pair_in, field_in, spread, near, far, basis, field, coupling, pair, residual, projected, sems, arrived, edges_arrived):
+def project_kernel(basis_in, field_in, spread, basis, field, projected, sems, arrived):
     blocks, nodes, columns = field.shape
-    edge_loads = start_all(
-        [
-            (source.at[b], target.at[i])
-            for source, target in ((pair_in, pair), (coupling_in, coupling), (field_in, residual))
-            for i, b in enumerate((0, blocks - 1))
-        ],
-        edges_arrived,
-    )
-    loads = start_all([(basis_in, basis), (field_in, field)], arrived)
-    for load in edge_loads:
-        load.wait()
-    even = odd[1] == 0
-    start, beside, own = block_sweep(pair[0], coupling[0], residual[0])
-    last, beyond, own_last = block_sweep(pair[1], coupling[1], residual[1])
-    to_previous = jnp.concatenate([beside[:, :nodes], own], axis=1)
-    to_next = jnp.concatenate([beyond[:, nodes:], own_last], axis=1)
-    near[:nodes] = jnp.where(even, last, start)
-    far[:nodes] = jnp.where(even, start, last)
-    near[nodes:] = jnp.where(even, to_next, to_previous)
-    far[nodes:] = jnp.where(even, to_previous, to_next)
-    for load in loads:
+    for load in start_all([(basis_in, basis), (field_in, field)], arrived):
         load.wait()
     projected[...] = dot(basis[...], field[...].reshape(blocks * nodes, columns))
     for copy in send_out(projected, spread, sems):
@@ -378,24 +381,29 @@
     spread_out = ((subs, own_coarse, columns), wide, pltpu.HBM)
     spreading = [pltpu.VMEM((own_coarse, columns), wide), pltpu.SemaphoreType.DMA((subs,))]
 
-    spread, near, far = call(
-        first_kernel,
-        [spread_out, small, small],
+    (spread,) = call(
+        project_kernel,
+        [spread_out],
         [
             pltpu.VMEM(basis_all.shape, wide),
             pltpu.VMEM((blocks, nodes, columns), wide),
-            *[pltpu.VMEM((2, nodes, columns), wide)] * 3,
             *spreading,
             pltpu.SemaphoreType.DMA((2,)),
-            pltpu.SemaphoreType.DMA((6,)),
-        ],
-        odd, basis_all, coupling[0], diag_pair[0], residual,
-        slow=4,
+        ],
+        basis_all, residual,
+        slow=2,
     )
     spread, odd, residual, coupling, diag_pair, side, basis_all = lax.optimization_barrier(
         (spread, odd, residual, coupling, diag_pair, side, basis_all)
     )
     pair = diag_pair[0]
+    near, far = call(
+        edge_kernel,
+        [small, small],
+        [pltpu.VMEM((2, nodes, columns), wide)] * 3 + [pltpu.SemaphoreType.DMA((6,))],
+        odd, coupling[0], pair, residual,
+        slow=3,
+    )
     halo = swap(near, far, "sub")
     sweep, sweep_own, tiles, tiles_own, edge_tiles, start, sides, basis_rows, basis_columns, coarse_rows = call(
         prepare_kernel,

time: 121 us -> 121 us (level)
  waiting for transfers between devices: 6.81 us -> 5.39 us
    all_to_all x2, waiting for transfers between devices: 5.43 us -> 4.06 us  [gather_sub(): lax.all_to_all(spread, 'sub', 0, 0, tiled=True)]
    pallas_call x12 -> x13, Pallas kernels: 18.2 us -> 19.2 us  [call(): pl.pallas_call(kernel, out_shape=[(space or jax.ShapeDtypeStruct)(shape,...]
  transfers between devices with their start and end apart: 12 -> 12, of which waited for: 4 -> 3; matrix products, arithmetic and copies ran while one was open for 0% -> 0% of each run, Pallas kernels for 8% -> 10%
where the time goes in v6:
time: 121 us; the launch traced here: 120 us
  starting transfers between devices  52.9 us (44%)
  blocking collectives  40.8 us (34%)
  Pallas kernels  19.2 us (16%)
  waiting for transfers between devices  5.39 us (4%)
    all_to_all x2, blocking collectives, total(): lax.all_to_all(spread, axes, 0, 0, axis_index_groups=groups, tiled=True)  36.6 us
    all_to_all x2, starting transfers between devices, gather_sub(): lax.all_to_all(spread, 'sub', 0, 0, tiled=True)  20.5 us
    pallas_call x13, Pallas kernels, call(): pl.pallas_call(kernel, out_shape=[(space or jax.ShapeDtypeStruct)(shape,...  19.2 us
    ppermute x4, starting transfers between devices, swap(): return (lax.ppermute(to_near, axis, near), from_far)  15.4 us
    ppermute x2, starting transfers between devices, precondition(): lax.ppermute(far_face, 'sec', pairings('sec')[1])  14.3 us
    all_gather x2, blocking collectives, precondition(): lax.all_gather(near_face, 'sec', axis_index_groups=pairs)  4.16 us
    all_to_all x2, waiting for transfers between devices, gather_sub(): lax.all_to_all(spread, 'sub', 0, 0, tiled=True)  4.06 us
    ppermute x4, starting transfers between devices, swap(): from_far = lax.ppermute(to_far, axis, far)  2.65 us
  transfers between devices with their start and end apart: 12, of which 3 were waited for; matrix products, arithmetic and copies ran while one was open for 0% of the time, Pallas kernels for 10%

profile of v6, /device:TPU:1, one launch (start us, length us, event | category | flops | bytes accessed | tf_op | source)
XLA Modules:
  0.0 119.8 jit_solution(5133159750069855457)
XLA Ops:
  0.0 0.1 pad_add_fusion.odd
  0.1 2.4 %shard_map.64 = f32[16,64,128]{2,1,0:T(8,128)} custom-call(f32[64,768]{1,0:T(8,128)} %bitcast.68, f32[12,64,128]{2,1,0:T(8,128)} %bitcast.53), custom_call_target="tpu_custom_call" | custom-call | flops 1000 | bytes 1000 | tf_op jit(solution)/shard_map/pallas_call | solution.py:353
  2.5 10.4 %all-to-all-start = ((f32[16,64,128]{2,1,0:T(8,128)}), f32[16,64,128]{2,1,0:T(8,128)S(1)}, u32[]{:S(2)}, u32[]{:S(2)}) async-start(f32[16,64,128]{2,1,0:T(8,128)} %shard_map.64), calls=%async_computation | async-start | bytes 1048576 | tf_op jit(solution)/shard_map/all_to_all | solution.py:32
  12.9 0.0 copy-start.12
  12.9 1.8 %shard_map.67 = (f32[128,128]{1,0:T(8,128)S(1)}, f32[128,128]{1,0:T(8,128)S(1)}) custom-call(s32[2]{0:T(128)S(1)} %pad_add_fusion.odd, f32[12,64,128]{2,1,0:T(8,128)} %bitcast.66, f32[12,64,128]{2,1,0:T(8,128)} %bitcast.57, f32[12,64,128]{2,1,0:T(8,128)} %bitcast.54), custom_call_target="tpu_custom_call" | custom-call | flops 1000 | bytes 1000 | tf_op jit(solution)/shard_map/pallas_call | solution.py:353
  14.7 0.7 collective-permute-start
  15.4 5.7 %collective-permute-start.1 = (f32[128,128]{1,0:T(8,128)S(1)}, f32[128,128]{1,0:T(8,128)S(1)}, u32[]{:S(2)}, u32[]{:S(2)}) collective-permute-start(f32[128,128]{1,0:T(8,128)S(1)} %get-tuple-element.66), channel_id=1, source_target_pairs={{0,1},{1,0},{2,3},{3,2},{4,5},{5,4},{6,7},{7,6},{8,9},{9,8},{10,11... | collective-permute-start | bytes 196616 | tf_op jit(solution)/shard_map/ppermute | solution.py:28
  21.1 0.0 copy-done.12
  21.1 3.3 %shard_map.65 = (bf16[12,128,128]{2,1,0:T(8,128)(2,1)S(1)}, bf16[12,64,128]{2,1,0:T(8,128)(2,1)S(1)}, bf16[12,128,128]{2,1,0:T(8,128)(2,1)}, bf16[12,64,128]{2,1...) custom-call(f32[12,32]{1,0:T(8,128)S(1)} %bitcast.64, ...), custom_call_target="tpu_custom_call" | custom-call | flops 1000 | bytes 1000 | tf_op jit(solution)/shard_map/pallas_call | solution.py:353
  24.4 1.1 shard_map.66
  25.5 0.0 collective-permute-done.far.far_tile
  25.5 0.0 collective-permute-done.1.near.near_tile
  25.5 1.6 %shard_map.68.local = f32[12,64,128]{2,1,0:T(8,128)S(1)} custom-call(s32[2]{0:T(128)S(1)} %pad_add_fusion.odd, bf16[12,128,128]{2,1,0:T(8,128)(2,1)S(1)} %get-tuple-element.60.tiles, bf16[12,64,128]{2,1,0:T(8,128)(2,1)S(1)} %get-tuple-element.61.tiles_own, f32[12,64,128]{2,1,0:T(8,128)S(1)} %get-tuple-element.62.start, ...), custom_call_target="tpu_custom_call" | custom-call | flops 1000 | bytes 1000 | tf_op jit(solution)/shard_map/pallas_call | solution.py:353
  27.1 0.0 all-to-all-done
  27.1 0.0 copy-start.2
  27.2 0.0 copy-start.4
  27.2 1.2 shard_map.69
  28.3 9.9 %collective-permute-start.2 = (f32[12,16,128]{2,1,0:T(8,128)S(1)}, f32[12,16,128]{2,1,0:T(8,128)S(1)}, u32[]{:S(2)}, u32[]{:S(2)}) collective-permute-start(f32[12,16,128]{2,1,0:T(8,128)S(1)} %get-tuple-element.68), channel_id=1, source_target_pairs={{16,32},{48,64},{80,96},{112,128},{144,160},{176,192},{208,224},{2... | collective-permute-start | bytes 294920 | tf_op jit(solution)/shard_map/ppermute | solution.py:459
  38.3 2.0 %collective-permute-start.3 = (f32[64,128]{1,0:T(8,128)S(1)}, f32[64,128]{1,0:T(8,128)S(1)}, u32[]{:S(2)}, u32[]{:S(2)}) collective-permute-start(f32[64,128]{1,0:T(8,128)S(1)} %get-tuple-element.70), channel_id=1, source_target_pairs={{0,1},{1,0},{2,3},{3,2},{4,5},{5,4},{6,7},{7,6},{8,9},{9,8},{10,11... | collective-permute-start | bytes 98312 | tf_op jit(solution)/shard_map/ppermute | solution.py:28
  40.3 0.7 collective-permute-start.4
  41.0 0.0 copy-done.2
  41.0 0.0 copy-done.4
  41.0 0.0 copy-start
  41.0 0.0 copy-start.1
  41.0 0.0 copy-start.9
  41.0 0.5 shard_map.70.linear
  41.5 0.0 copy-start.3
  41.5 0.0 copy-start.7
  41.5 2.1 %all-gather = f32[24,16,128]{2,1,0:T(8,128)S(1)} all-gather(f32[12,16,128]{2,1,0:T(8,128)S(1)} %get-tuple-element.69), channel_id=2, replica_groups={{0,16},{32,48},{64,80},{96,112},{128,144},{160,176},{192,208},{224,240}..., dimensions={0}, use_global_device_ids=true | all-gather | bytes 294912 | tf_op jit(solution)/shard_map/all_gather | solution.py:458
  43.6 0.0 collective-permute-done.3.near_block
  43.6 0.0 collective-permute-done.4.far_block
  43.6 0.0 collective-permute-done.2.far_face
  43.6 0.0 copy-done
  43.6 0.0 copy-done.1
  43.6 0.0 copy-done.9
  43.6 0.0 copy-done.3
  43.7 0.0 copy-done.7
  43.7 2.2 %shard_map.71 = (f32[12,64,128]{2,1,0:T(8,128)}, f32[12,64,128]{2,1,0:T(8,128)}, f32[16,64,128]{2,1,0:T(8,128)}, f32[12,64,128]{2,1,0:T(8,128)S(1)}, f32[64,128]{1,0:T(8,128)}, /*index=5*/f32[64,128]{1,0:T(8,128)}) custom-call(s32[2]{0:T(128)S(1)} %pad_add_fusion.odd, bf16[2,128,128]{2,1,0:T(8,128)(2,1)S(1)} %copy-done.7, f32[12,32,128]{2,1,0:T(8,128)S(1)} %copy-done.3, ...), custom_call_target="tpu_custom_call" | custom-call | flops 1000 | bytes 1000 | tf_op jit(solution)/shard_map/pallas_call | solution.py:353
  45.9 10.1 %all-to-all-start.1 = ((f32[16,64,128]{2,1,0:T(8,128)}), f32[16,64,128]{2,1,0:T(8,128)S(1)}, u32[]{:S(2)}, u32[]{:S(2)}) async-start(f32[16,64,128]{2,1,0:T(8,128)} %get-tuple-element.74), calls=%async_computation.1 | async-start | bytes 1048576 | tf_op jit(solution)/shard_map/all_to_all | solution.py:32
  56.0 0.7 collective-permute-start.5
  56.7 5.7 %collective-permute-start.6 = (f32[64,128]{1,0:T(8,128)S(1)}, f32[64,128]{1,0:T(8,128)S(1)}, u32[]{:S(2)}, u32[]{:S(2)}) collective-permute-start(f32[64,128]{1,0:T(8,128)S(1)} %copy-done.13), channel_id=1, source_target_pairs={{0,1},{1,0},{2,3},{3,2},{4,5},{5,4},{6,7},{7,6},{8,9},{9,8},{10,11... | collective-permute-start | bytes 98312 | tf_op jit(solution)/shard_map/ppermute | solution.py:28
  62.4 1.1 shard_map.72
  63.5 0.0 collective-permute-done.5.far
  63.5 1.1 collective-permute-done.6.near
  64.7 0.0 copy-done.10
  64.7 1.6 %shard_map.73.local = f32[12,64,128]{2,1,0:T(8,128)S(1)} custom-call(s32[2]{0:T(128)S(1)} %pad_add_fusion.odd, bf16[12,128,128]{2,1,0:T(8,128)(2,1)S(1)} %get-tuple-element.60.tiles, bf16[12,64,128]{2,1,0:T(8,128)(2,1)S(1)} %get-tuple-element.61.tiles_own, f32[12,64,128]{2,1,0:T(8,128)S(1)} %get-tuple-element.75.start, ...), custom_call_target="tpu_custom_call" | custom-call | flops 1000 | bytes 1000 | tf_op jit(solution)/shard_map/pallas_call | solution.py:353
  66.3 4.1 %all-to-all-done.1 = f32[16,64,128]{2,1,0:T(8,128)S(1)} async-done(((f32[16,64,128]{2,1,0:T(8,128)}), f32[16,64,128]{2,1,0:T(8,128)S(1)}, u32[]{:S(2)}, u32[]{:S(2)}) %all-to-all-start.1) | async-done | bytes 524320 | tf_op jit(solution)/shard_map/all_to_all | solution.py:32
  70.3 1.1 shard_map.74
  71.5 4.4 %collective-permute-start.7 = (f32[12,16,128]{2,1,0:T(8,128)S(1)}, f32[12,16,128]{2,1,0:T(8,128)S(1)}, u32[]{:S(2)}, u32[]{:S(2)}) collective-permute-start(f32[12,16,128]{2,1,0:T(8,128)S(1)} %get-tuple-element.83), channel_id=1, source_target_pairs={{16,32},{48,64},{80,96},{112,128},{144,160},{176,192},{208,224},{2... | collective-permute-start | bytes 294920 | tf_op jit(solution)/shard_map/ppermute | solution.py:459
  75.9 0.0 copy-start.5
  75.9 0.5 shard_map.75.linear
  76.3 2.0 %collective-permute-start.8 = (f32[64,128]{1,0:T(8,128)S(1)}, f32[64,128]{1,0:T(8,128)S(1)}, u32[]{:S(2)}, u32[]{:S(2)}) collective-permute-start(f32[64,128]{1,0:T(8,128)S(1)} %get-tuple-element.85), channel_id=1, source_target_pairs={{0,1},{1,0},{2,3},{3,2},{4,5},{5,4},{6,7},{7,6},{8,9},{9,8},{10,11... | collective-permute-start | bytes 98312 | tf_op jit(solution)/shard_map/ppermute | solution.py:28
  78.4 0.7 collective-permute-start.9
  79.1 2.1 %all-gather.1 = f32[24,16,128]{2,1,0:T(8,128)S(1)} all-gather(f32[12,16,128]{2,1,0:T(8,128)S(1)} %get-tuple-element.84), channel_id=3, replica_groups={{0,16},{32,48},{64,80},{96,112},{128,144},{160,176},{192,208},{224,240}..., dimensions={0}, use_global_device_ids=true | all-gather | bytes 294912 | tf_op jit(solution)/shard_map/all_gather | solution.py:458
  81.1 0.0 collective-permute-done.8.near_block
  81.1 0.0 collective-permute-done.9.far_block
  81.1 0.2 collective-permute-done.7.far_face
  81.3 0.0 copy-done.5
  81.3 0.0 copy-done.8
  81.3 0.8 shard_map.76
  82.2 19.2 %all_to_all.20 = f32[16,1,640]{2,1,0:T(1,128)S(1)} all-to-all(f32[16,1,640]{2,1,0:T(1,128)S(1)} %broadcast_in_dim.9), channel_id=1, replica_groups={{0,16,64,80,128,144,192,208,256,272,320,336,384,400,448,464},{32,48,96,..., dimensions={0} | all-to-all | bytes 81920 | tf_op jit(solution)/shard_map/all_to_all | solution.py:47
  101.5 17.4 %all_to_all.21 = f32[32,1,640]{2,1,0:T(1,128)S(1)} all-to-all(f32[32,1,640]{2,1,0:T(1,128)S(1)} %broadcast_in_dim.20), channel_id=1, replica_groups={{0,1,2,3,4,5,6,7,8,9,10,11,12,13,14,15,32,33,34,35,36,37,38,39,40,41,42..., dimensions={0} | all-to-all | bytes 163840 | tf_op jit(solution)/shard_map/all_to_all | solution.py:47
  118.9 0.1 reduce_sum.21
  119.0 0.8 add_bitcast_fusion
  (17 shorter events, 0.2 us)
Async XLA Ops:
  2.5 24.7 %all-to-all-start = ((f32[16,64,128]{2,1,0:T(8,128)}), f32[16,64,128]{2,1,0:T(8,128)S(1)}, u32[]{:S(2)}, u32[]{:S(2)}) async-start(f32[16,64,128]{2,1,0:T(8,128)} %shard_map.64), calls=%async_computation | async-start | bytes 1048576 | tf_op jit(solution)/shard_map/all_to_all | solution.py:32
  12.9 8.2 %copy-start.12 = (f32[1,12,32]{2,0,1:T(1,128)S(1)}, f32[1,12,32]{2,0,1:T(1,128)}, u32[]{:S(2)}) copy-start(f32[1,12,32]{2,0,1:T(1,128)} %param.9) | copy-start | bytes 4612
  14.7 10.8 %collective-permute-start = (f32[128,128]{1,0:T(8,128)S(1)}, f32[128,128]{1,0:T(8,128)S(1)}, u32[]{:S(2)}, u32[]{:S(2)}) collective-permute-start(f32[128,128]{1,0:T(8,128)S(1)} %get-tuple-element.65), channel_id=1, source_target_pairs={{1,2},{3,4},{5,6},{7,8},{9,10},{11,12},{13,14},{2,1},{4,3},{6,5},{... | collective-permute-start | bytes 196616 | tf_op jit(solution)/shard_map/ppermute | solution.py:27
  15.4 10.1 %collective-permute-start.1 = (f32[128,128]{1,0:T(8,128)S(1)}, f32[128,128]{1,0:T(8,128)S(1)}, u32[]{:S(2)}, u32[]{:S(2)}) collective-permute-start(f32[128,128]{1,0:T(8,128)S(1)} %get-tuple-element.66), channel_id=1, source_target_pairs={{0,1},{1,0},{2,3},{3,2},{4,5},{5,4},{6,7},{7,6},{8,9},{9,8},{10,11... | collective-permute-start | bytes 196616 | tf_op jit(solution)/shard_map/ppermute | solution.py:28
  27.1 13.8 %copy-start.2 = (bf16[12,128,128]{2,1,0:T(8,128)(2,1)S(1)}, bf16[12,128,128]{2,1,0:T(8,128)(2,1)}, u32[]{:S(2)}) copy-start(bf16[12,128,128]{2,1,0:T(8,128)(2,1)} %get-tuple-element.55.tiles) | copy-start | bytes 1179652
  27.2 13.8 %copy-start.4 = (bf16[12,64,128]{2,1,0:T(8,128)(2,1)S(1)}, bf16[12,64,128]{2,1,0:T(8,128)(2,1)}, u32[]{:S(2)}) copy-start(bf16[12,64,128]{2,1,0:T(8,128)(2,1)} %get-tuple-element.56.tiles_own) | copy-start | bytes 589828
  28.3 15.3 %collective-permute-start.2 = (f32[12,16,128]{2,1,0:T(8,128)S(1)}, f32[12,16,128]{2,1,0:T(8,128)S(1)}, u32[]{:S(2)}, u32[]{:S(2)}) collective-permute-start(f32[12,16,128]{2,1,0:T(8,128)S(1)} %get-tuple-element.68), channel_id=1, source_target_pairs={{16,32},{48,64},{80,96},{112,128},{144,160},{176,192},{208,224},{2... | collective-permute-start | bytes 294920 | tf_op jit(solution)/shard_map/ppermute | solution.py:459
  38.3 5.3 %collective-permute-start.3 = (f32[64,128]{1,0:T(8,128)S(1)}, f32[64,128]{1,0:T(8,128)S(1)}, u32[]{:S(2)}, u32[]{:S(2)}) collective-permute-start(f32[64,128]{1,0:T(8,128)S(1)} %get-tuple-element.70), channel_id=1, source_target_pairs={{0,1},{1,0},{2,3},{3,2},{4,5},{5,4},{6,7},{7,6},{8,9},{9,8},{10,11... | collective-permute-start | bytes 98312 | tf_op jit(solution)/shard_map/ppermute | solution.py:28
  40.3 3.3 %collective-permute-start.4 = (f32[64,128]{1,0:T(8,128)S(1)}, f32[64,128]{1,0:T(8,128)S(1)}, u32[]{:S(2)}, u32[]{:S(2)}) collective-permute-start(f32[64,128]{1,0:T(8,128)S(1)} %get-tuple-element.71), channel_id=1, source_target_pairs={{1,2},{3,4},{5,6},{7,8},{9,10},{11,12},{13,14},{2,1},{4,3},{6,5},{... | collective-permute-start | bytes 98312 | tf_op jit(solution)/shard_map/ppermute | solution.py:27
  41.0 2.6 %copy-start = (f32[1,12,64,128]{3,2,1,0:T(8,128)S(1)}, f32[1,12,64,128]{3,2,1,0:T(8,128)}, u32[]{:S(2)}) copy-start(f32[1,12,64,128]{3,2,1,0:T(8,128)} %param.6) | copy-start | bytes 1179652
  41.0 2.6 %copy-start.1 = (f32[1,12,64,128]{3,2,1,0:T(8,128)S(1)}, f32[1,12,64,128]{3,2,1,0:T(8,128)}, u32[]{:S(2)}) copy-start(f32[1,12,64,128]{3,2,1,0:T(8,128)} %param.8) | copy-start | bytes 1179652
  41.0 2.6 %copy-start.9 = (bf16[128,768]{1,0:T(8,128)(2,1)S(1)}, bf16[128,768]{1,0:T(8,128)(2,1)}, u32[]{:S(2)}) copy-start(bf16[128,768]{1,0:T(8,128)(2,1)} %get-tuple-element.54.basis_rows) | copy-start | bytes 589828
  41.5 2.1 %copy-start.3 = (f32[12,32,128]{2,1,0:T(8,128)S(1)}, f32[12,32,128]{2,1,0:T(8,128)}, u32[]{:S(2)}) copy-start(f32[12,32,128]{2,1,0:T(8,128)} %get-tuple-element.53.sides) | copy-start | bytes 589828
  41.5 2.1 %copy-start.7 = (bf16[2,128,128]{2,1,0:T(8,128)(2,1)S(1)}, bf16[2,128,128]{2,1,0:T(8,128)(2,1)}, u32[]{:S(2)}) copy-start(bf16[2,128,128]{2,1,0:T(8,128)(2,1)} %get-tuple-element.52.edge_tiles) | copy-start | bytes 196612
  45.9 10.1 %copy-start.14 = (f32[64,128]{1,0:T(8,128)S(1)}, f32[64,128]{1,0:T(8,128)}, u32[]{:S(2)}) copy-start(f32[64,128]{1,0:T(8,128)} %get-tuple-element.78) | copy-start | bytes 98308
  45.9 10.8 %copy-start.13 = (f32[64,128]{1,0:T(8,128)S(1)}, f32[64,128]{1,0:T(8,128)}, u32[]{:S(2)}) copy-start(f32[64,128]{1,0:T(8,128)} %get-tuple-element.79) | copy-start | bytes 98308
  45.9 24.4 %all-to-all-start.1 = ((f32[16,64,128]{2,1,0:T(8,128)}), f32[16,64,128]{2,1,0:T(8,128)S(1)}, u32[]{:S(2)}, u32[]{:S(2)}) async-start(f32[16,64,128]{2,1,0:T(8,128)} %get-tuple-element.74), calls=%async_computation.1 | async-start | bytes 1048576 | tf_op jit(solution)/shard_map/all_to_all | solution.py:32
  56.0 7.5 %collective-permute-start.5 = (f32[64,128]{1,0:T(8,128)S(1)}, f32[64,128]{1,0:T(8,128)S(1)}, u32[]{:S(2)}, u32[]{:S(2)}) collective-permute-start(f32[64,128]{1,0:T(8,128)S(1)} %copy-done.14), channel_id=1, source_target_pairs={{1,2},{3,4},{5,6},{7,8},{9,10},{11,12},{13,14},{2,1},{4,3},{6,5},{... | collective-permute-start | bytes 98312 | tf_op jit(solution)/shard_map/ppermute | solution.py:27
  56.7 8.0 %collective-permute-start.6 = (f32[64,128]{1,0:T(8,128)S(1)}, f32[64,128]{1,0:T(8,128)S(1)}, u32[]{:S(2)}, u32[]{:S(2)}) collective-permute-start(f32[64,128]{1,0:T(8,128)S(1)} %copy-done.13), channel_id=1, source_target_pairs={{0,1},{1,0},{2,3},{3,2},{4,5},{5,4},{6,7},{7,6},{8,9},{9,8},{10,11... | collective-permute-start | bytes 98312 | tf_op jit(solution)/shard_map/ppermute | solution.py:28
  62.4 2.3 %copy-start.10 = (f32[64,128]{1,0:T(8,128)S(1)}, f32[64,128]{1,0:T(8,128)}, u32[]{:S(2)}) copy-start(f32[64,128]{1,0:T(8,128)} %get-tuple-element.80.far_tile) | copy-start | bytes 98308
  62.4 2.3 %copy-start.11 = (f32[64,128]{1,0:T(8,128)S(1)}, f32[64,128]{1,0:T(8,128)}, u32[]{:S(2)}) copy-start(f32[64,128]{1,0:T(8,128)} %get-tuple-element.81.near_tile) | copy-start | bytes 98308
  71.5 9.8 %collective-permute-start.7 = (f32[12,16,128]{2,1,0:T(8,128)S(1)}, f32[12,16,128]{2,1,0:T(8,128)S(1)}, u32[]{:S(2)}, u32[]{:S(2)}) collective-permute-start(f32[12,16,128]{2,1,0:T(8,128)S(1)} %get-tuple-element.83), channel_id=1, source_target_pairs={{16,32},{48,64},{80,96},{112,128},{144,160},{176,192},{208,224},{2... | collective-permute-start | bytes 294920 | tf_op jit(solution)/shard_map/ppermute | solution.py:459
  75.9 5.5 %copy-start.5 = (f32[12,64,128]{2,1,0:T(8,128)S(1)}, f32[12,64,128]{2,1,0:T(8,128)}, u32[]{:S(2)}) copy-start(f32[12,64,128]{2,1,0:T(8,128)} %get-tuple-element.72.image) | copy-start | bytes 1179652
  75.9 5.4 %copy-start.6 = (f32[12,64,128]{2,1,0:T(8,128)S(1)}, f32[12,64,128]{2,1,0:T(8,128)}, u32[]{:S(2)}) copy-start(f32[12,64,128]{2,1,0:T(8,128)} %get-tuple-element.73.rest) | copy-start | bytes 1179652
  76.3 4.8 %collective-permute-start.8 = (f32[64,128]{1,0:T(8,128)S(1)}, f32[64,128]{1,0:T(8,128)S(1)}, u32[]{:S(2)}, u32[]{:S(2)}) collective-permute-start(f32[64,128]{1,0:T(8,128)S(1)} %get-tuple-element.85), channel_id=1, source_target_pairs={{0,1},{1,0},{2,3},{3,2},{4,5},{5,4},{6,7},{7,6},{8,9},{9,8},{10,11... | collective-permute-start | bytes 98312 | tf_op jit(solution)/shard_map/ppermute | solution.py:28
  78.4 2.8 %collective-permute-start.9 = (f32[64,128]{1,0:T(8,128)S(1)}, f32[64,128]{1,0:T(8,128)S(1)}, u32[]{:S(2)}, u32[]{:S(2)}) collective-permute-start(f32[64,128]{1,0:T(8,128)S(1)} %get-tuple-element.86), channel_id=1, source_target_pairs={{1,2},{3,4},{5,6},{7,8},{9,10},{11,12},{13,14},{2,1},{4,3},{6,5},{... | collective-permute-start | bytes 98312 | tf_op jit(solution)/shard_map/ppermute | solution.py:27
  79.0 2.3 %copy-start.8 = (bf16[2,128,128]{2,1,0:T(8,128)(2,1)S(1)}, bf16[2,128,128]{2,1,0:T(8,128)(2,1)}, u32[]{:S(2)}) copy-start(bf16[2,128,128]{2,1,0:T(8,128)(2,1)} %get-tuple-element.52.edge_tiles) | copy-start | bytes 196612

commit v7 on v6

--- a/solution.py
+++ b/solution.py
@@ -317,9 +317,20 @@
 
 def project_kernel(basis_in, field_in, spread, basis, field, projected, sems, arrived):
     blocks, nodes, columns = field.shape
-    for load in start_all([(basis_in, basis), (field_in, field)], arrived):
-        load.wait()
-    projected[...] = dot(basis[...], field[...].reshape(blocks * nodes, columns))
+    third = blocks // 3
+    loads = start_all(
+        [(basis_in, basis)]
+        + [(field_in.at[at : at + third], field.at[at : at + third]) for at in range(0, blocks, third)],
+        arrived,
+    )
+    loads[0].wait()
+    parts = []
+    for i in range(3):
+        loads[i + 1].wait()
+        rows = rows_split(basis[:, i * third * nodes : (i + 1) * third * nodes])
+        values = field[i * third : (i + 1) * third].reshape(third * nodes, columns)
+        parts.append(product(rows, columns_split(values)))
+    projected[...] = parts[0] + parts[1] + parts[2]
     for copy in send_out(projected, spread, sems):
         copy.wait()
 
@@ -388,7 +399,7 @@
             pltpu.VMEM(basis_all.shape, wide),
             pltpu.VMEM((blocks, nodes, columns), wide),
             *spreading,
-            pltpu.SemaphoreType.DMA((2,)),
+            pltpu.SemaphoreType.DMA((4,)),
         ],
         basis_all, residual,
         slow=2,

time: 121 us -> 121 us (level)
  no operation moved by 1% of the time
where the time goes in v7:
time: 121 us; the launch traced here: 120 us
  starting transfers between devices  52.9 us (44%)
  blocking collectives  40.8 us (34%)
  Pallas kernels  19.3 us (16%)
  waiting for transfers between devices  5.39 us (4%)
    all_to_all x2, blocking collectives, total(): lax.all_to_all(spread, axes, 0, 0, axis_index_groups=groups, tiled=True)  36.6 us
    all_to_all x2, starting transfers between devices, gather_sub(): lax.all_to_all(spread, 'sub', 0, 0, tiled=True)  20.5 us
    pallas_call x13, Pallas kernels, call(): pl.pallas_call(kernel, out_shape=[(space or jax.ShapeDtypeStruct)(shape,...  19.3 us
    ppermute x4, starting transfers between devices, swap(): return (lax.ppermute(to_near, axis, near), from_far)  15.4 us
    ppermute x2, starting transfers between devices, precondition(): lax.ppermute(far_face, 'sec', pairings('sec')[1])  14.3 us
    all_gather x2, blocking collectives, precondition(): lax.all_gather(near_face, 'sec', axis_index_groups=pairs)  4.16 us
    all_to_all x2, waiting for transfers between devices, gather_sub(): lax.all_to_all(spread, 'sub', 0, 0, tiled=True)  4.06 us
    ppermute x4, starting transfers between devices, swap(): from_far = lax.ppermute(to_far, axis, far)  2.65 us
  transfers between devices with their start and end apart: 12, of which 3 were waited for; matrix products, arithmetic and copies ran while one was open for 0% of the time, Pallas kernels for 10%

profile of v7, /device:TPU:1, one launch (start us, length us, event | category | flops | bytes accessed | tf_op | source)
XLA Modules:
  0.0 119.9 jit_solution(7982733492295027249)
XLA Ops:
  0.0 0.1 pad_add_fusion.odd
  0.1 2.5 %shard_map.64 = f32[16,64,128]{2,1,0:T(8,128)} custom-call(f32[64,768]{1,0:T(8,128)} %bitcast.68, f32[12,64,128]{2,1,0:T(8,128)} %bitcast.53), custom_call_target="tpu_custom_call" | custom-call | flops 1000 | bytes 1000 | tf_op jit(solution)/shard_map/pallas_call | solution.py:364
  2.6 10.4 %all-to-all-start = ((f32[16,64,128]{2,1,0:T(8,128)}), f32[16,64,128]{2,1,0:T(8,128)S(1)}, u32[]{:S(2)}, u32[]{:S(2)}) async-start(f32[16,64,128]{2,1,0:T(8,128)} %shard_map.64), calls=%async_computation | async-start | bytes 1048576 | tf_op jit(solution)/shard_map/all_to_all | solution.py:32
  13.0 0.0 copy-start.12
  13.0 1.8 %shard_map.67 = (f32[128,128]{1,0:T(8,128)S(1)}, f32[128,128]{1,0:T(8,128)S(1)}) custom-call(s32[2]{0:T(128)S(1)} %pad_add_fusion.odd, f32[12,64,128]{2,1,0:T(8,128)} %bitcast.66, f32[12,64,128]{2,1,0:T(8,128)} %bitcast.57, f32[12,64,128]{2,1,0:T(8,128)} %bitcast.54), custom_call_target="tpu_custom_call" | custom-call | flops 1000 | bytes 1000 | tf_op jit(solution)/shard_map/pallas_call | solution.py:364
  14.8 0.7 collective-permute-start
  15.5 5.7 %collective-permute-start.1 = (f32[128,128]{1,0:T(8,128)S(1)}, f32[128,128]{1,0:T(8,128)S(1)}, u32[]{:S(2)}, u32[]{:S(2)}) collective-permute-start(f32[128,128]{1,0:T(8,128)S(1)} %get-tuple-element.66), channel_id=1, source_target_pairs={{0,1},{1,0},{2,3},{3,2},{4,5},{5,4},{6,7},{7,6},{8,9},{9,8},{10,11... | collective-permute-start | bytes 196616 | tf_op jit(solution)/shard_map/ppermute | solution.py:28
  21.2 0.0 copy-done.12
  21.2 3.3 %shard_map.65 = (bf16[12,128,128]{2,1,0:T(8,128)(2,1)S(1)}, bf16[12,64,128]{2,1,0:T(8,128)(2,1)S(1)}, bf16[12,128,128]{2,1,0:T(8,128)(2,1)}, bf16[12,64,128]{2,1...) custom-call(f32[12,32]{1,0:T(8,128)S(1)} %bitcast.64, ...), custom_call_target="tpu_custom_call" | custom-call | flops 1000 | bytes 1000 | tf_op jit(solution)/shard_map/pallas_call | solution.py:364
  24.6 1.1 shard_map.66
  25.6 0.0 collective-permute-done.far.far_tile
  25.7 0.0 collective-permute-done.1.near.near_tile
  25.7 1.6 %shard_map.68.local = f32[12,64,128]{2,1,0:T(8,128)S(1)} custom-call(s32[2]{0:T(128)S(1)} %pad_add_fusion.odd, bf16[12,128,128]{2,1,0:T(8,128)(2,1)S(1)} %get-tuple-element.60.tiles, bf16[12,64,128]{2,1,0:T(8,128)(2,1)S(1)} %get-tuple-element.61.tiles_own, f32[12,64,128]{2,1,0:T(8,128)S(1)} %get-tuple-element.62.start, ...), custom_call_target="tpu_custom_call" | custom-call | flops 1000 | bytes 1000 | tf_op jit(solution)/shard_map/pallas_call | solution.py:364
  27.3 0.0 all-to-all-done
  27.3 0.0 copy-start.2
  27.3 0.0 copy-start.4
  27.3 1.2 shard_map.69
  28.5 9.9 %collective-permute-start.2 = (f32[12,16,128]{2,1,0:T(8,128)S(1)}, f32[12,16,128]{2,1,0:T(8,128)S(1)}, u32[]{:S(2)}, u32[]{:S(2)}) collective-permute-start(f32[12,16,128]{2,1,0:T(8,128)S(1)} %get-tuple-element.68), channel_id=1, source_target_pairs={{16,32},{48,64},{80,96},{112,128},{144,160},{176,192},{208,224},{2... | collective-permute-start | bytes 294920 | tf_op jit(solution)/shard_map/ppermute | solution.py:470
  38.4 2.0 %collective-permute-start.3 = (f32[64,128]{1,0:T(8,128)S(1)}, f32[64,128]{1,0:T(8,128)S(1)}, u32[]{:S(2)}, u32[]{:S(2)}) collective-permute-start(f32[64,128]{1,0:T(8,128)S(1)} %get-tuple-element.70), channel_id=1, source_target_pairs={{0,1},{1,0},{2,3},{3,2},{4,5},{5,4},{6,7},{7,6},{8,9},{9,8},{10,11... | collective-permute-start | bytes 98312 | tf_op jit(solution)/shard_map/ppermute | solution.py:28
  40.4 0.7 collective-permute-start.4
  41.1 0.0 copy-done.2
  41.1 0.0 copy-done.4
  41.1 0.0 copy-start
  41.2 0.0 copy-start.1
  41.2 0.0 copy-start.9
  41.2 0.5 shard_map.70.linear
  41.6 0.0 copy-start.3
  41.7 0.0 copy-start.7
  41.7 2.1 %all-gather = f32[24,16,128]{2,1,0:T(8,128)S(1)} all-gather(f32[12,16,128]{2,1,0:T(8,128)S(1)} %get-tuple-element.69), channel_id=2, replica_groups={{0,16},{32,48},{64,80},{96,112},{128,144},{160,176},{192,208},{224,240}..., dimensions={0}, use_global_device_ids=true | all-gather | bytes 294912 | tf_op jit(solution)/shard_map/all_gather | solution.py:469
  43.7 0.0 collective-permute-done.3.near_block
  43.7 0.0 collective-permute-done.4.far_block
  43.8 0.0 collective-permute-done.2.far_face
  43.8 0.0 copy-done
  43.8 0.0 copy-done.1
  43.8 0.0 copy-done.9
  43.8 0.0 copy-done.3
  43.8 2.2 %shard_map.71 = (f32[12,64,128]{2,1,0:T(8,128)}, f32[12,64,128]{2,1,0:T(8,128)}, f32[16,64,128]{2,1,0:T(8,128)}, f32[12,64,128]{2,1,0:T(8,128)S(1)}, f32[64,128]{1,0:T(8,128)}, /*index=5*/f32[64,128]{1,0:T(8,128)}) custom-call(s32[2]{0:T(128)S(1)} %pad_add_fusion.odd, bf16[2,128,128]{2,1,0:T(8,128)(2,1)S(1)} %copy-done.7, f32[12,32,128]{2,1,0:T(8,128)S(1)} %copy-done.3, ...), custom_call_target="tpu_custom_call" | custom-call | flops 1000 | bytes 1000 | tf_op jit(solution)/shard_map/pallas_call | solution.py:364
  46.0 0.0 copy-start.14
  46.0 0.0 copy-start.13
  46.0 10.1 %all-to-all-start.1 = ((f32[16,64,128]{2,1,0:T(8,128)}), f32[16,64,128]{2,1,0:T(8,128)S(1)}, u32[]{:S(2)}, u32[]{:S(2)}) async-start(f32[16,64,128]{2,1,0:T(8,128)} %get-tuple-element.74), calls=%async_computation.1 | async-start | bytes 1048576 | tf_op jit(solution)/shard_map/all_to_all | solution.py:32
  56.1 0.0 copy-done.14
  56.1 0.7 collective-permute-start.5
  56.8 5.7 %collective-permute-start.6 = (f32[64,128]{1,0:T(8,128)S(1)}, f32[64,128]{1,0:T(8,128)S(1)}, u32[]{:S(2)}, u32[]{:S(2)}) collective-permute-start(f32[64,128]{1,0:T(8,128)S(1)} %copy-done.13), channel_id=1, source_target_pairs={{0,1},{1,0},{2,3},{3,2},{4,5},{5,4},{6,7},{7,6},{8,9},{9,8},{10,11... | collective-permute-start | bytes 98312 | tf_op jit(solution)/shard_map/ppermute | solution.py:28
  62.6 1.1 shard_map.72
  63.6 0.0 collective-permute-done.5.far
  63.7 1.1 collective-permute-done.6.near
  64.8 1.6 %shard_map.73.local = f32[12,64,128]{2,1,0:T(8,128)S(1)} custom-call(s32[2]{0:T(128)S(1)} %pad_add_fusion.odd, bf16[12,128,128]{2,1,0:T(8,128)(2,1)S(1)} %get-tuple-element.60.tiles, bf16[12,64,128]{2,1,0:T(8,128)(2,1)S(1)} %get-tuple-element.61.tiles_own, f32[12,64,128]{2,1,0:T(8,128)S(1)} %get-tuple-element.75.start, ...), custom_call_target="tpu_custom_call" | custom-call | flops 1000 | bytes 1000 | tf_op jit(solution)/shard_map/pallas_call | solution.py:364
  66.4 4.1 %all-to-all-done.1 = f32[16,64,128]{2,1,0:T(8,128)S(1)} async-done(((f32[16,64,128]{2,1,0:T(8,128)}), f32[16,64,128]{2,1,0:T(8,128)S(1)}, u32[]{:S(2)}, u32[]{:S(2)}) %all-to-all-start.1) | async-done | bytes 524320 | tf_op jit(solution)/shard_map/all_to_all | solution.py:32
  70.5 1.1 shard_map.74
  71.6 4.4 %collective-permute-start.7 = (f32[12,16,128]{2,1,0:T(8,128)S(1)}, f32[12,16,128]{2,1,0:T(8,128)S(1)}, u32[]{:S(2)}, u32[]{:S(2)}) collective-permute-start(f32[12,16,128]{2,1,0:T(8,128)S(1)} %get-tuple-element.83), channel_id=1, source_target_pairs={{16,32},{48,64},{80,96},{112,128},{144,160},{176,192},{208,224},{2... | collective-permute-start | bytes 294920 | tf_op jit(solution)/shard_map/ppermute | solution.py:470
  76.0 0.0 copy-start.5
  76.0 0.5 shard_map.75.linear
  76.5 2.0 %collective-permute-start.8 = (f32[64,128]{1,0:T(8,128)S(1)}, f32[64,128]{1,0:T(8,128)S(1)}, u32[]{:S(2)}, u32[]{:S(2)}) collective-permute-start(f32[64,128]{1,0:T(8,128)S(1)} %get-tuple-element.85), channel_id=1, source_target_pairs={{0,1},{1,0},{2,3},{3,2},{4,5},{5,4},{6,7},{7,6},{8,9},{9,8},{10,11... | collective-permute-start | bytes 98312 | tf_op jit(solution)/shard_map/ppermute | solution.py:28
  78.5 0.7 collective-permute-start.9
  79.2 2.1 %all-gather.1 = f32[24,16,128]{2,1,0:T(8,128)S(1)} all-gather(f32[12,16,128]{2,1,0:T(8,128)S(1)} %get-tuple-element.84), channel_id=3, replica_groups={{0,16},{32,48},{64,80},{96,112},{128,144},{160,176},{192,208},{224,240}..., dimensions={0}, use_global_device_ids=true | all-gather | bytes 294912 | tf_op jit(solution)/shard_map/all_gather | solution.py:469
  81.3 0.0 collective-permute-done.8.near_block
  81.3 0.0 collective-permute-done.9.far_block
  81.3 0.2 collective-permute-done.7.far_face
  81.5 0.0 copy-done.8
  81.5 0.8 shard_map.76
  82.3 19.2 %all_to_all.20 = f32[16,1,640]{2,1,0:T(1,128)S(1)} all-to-all(f32[16,1,640]{2,1,0:T(1,128)S(1)} %broadcast_in_dim.9), channel_id=1, replica_groups={{0,16,64,80,128,144,192,208,256,272,320,336,384,400,448,464},{32,48,96,..., dimensions={0} | all-to-all | bytes 81920 | tf_op jit(solution)/shard_map/all_to_all | solution.py:47
  101.7 17.4 %all_to_all.21 = f32[32,1,640]{2,1,0:T(1,128)S(1)} all-to-all(f32[32,1,640]{2,1,0:T(1,128)S(1)} %broadcast_in_dim.20), channel_id=1, replica_groups={{0,1,2,3,4,5,6,7,8,9,10,11,12,13,14,15,32,33,34,35,36,37,38,39,40,41,42..., dimensions={0} | all-to-all | bytes 163840 | tf_op jit(solution)/shard_map/all_to_all | solution.py:47
  119.0 0.1 reduce_sum.21
  119.1 0.8 add_bitcast_fusion
  (17 shorter events, 0.2 us)
Async XLA Ops:
  2.6 24.6 %all-to-all-start = ((f32[16,64,128]{2,1,0:T(8,128)}), f32[16,64,128]{2,1,0:T(8,128)S(1)}, u32[]{:S(2)}, u32[]{:S(2)}) async-start(f32[16,64,128]{2,1,0:T(8,128)} %shard_map.64), calls=%async_computation | async-start | bytes 1048576 | tf_op jit(solution)/shard_map/all_to_all | solution.py:32
  13.0 8.2 %copy-start.12 = (f32[1,12,32]{2,0,1:T(1,128)S(1)}, f32[1,12,32]{2,0,1:T(1,128)}, u32[]{:S(2)}) copy-start(f32[1,12,32]{2,0,1:T(1,128)} %param.9) | copy-start | bytes 4612
  14.8 10.8 %collective-permute-start = (f32[128,128]{1,0:T(8,128)S(1)}, f32[128,128]{1,0:T(8,128)S(1)}, u32[]{:S(2)}, u32[]{:S(2)}) collective-permute-start(f32[128,128]{1,0:T(8,128)S(1)} %get-tuple-element.65), channel_id=1, source_target_pairs={{1,2},{3,4},{5,6},{7,8},{9,10},{11,12},{13,14},{2,1},{4,3},{6,5},{... | collective-permute-start | bytes 196616 | tf_op jit(solution)/shard_map/ppermute | solution.py:27
  15.5 10.1 %collective-permute-start.1 = (f32[128,128]{1,0:T(8,128)S(1)}, f32[128,128]{1,0:T(8,128)S(1)}, u32[]{:S(2)}, u32[]{:S(2)}) collective-permute-start(f32[128,128]{1,0:T(8,128)S(1)} %get-tuple-element.66), channel_id=1, source_target_pairs={{0,1},{1,0},{2,3},{3,2},{4,5},{5,4},{6,7},{7,6},{8,9},{9,8},{10,11... | collective-permute-start | bytes 196616 | tf_op jit(solution)/shard_map/ppermute | solution.py:28
  27.3 13.8 %copy-start.2 = (bf16[12,128,128]{2,1,0:T(8,128)(2,1)S(1)}, bf16[12,128,128]{2,1,0:T(8,128)(2,1)}, u32[]{:S(2)}) copy-start(bf16[12,128,128]{2,1,0:T(8,128)(2,1)} %get-tuple-element.55.tiles) | copy-start | bytes 1179652
  27.3 13.8 %copy-start.4 = (bf16[12,64,128]{2,1,0:T(8,128)(2,1)S(1)}, bf16[12,64,128]{2,1,0:T(8,128)(2,1)}, u32[]{:S(2)}) copy-start(bf16[12,64,128]{2,1,0:T(8,128)(2,1)} %get-tuple-element.56.tiles_own) | copy-start | bytes 589828
  28.5 15.3 %collective-permute-start.2 = (f32[12,16,128]{2,1,0:T(8,128)S(1)}, f32[12,16,128]{2,1,0:T(8,128)S(1)}, u32[]{:S(2)}, u32[]{:S(2)}) collective-permute-start(f32[12,16,128]{2,1,0:T(8,128)S(1)} %get-tuple-element.68), channel_id=1, source_target_pairs={{16,32},{48,64},{80,96},{112,128},{144,160},{176,192},{208,224},{2... | collective-permute-start | bytes 294920 | tf_op jit(solution)/shard_map/ppermute | solution.py:470
  38.4 5.3 %collective-permute-start.3 = (f32[64,128]{1,0:T(8,128)S(1)}, f32[64,128]{1,0:T(8,128)S(1)}, u32[]{:S(2)}, u32[]{:S(2)}) collective-permute-start(f32[64,128]{1,0:T(8,128)S(1)} %get-tuple-element.70), channel_id=1, source_target_pairs={{0,1},{1,0},{2,3},{3,2},{4,5},{5,4},{6,7},{7,6},{8,9},{9,8},{10,11... | collective-permute-start | bytes 98312 | tf_op jit(solution)/shard_map/ppermute | solution.py:28
  40.4 3.3 %collective-permute-start.4 = (f32[64,128]{1,0:T(8,128)S(1)}, f32[64,128]{1,0:T(8,128)S(1)}, u32[]{:S(2)}, u32[]{:S(2)}) collective-permute-start(f32[64,128]{1,0:T(8,128)S(1)} %get-tuple-element.71), channel_id=1, source_target_pairs={{1,2},{3,4},{5,6},{7,8},{9,10},{11,12},{13,14},{2,1},{4,3},{6,5},{... | collective-permute-start | bytes 98312 | tf_op jit(solution)/shard_map/ppermute | solution.py:27
  41.1 2.6 %copy-start = (f32[1,12,64,128]{3,2,1,0:T(8,128)S(1)}, f32[1,12,64,128]{3,2,1,0:T(8,128)}, u32[]{:S(2)}) copy-start(f32[1,12,64,128]{3,2,1,0:T(8,128)} %param.6) | copy-start | bytes 1179652
  41.2 2.6 %copy-start.1 = (f32[1,12,64,128]{3,2,1,0:T(8,128)S(1)}, f32[1,12,64,128]{3,2,1,0:T(8,128)}, u32[]{:S(2)}) copy-start(f32[1,12,64,128]{3,2,1,0:T(8,128)} %param.8) | copy-start | bytes 1179652
  41.2 2.6 %copy-start.9 = (bf16[128,768]{1,0:T(8,128)(2,1)S(1)}, bf16[128,768]{1,0:T(8,128)(2,1)}, u32[]{:S(2)}) copy-start(bf16[128,768]{1,0:T(8,128)(2,1)} %get-tuple-element.54.basis_rows) | copy-start | bytes 589828
  41.6 2.1 %copy-start.3 = (f32[12,32,128]{2,1,0:T(8,128)S(1)}, f32[12,32,128]{2,1,0:T(8,128)}, u32[]{:S(2)}) copy-start(f32[12,32,128]{2,1,0:T(8,128)} %get-tuple-element.53.sides) | copy-start | bytes 589828
  41.7 2.1 %copy-start.7 = (bf16[2,128,128]{2,1,0:T(8,128)(2,1)S(1)}, bf16[2,128,128]{2,1,0:T(8,128)(2,1)}, u32[]{:S(2)}) copy-start(bf16[2,128,128]{2,1,0:T(8,128)(2,1)} %get-tuple-element.52.edge_tiles) | copy-start | bytes 196612
  46.0 10.1 %copy-start.14 = (f32[64,128]{1,0:T(8,128)S(1)}, f32[64,128]{1,0:T(8,128)}, u32[]{:S(2)}) copy-start(f32[64,128]{1,0:T(8,128)} %get-tuple-element.78) | copy-start | bytes 98308
  46.0 10.8 %copy-start.13 = (f32[64,128]{1,0:T(8,128)S(1)}, f32[64,128]{1,0:T(8,128)}, u32[]{:S(2)}) copy-start(f32[64,128]{1,0:T(8,128)} %get-tuple-element.79) | copy-start | bytes 98308
  46.0 24.4 %all-to-all-start.1 = ((f32[16,64,128]{2,1,0:T(8,128)}), f32[16,64,128]{2,1,0:T(8,128)S(1)}, u32[]{:S(2)}, u32[]{:S(2)}) async-start(f32[16,64,128]{2,1,0:T(8,128)} %get-tuple-element.74), calls=%async_computation.1 | async-start | bytes 1048576 | tf_op jit(solution)/shard_map/all_to_all | solution.py:32
  56.1 7.5 %collective-permute-start.5 = (f32[64,128]{1,0:T(8,128)S(1)}, f32[64,128]{1,0:T(8,128)S(1)}, u32[]{:S(2)}, u32[]{:S(2)}) collective-permute-start(f32[64,128]{1,0:T(8,128)S(1)} %copy-done.14), channel_id=1, source_target_pairs={{1,2},{3,4},{5,6},{7,8},{9,10},{11,12},{13,14},{2,1},{4,3},{6,5},{... | collective-permute-start | bytes 98312 | tf_op jit(solution)/shard_map/ppermute | solution.py:27
  56.8 8.0 %collective-permute-start.6 = (f32[64,128]{1,0:T(8,128)S(1)}, f32[64,128]{1,0:T(8,128)S(1)}, u32[]{:S(2)}, u32[]{:S(2)}) collective-permute-start(f32[64,128]{1,0:T(8,128)S(1)} %copy-done.13), channel_id=1, source_target_pairs={{0,1},{1,0},{2,3},{3,2},{4,5},{5,4},{6,7},{7,6},{8,9},{9,8},{10,11... | collective-permute-start | bytes 98312 | tf_op jit(solution)/shard_map/ppermute | solution.py:28
  62.5 2.3 %copy-start.10 = (f32[64,128]{1,0:T(8,128)S(1)}, f32[64,128]{1,0:T(8,128)}, u32[]{:S(2)}) copy-start(f32[64,128]{1,0:T(8,128)} %get-tuple-element.80.far_tile) | copy-start | bytes 98308
  62.5 2.3 %copy-start.11 = (f32[64,128]{1,0:T(8,128)S(1)}, f32[64,128]{1,0:T(8,128)}, u32[]{:S(2)}) copy-start(f32[64,128]{1,0:T(8,128)} %get-tuple-element.81.near_tile) | copy-start | bytes 98308
  71.6 9.8 %collective-permute-start.7 = (f32[12,16,128]{2,1,0:T(8,128)S(1)}, f32[12,16,128]{2,1,0:T(8,128)S(1)}, u32[]{:S(2)}, u32[]{:S(2)}) collective-permute-start(f32[12,16,128]{2,1,0:T(8,128)S(1)} %get-tuple-element.83), channel_id=1, source_target_pairs={{16,32},{48,64},{80,96},{112,128},{144,160},{176,192},{208,224},{2... | collective-permute-start | bytes 294920 | tf_op jit(solution)/shard_map/ppermute | solution.py:470
  76.0 5.5 %copy-start.5 = (f32[12,64,128]{2,1,0:T(8,128)S(1)}, f32[12,64,128]{2,1,0:T(8,128)}, u32[]{:S(2)}) copy-start(f32[12,64,128]{2,1,0:T(8,128)} %get-tuple-element.72.image) | copy-start | bytes 1179652
  76.0 5.4 %copy-start.6 = (f32[12,64,128]{2,1,0:T(8,128)S(1)}, f32[12,64,128]{2,1,0:T(8,128)}, u32[]{:S(2)}) copy-start(f32[12,64,128]{2,1,0:T(8,128)} %get-tuple-element.73.rest) | copy-start | bytes 1179652
  76.5 4.8 %collective-permute-start.8 = (f32[64,128]{1,0:T(8,128)S(1)}, f32[64,128]{1,0:T(8,128)S(1)}, u32[]{:S(2)}, u32[]{:S(2)}) collective-permute-start(f32[64,128]{1,0:T(8,128)S(1)} %get-tuple-element.85), channel_id=1, source_target_pairs={{0,1},{1,0},{2,3},{3,2},{4,5},{5,4},{6,7},{7,6},{8,9},{9,8},{10,11... | collective-permute-start | bytes 98312 | tf_op jit(solution)/shard_map/ppermute | solution.py:28
  78.5 2.8 %collective-permute-start.9 = (f32[64,128]{1,0:T(8,128)S(1)}, f32[64,128]{1,0:T(8,128)S(1)}, u32[]{:S(2)}, u32[]{:S(2)}) collective-permute-start(f32[64,128]{1,0:T(8,128)S(1)} %get-tuple-element.86), channel_id=1, source_target_pairs={{1,2},{3,4},{5,6},{7,8},{9,10},{11,12},{13,14},{2,1},{4,3},{6,5},{... | collective-permute-start | bytes 98312 | tf_op jit(solution)/shard_map/ppermute | solution.py:27
  79.2 2.3 %copy-start.8 = (bf16[2,128,128]{2,1,0:T(8,128)(2,1)S(1)}, bf16[2,128,128]{2,1,0:T(8,128)(2,1)}, u32[]{:S(2)}) copy-start(bf16[2,128,128]{2,1,0:T(8,128)(2,1)} %get-tuple-element.52.edge_tiles) | copy-start | bytes 196612
